TPU v7x, 512 devices: a whole 4x8x8 slice. The times are simulated.
512 devices in a mesh: blk: 64 (over y, x, z_lo), rep: 8 (over z_hi, core).
Axes of the slice: x: 4, y: 8, z: 8 (z_hi: 4, z_lo: 2; z = z_hi * 2 + z_lo), core: 2. Of those that a mesh axis runs over, the one named last changes fastest.
Arguments:
- hidden_pre: bfloat16 [8192, 1024], P('blk'), may hold values from -6 to 6
- adj_vals: bfloat16 [64, 16, 128, 128], P('blk', 'rep'), may hold values from -0.125 to 0.125
- adj_cols: int32 [64, 16], P('blk', 'rep'), may hold values from 0 to 63, as said below
- w_out: bfloat16 [1024, 1024], replicated, may hold values from -0.1875 to 0.1875
- cotangent: bfloat16 [8192, 1024], P('blk'), may hold values from -6 to 6
Outputs:
- aggregated: bfloat16 [8192, 1024], P('blk', 'rep')
- grad_weight: float32 [1024, 1024], P('blk', 'rep')
- grad_pre: bfloat16 [8192, 1024], P('blk', 'rep')
Inputs may be any that keep to these rules, and one draw needn't show every extreme that they name: For block-row i, let b = i // 1 and, for slot k, s = (b - adj_cols[i, k]) mod (64). Then s // 8 == k // 2, and the slots of one block-row with equal k // 2 have distinct s.
All inputs are finite; a program needn't handle non-finite values.
Results may differ from a plain program's by a relative error of at most 0.014.
Values may be sent and summed in bfloat16 or wider, within the bound.
A program may use at most 64 MiB of HBM per device.

v0:
```python
import jax
import jax.numpy as jnp
from jax import lax
from jax.sharding import PartitionSpec as P


def passed_along(value, axis, steps):
    count = lax.axis_size(axis)
    pairs = [(source, (source + steps) % count) for source in range(count)]
    return lax.ppermute(value, axis, pairs)


def spread_into(matches, contribution):
    return jnp.sum(
        jnp.where(matches[:, :, :, None, None], contribution[:, :, None], 0.0), axis=(0, 1)
    )


def shards(hidden_pre, adj_vals, adj_cols, w_out, cotangent):
    row_count, feature_width = hidden_pre.shape
    row_blocks = adj_vals.shape[0]
    tile_size = adj_vals.shape[2]
    blk_count = lax.axis_size("blk")
    rep_count = lax.axis_size("rep")
    section_span = blk_count // rep_count
    bit_total = (rep_count - 1).bit_length()
    blk_pos = lax.axis_index("blk")
    rep_pos = lax.axis_index("rep")
    cols_here = feature_width // rep_count
    owners = adj_cols // row_blocks
    within = jnp.mod(blk_pos - owners, blk_count) - rep_pos * section_span
    inside = adj_cols % row_blocks
    block_range = jnp.arange(row_blocks, dtype=jnp.int32)
    zero_out = jnp.zeros((row_blocks, tile_size, feature_width), jnp.float32)
    w_columns = lax.dynamic_slice_in_dim(w_out, rep_pos * cols_here, cols_here, 1)

    def pick_mask(turn_index):
        return (within == turn_index)[:, :, None] & (
            inside[:, :, None] == block_range[None, None, :]
        )

    hidden_act = jnp.maximum(hidden_pre, 0)
    partial_value = jnp.dot(hidden_act, w_columns, preferred_element_type=jnp.float32).astype(
        jnp.bfloat16
    )
    projected = lax.all_gather(partial_value, "rep", axis=1, tiled=True)
    visiting = projected
    for bit_index in range(bit_total):
        shifted = passed_along(visiting, "blk", section_span << bit_index)
        visiting = jnp.where(rep_pos >> bit_index & 1 == 1, shifted, visiting)

    def forward_turn(current, turn_index):
        selector = pick_mask(turn_index).astype(jnp.bfloat16)
        blocks = current.reshape(row_blocks, tile_size, feature_width)
        picked = jnp.einsum(
            "jkq,qtd->jktd", selector, blocks, preferred_element_type=jnp.float32
        ).astype(jnp.bfloat16)
        return jnp.einsum("jkab,jkbd->jad", adj_vals, picked, preferred_element_type=jnp.float32)

    def forward_step(carry, turn_index):
        current, output_sum = carry
        output_sum = output_sum + forward_turn(current, turn_index)
        kept_rows = None
        current = passed_along(current, "blk", 1)
        return ((current, output_sum), kept_rows)

    (final_rows, output_sum), kept_rows = lax.scan(
        forward_step, (visiting, zero_out), jnp.arange(section_span - 1, dtype=jnp.int32)
    )
    output_sum = output_sum + forward_turn(final_rows, section_span - 1)
    out_part = lax.psum_scatter(
        output_sum.reshape(row_count, feature_width).astype(jnp.bfloat16),
        "rep",
        scatter_dimension=1,
        tiled=True,
    )
    grad_block = cotangent.reshape(row_blocks, tile_size, feature_width)
    contribution = jnp.einsum(
        "jkab,jad->jkbd", adj_vals, grad_block, preferred_element_type=jnp.float32
    )

    def carry_step(carried, turn_index):
        carried = carried + spread_into(pick_mask(section_span - 1 - turn_index), contribution)
        return (passed_along(carried, "blk", -1), None)

    carried, ignored = lax.scan(carry_step, zero_out, jnp.arange(section_span - 1, dtype=jnp.int32))
    carried = carried + spread_into(pick_mask(0), contribution)
    for bit_index in range(bit_total):
        shifted = passed_along(
            carried.astype(jnp.bfloat16), "blk", -(section_span << bit_index)
        ).astype(carried.dtype)
        carried = jnp.where(rep_pos >> bit_index & 1 == 1, shifted, carried)
    back_part = lax.psum_scatter(
        carried.reshape(row_count, feature_width), "rep", scatter_dimension=1, tiled=True
    )
    back_grad = back_part.astype(jnp.bfloat16)
    grad_weight = lax.psum_scatter(
        lax.dot_general(
            hidden_act, back_grad, (((0,), (0,)), ((), ())), preferred_element_type=jnp.float32
        ),
        "blk",
        scatter_dimension=0,
        tiled=True,
    )
    back_full = lax.all_gather(back_grad, "rep", axis=1, tiled=True)
    w_rows = lax.dynamic_slice_in_dim(w_out, rep_pos * cols_here, cols_here, 0)
    grad_in = lax.dot_general(
        back_full, w_rows, (((1,), (1,)), ((), ())), preferred_element_type=jnp.float32
    )
    pre_part = lax.dynamic_slice_in_dim(hidden_pre, rep_pos * cols_here, cols_here, 1)
    grad_pre = jnp.where(pre_part > 0, grad_in, 0.0).astype(jnp.bfloat16)
    return (out_part, grad_weight, grad_pre)


def solution(mesh):
    placed = (P("blk", None), P("blk", "rep", None, None), P("blk", "rep"), P(), P("blk", None))
    return jax.shard_map(
        shards,
        mesh=mesh,
        in_specs=placed,
        out_specs=(P("blk", "rep"), P("blk", "rep"), P("blk", "rep")),
        check_vma=False,
    )
```

profile of v0, /device:TPU:6, one launch (start us, length us, event | category | flops | bytes accessed | tf_op | source)
XLA Modules:
  0.0 693.6 jit_solution(1828787675232386095)
XLA Ops:
  11.0 134.6 %while.25 = (s32[]{:T(128)}, f32[1,128,1024]{2,1,0:T(8,128)}, s32[7]{0:T(128)S(1)}, s32[1,2]{1,0:T(1,128)S(1)}, f32[1,2,128,1024]{3,2,1,0:T(8,128)S(1)}, /*index=5*/s32[]{:T(128)}, s32[1]{0:T(128)}) while((s32[]{:T(128)}, f32[1,128,1024]{2,1,0:T(8,128)}, s32[7]{0:T(128)S(1)}, s32[1,2]{1,0:T(1,128)S(1)}, f32[1,2,128,1024]{3,2,1,0:T(8,128)S(1)}, ...), condition=%wide.region_5.6_spmd, body=%wide.region_3.5_spmd.sunk | while | flops 524293 | bytes 5243037 | solution.py:86
  14.4 4.5 collective-permute-start
  18.9 12.0 %collective-permute-done = f32[1,128,1024]{2,1,0:T(8,128)} collective-permute-done((f32[1,128,1024]{2,1,0:T(8,128)}, f32[1,128,1024]{2,1,0:T(8,128)}, u32[]{:S(2)}, u32[]{:S(2)}) %collective-permute-start) | collective-permute-done | bytes 524320 | tf_op jit(solution)/shard_map/while/body/eval_jaxpr/ppermute | solution.py:10
  34.2 4.8 collective-permute-start
  39.0 13.2 %collective-permute-done = f32[1,128,1024]{2,1,0:T(8,128)} collective-permute-done((f32[1,128,1024]{2,1,0:T(8,128)}, f32[1,128,1024]{2,1,0:T(8,128)}, u32[]{:S(2)}, u32[]{:S(2)}) %collective-permute-start) | collective-permute-done | bytes 524320 | tf_op jit(solution)/shard_map/while/body/eval_jaxpr/ppermute | solution.py:10
  55.5 2.7 collective-permute-start
  58.2 14.4 %collective-permute-done = f32[1,128,1024]{2,1,0:T(8,128)} collective-permute-done((f32[1,128,1024]{2,1,0:T(8,128)}, f32[1,128,1024]{2,1,0:T(8,128)}, u32[]{:S(2)}, u32[]{:S(2)}) %collective-permute-start) | collective-permute-done | bytes 524320 | tf_op jit(solution)/shard_map/while/body/eval_jaxpr/ppermute | solution.py:10
  77.8 14.2 %collective-permute-done = f32[1,128,1024]{2,1,0:T(8,128)} collective-permute-done((f32[1,128,1024]{2,1,0:T(8,128)}, f32[1,128,1024]{2,1,0:T(8,128)}, u32[]{:S(2)}, u32[]{:S(2)}) %collective-permute-start) | collective-permute-done | bytes 524320 | tf_op jit(solution)/shard_map/while/body/eval_jaxpr/ppermute | solution.py:10
  97.2 13.3 %collective-permute-done = f32[1,128,1024]{2,1,0:T(8,128)} collective-permute-done((f32[1,128,1024]{2,1,0:T(8,128)}, f32[1,128,1024]{2,1,0:T(8,128)}, u32[]{:S(2)}, u32[]{:S(2)}) %collective-permute-start) | collective-permute-done | bytes 524320 | tf_op jit(solution)/shard_map/while/body/eval_jaxpr/ppermute | solution.py:10
  115.8 12.4 %collective-permute-done = f32[1,128,1024]{2,1,0:T(8,128)} collective-permute-done((f32[1,128,1024]{2,1,0:T(8,128)}, f32[1,128,1024]{2,1,0:T(8,128)}, u32[]{:S(2)}, u32[]{:S(2)}) %collective-permute-start) | collective-permute-done | bytes 524320 | tf_op jit(solution)/shard_map/while/body/eval_jaxpr/ppermute | solution.py:10
  133.4 12.3 %collective-permute-done = f32[1,128,1024]{2,1,0:T(8,128)} collective-permute-done((f32[1,128,1024]{2,1,0:T(8,128)}, f32[1,128,1024]{2,1,0:T(8,128)}, u32[]{:S(2)}, u32[]{:S(2)}) %collective-permute-start) | collective-permute-done | bytes 524320 | tf_op jit(solution)/shard_map/while/body/eval_jaxpr/ppermute | solution.py:10
  146.9 12.7 %collective-permute-start.5 = (bf16[1,128,1024]{2,1,0:T(8,128)(2,1)S(1)}, bf16[1,128,1024]{2,1,0:T(8,128)(2,1)S(1)}, u32[]{:S(2)}, u32[]{:S(2)}) collective-permute-start(bf16[1,128,1024]{2,1,0:T(8,128)(2,1)S(1)} %get-tuple-element.161), channel_id=1, source_target_pairs={{0,448},{8,456},{16,464},{24,472},{32,480},{40,488},{48,496},{56,5... | collective-permute-start | bytes 786440 | tf_op jit(solution)/shard_map/ppermute | solution.py:10
  160.8 19.5 %all_gather.6 = bf16[128,1024]{1,0:T(8,128)(2,1)S(1)} all-gather(bf16[128,128]{1,0:T(8,128)(2,1)S(1)} %convolution_convert_fusion), channel_id=1, replica_groups=mesh['blk'=64,'rep'=8] {'rep'}, dimensions={1}, use_global_device_ids=true | all-gather | bytes 294912 | tf_op jit(solution)/shard_map/all_gather | solution.py:46
  183.0 3.4 collective-permute-start.6
  186.4 5.7 collective-permute-done.2
  196.3 4.7 collective-permute-start.7
  201.0 9.4 %collective-permute-done.3 = bf16[128,1024]{1,0:T(8,128)(2,1)} collective-permute-done((bf16[128,1024]{1,0:T(8,128)(2,1)}, bf16[128,1024]{1,0:T(8,128)(2,1)}, u32[]{:S(2)}, u32[]{:S(2)}) %collective-permute-start.3) | collective-permute-done | bytes 262176 | tf_op jit(solution)/shard_map/ppermute | solution.py:10
  212.0 4.5 collective-permute-start.4
  220.8 13.4 %collective-permute-done.4 = bf16[128,1024]{1,0:T(8,128)(2,1)} collective-permute-done((bf16[128,1024]{1,0:T(8,128)(2,1)}, bf16[128,1024]{1,0:T(8,128)(2,1)}, u32[]{:S(2)}, u32[]{:S(2)}) %collective-permute-start.4) | collective-permute-done | bytes 262176 | tf_op jit(solution)/shard_map/ppermute | solution.py:10
  236.0 98.8 %while.26 = (s32[]{:T(128)}, bf16[128,1024]{0,1:T(8,128)(2,1)}, f32[1,128,1024]{1,2,0:T(8,128)S(1)}, s32[7]{0:T(128)S(1)}, s32[1,2]{1,0:T(1,128)S(1)}, /*index=5...) while((s32[]{:T(128)}, bf16[128,1024]{0,1:T(8,128)(2,1)}, f32[1,128,1024]{1,2,0:T(8,128)S(1)}, ...), condition=%wide.region_1.2_spmd.clone, body=%wide.region_0.1_spmd.clone.sunk | while | flops 68026376 | bytes 3997871 | solution.py:67
  236.9 11.2 %collective-permute-start.1 = (bf16[128,1024]{0,1:T(8,128)(2,1)S(1)}, bf16[128,1024]{0,1:T(8,128)(2,1)}, u32[]{:S(2)}, u32[]{:S(2)}) collective-permute-start(bf16[128,1024]{0,1:T(8,128)(2,1)S(1)} %copy.16), channel_id=1, source_target_pairs={{0,8},{8,16},{16,24},{24,32},{32,40},{40,48},{48,56},{56,64},{64,7... | collective-permute-start | bytes 786440 | tf_op jit(solution)/shard_map/while/body/eval_jaxpr/ppermute | solution.py:10
  249.8 4.5 collective-permute-done.1
  255.3 13.5 %collective-permute-start.1 = (bf16[128,1024]{0,1:T(8,128)(2,1)S(1)}, bf16[128,1024]{0,1:T(8,128)(2,1)}, u32[]{:S(2)}, u32[]{:S(2)}) collective-permute-start(bf16[128,1024]{0,1:T(8,128)(2,1)S(1)} %copy.16), channel_id=1, source_target_pairs={{0,8},{8,16},{16,24},{24,32},{32,40},{40,48},{48,56},{56,64},{64,7... | collective-permute-start | bytes 786440 | tf_op jit(solution)/shard_map/while/body/eval_jaxpr/ppermute | solution.py:10
  270.5 3.3 collective-permute-done.1
  274.8 6.8 collective-permute-start.1
  286.4 7.5 %collective-permute-start.1 = (bf16[128,1024]{0,1:T(8,128)(2,1)S(1)}, bf16[128,1024]{0,1:T(8,128)(2,1)}, u32[]{:S(2)}, u32[]{:S(2)}) collective-permute-start(bf16[128,1024]{0,1:T(8,128)(2,1)S(1)} %copy.16), channel_id=1, source_target_pairs={{0,8},{8,16},{16,24},{24,32},{32,40},{40,48},{48,56},{56,64},{64,7... | collective-permute-start | bytes 786440 | tf_op jit(solution)/shard_map/while/body/eval_jaxpr/ppermute | solution.py:10
  298.8 7.5 %collective-permute-start.1 = (bf16[128,1024]{0,1:T(8,128)(2,1)S(1)}, bf16[128,1024]{0,1:T(8,128)(2,1)}, u32[]{:S(2)}, u32[]{:S(2)}) collective-permute-start(bf16[128,1024]{0,1:T(8,128)(2,1)S(1)} %copy.16), channel_id=1, source_target_pairs={{0,8},{8,16},{16,24},{24,32},{32,40},{40,48},{48,56},{56,64},{64,7... | collective-permute-start | bytes 786440 | tf_op jit(solution)/shard_map/while/body/eval_jaxpr/ppermute | solution.py:10
  311.1 7.5 %collective-permute-start.1 = (bf16[128,1024]{0,1:T(8,128)(2,1)S(1)}, bf16[128,1024]{0,1:T(8,128)(2,1)}, u32[]{:S(2)}, u32[]{:S(2)}) collective-permute-start(bf16[128,1024]{0,1:T(8,128)(2,1)S(1)} %copy.16), channel_id=1, source_target_pairs={{0,8},{8,16},{16,24},{24,32},{32,40},{40,48},{48,56},{56,64},{64,7... | collective-permute-start | bytes 786440 | tf_op jit(solution)/shard_map/while/body/eval_jaxpr/ppermute | solution.py:10
  323.4 7.5 %collective-permute-start.1 = (bf16[128,1024]{0,1:T(8,128)(2,1)S(1)}, bf16[128,1024]{0,1:T(8,128)(2,1)}, u32[]{:S(2)}, u32[]{:S(2)}) collective-permute-start(bf16[128,1024]{0,1:T(8,128)(2,1)S(1)} %copy.16), channel_id=1, source_target_pairs={{0,8},{8,16},{16,24},{24,32},{32,40},{40,48},{48,56},{56,64},{64,7... | collective-permute-start | bytes 786440 | tf_op jit(solution)/shard_map/while/body/eval_jaxpr/ppermute | solution.py:10
  338.9 42.2 %reduce-scatter.4.cloned.1.call-done = bf16[128,128]{0,1:T(8,128)(2,1)} async-done(((bf16[128,1024]{0,1:T(8,128)(2,1)}), bf16[128,128]{0,1:T(8,128)(2,1)}) %reduce-scatter.4.cloned.1.call-update) | async-done | bytes 32784 | tf_op jit(solution)/shard_map/reduce_scatter | solution.py:71
  382.6 14.4 %all_gather.7 = bf16[128,1024]{1,0:T(8,128)(2,1)S(1)} all-gather(bf16[128,128]{1,0:T(8,128)(2,1)S(1)} %convert_element_type.55), channel_id=1, replica_groups=mesh['blk'=64,'rep'=8] {'rep'}, dimensions={1}, use_global_device_ids=true | all-gather | bytes 294912 | tf_op jit(solution)/shard_map/all_gather | solution.py:105
  397.8 289.3 %reduce-scatter.8.cloned.1.call-done = f32[16,128]{1,0:T(8,128)} async-done(((f32[1024,128]{1,0:T(8,128)}), f32[16,128]{1,0:T(8,128)}) %reduce-scatter.8.cloned.1.call-update) | async-done | bytes 8208 | tf_op jit(solution)/shard_map/reduce_scatter | solution.py:97
  (115 shorter events, 82.6 us)
Async XLA Ops:
  7.2 152.5 %copy-start = (bf16[1024,1024]{1,0:T(8,128)(2,1)S(1)}, bf16[1024,1024]{1,0:T(8,128)(2,1)}, u32[]{:S(2)}) copy-start(bf16[1024,1024]{1,0:T(8,128)(2,1)} %param.12) | copy-start | bytes 6291460
  7.2 329.8 %reduce-scatter.6.cloned.1.call-start = ((), (), s32[]{:S(2)}) async-start(), calls=%async_computation.4 | async-start | bytes 589824 | tf_op jit(solution)/shard_map/reduce_scatter | solution.py:93
  14.4 16.5 %collective-permute-start = (f32[1,128,1024]{2,1,0:T(8,128)}, f32[1,128,1024]{2,1,0:T(8,128)}, u32[]{:S(2)}, u32[]{:S(2)}) collective-permute-start(f32[1,128,1024]{2,1,0:T(8,128)} %bitcast_add_fusion.4), channel_id=1, source_target_pairs={{0,504},{8,0},{16,8},{24,16},{32,24},{40,32},{48,40},{56,48},{64,5... | collective-permute-start | bytes 1572872 | tf_op jit(solution)/shard_map/while/body/eval_jaxpr/ppermute | solution.py:10
  34.2 18.0 %collective-permute-start = (f32[1,128,1024]{2,1,0:T(8,128)}, f32[1,128,1024]{2,1,0:T(8,128)}, u32[]{:S(2)}, u32[]{:S(2)}) collective-permute-start(f32[1,128,1024]{2,1,0:T(8,128)} %bitcast_add_fusion.4), channel_id=1, source_target_pairs={{0,504},{8,0},{16,8},{24,16},{32,24},{40,32},{48,40},{56,48},{64,5... | collective-permute-start | bytes 1572872 | tf_op jit(solution)/shard_map/while/body/eval_jaxpr/ppermute | solution.py:10
  55.5 17.1 %collective-permute-start = (f32[1,128,1024]{2,1,0:T(8,128)}, f32[1,128,1024]{2,1,0:T(8,128)}, u32[]{:S(2)}, u32[]{:S(2)}) collective-permute-start(f32[1,128,1024]{2,1,0:T(8,128)} %bitcast_add_fusion.4), channel_id=1, source_target_pairs={{0,504},{8,0},{16,8},{24,16},{32,24},{40,32},{48,40},{56,48},{64,5... | collective-permute-start | bytes 1572872 | tf_op jit(solution)/shard_map/while/body/eval_jaxpr/ppermute | solution.py:10
  75.9 16.1 %collective-permute-start = (f32[1,128,1024]{2,1,0:T(8,128)}, f32[1,128,1024]{2,1,0:T(8,128)}, u32[]{:S(2)}, u32[]{:S(2)}) collective-permute-start(f32[1,128,1024]{2,1,0:T(8,128)} %bitcast_add_fusion.4), channel_id=1, source_target_pairs={{0,504},{8,0},{16,8},{24,16},{32,24},{40,32},{48,40},{56,48},{64,5... | collective-permute-start | bytes 1572872 | tf_op jit(solution)/shard_map/while/body/eval_jaxpr/ppermute | solution.py:10
  95.3 15.2 %collective-permute-start = (f32[1,128,1024]{2,1,0:T(8,128)}, f32[1,128,1024]{2,1,0:T(8,128)}, u32[]{:S(2)}, u32[]{:S(2)}) collective-permute-start(f32[1,128,1024]{2,1,0:T(8,128)} %bitcast_add_fusion.4), channel_id=1, source_target_pairs={{0,504},{8,0},{16,8},{24,16},{32,24},{40,32},{48,40},{56,48},{64,5... | collective-permute-start | bytes 1572872 | tf_op jit(solution)/shard_map/while/body/eval_jaxpr/ppermute | solution.py:10
  113.9 14.3 %collective-permute-start = (f32[1,128,1024]{2,1,0:T(8,128)}, f32[1,128,1024]{2,1,0:T(8,128)}, u32[]{:S(2)}, u32[]{:S(2)}) collective-permute-start(f32[1,128,1024]{2,1,0:T(8,128)} %bitcast_add_fusion.4), channel_id=1, source_target_pairs={{0,504},{8,0},{16,8},{24,16},{32,24},{40,32},{48,40},{56,48},{64,5... | collective-permute-start | bytes 1572872 | tf_op jit(solution)/shard_map/while/body/eval_jaxpr/ppermute | solution.py:10
  131.5 14.2 %collective-permute-start = (f32[1,128,1024]{2,1,0:T(8,128)}, f32[1,128,1024]{2,1,0:T(8,128)}, u32[]{:S(2)}, u32[]{:S(2)}) collective-permute-start(f32[1,128,1024]{2,1,0:T(8,128)} %bitcast_add_fusion.4), channel_id=1, source_target_pairs={{0,504},{8,0},{16,8},{24,16},{32,24},{40,32},{48,40},{56,48},{64,5... | collective-permute-start | bytes 1572872 | tf_op jit(solution)/shard_map/while/body/eval_jaxpr/ppermute | solution.py:10
  146.9 35.3 %collective-permute-start.5 = (bf16[1,128,1024]{2,1,0:T(8,128)(2,1)S(1)}, bf16[1,128,1024]{2,1,0:T(8,128)(2,1)S(1)}, u32[]{:S(2)}, u32[]{:S(2)}) collective-permute-start(bf16[1,128,1024]{2,1,0:T(8,128)(2,1)S(1)} %get-tuple-element.161), channel_id=1, source_target_pairs={{0,448},{8,456},{16,464},{24,472},{32,480},{40,488},{48,496},{56,5... | collective-permute-start | bytes 786440 | tf_op jit(solution)/shard_map/ppermute | solution.py:10
  180.3 11.8 %collective-permute-start.2 = (bf16[128,1024]{1,0:T(8,128)(2,1)S(1)}, bf16[128,1024]{1,0:T(8,128)(2,1)}, u32[]{:S(2)}, u32[]{:S(2)}) collective-permute-start(bf16[128,1024]{1,0:T(8,128)(2,1)S(1)} %all_gather.6), channel_id=1, source_target_pairs={{0,64},{8,72},{16,80},{24,88},{32,96},{40,104},{48,112},{56,120},{... | collective-permute-start | bytes 786440 | tf_op jit(solution)/shard_map/ppermute | solution.py:10
  183.0 12.4 %collective-permute-start.6 = (bf16[1,128,1024]{2,1,0:T(8,128)(2,1)}, bf16[1,128,1024]{2,1,0:T(8,128)(2,1)S(1)}, u32[]{:S(2)}, u32[]{:S(2)}) collective-permute-start(bf16[1,128,1024]{2,1,0:T(8,128)(2,1)} %fusion.8), channel_id=1, source_target_pairs={{0,384},{8,392},{16,400},{24,408},{32,416},{40,424},{48,432},{56,4... | collective-permute-start | bytes 786440 | tf_op jit(solution)/shard_map/ppermute | solution.py:10
  192.8 17.5 %collective-permute-start.3 = (bf16[128,1024]{1,0:T(8,128)(2,1)}, bf16[128,1024]{1,0:T(8,128)(2,1)}, u32[]{:S(2)}, u32[]{:S(2)}) collective-permute-start(bf16[128,1024]{1,0:T(8,128)(2,1)} %broadcast_select_fusion), channel_id=1, source_target_pairs={{0,128},{8,136},{16,144},{24,152},{32,160},{40,168},{48,176},{56,1... | collective-permute-start | bytes 786440 | tf_op jit(solution)/shard_map/ppermute | solution.py:10
  195.4 5.5 copy-start.3
  196.3 22.5 %collective-permute-start.7 = (bf16[1,128,1024]{2,1,0:T(8,128)(2,1)}, bf16[1,128,1024]{2,1,0:T(8,128)(2,1)}, u32[]{:S(2)}, u32[]{:S(2)}) collective-permute-start(bf16[1,128,1024]{2,1,0:T(8,128)(2,1)} %fusion.17), channel_id=1, source_target_pairs={{0,256},{8,264},{16,272},{24,280},{32,288},{40,296},{48,304},{56,3... | collective-permute-start | bytes 786440 | tf_op jit(solution)/shard_map/ppermute | solution.py:10
  201.0 35.0 %copy-start.1 = (bf16[1,2,128,128]{3,2,1,0:T(8,128)(2,1)S(1)}, bf16[1,2,128,128]{3,2,1,0:T(8,128)(2,1)}, u32[]{:S(2)}) copy-start(bf16[1,2,128,128]{3,2,1,0:T(8,128)(2,1)} %param.10) | copy-start | bytes 196612
  212.0 22.1 %collective-permute-start.4 = (bf16[128,1024]{1,0:T(8,128)(2,1)}, bf16[128,1024]{1,0:T(8,128)(2,1)}, u32[]{:S(2)}, u32[]{:S(2)}) collective-permute-start(bf16[128,1024]{1,0:T(8,128)(2,1)} %broadcast_select_fusion.1), channel_id=1, source_target_pairs={{0,256},{8,264},{16,272},{24,280},{32,288},{40,296},{48,304},{56,3... | collective-permute-start | bytes 786440 | tf_op jit(solution)/shard_map/ppermute | solution.py:10
  220.7 160.4 %reduce-scatter.4.cloned.1.call-start = ((), (), s32[]{:S(2)}) async-start(), calls=%async_computation.3 | async-start | bytes 294912 | tf_op jit(solution)/shard_map/reduce_scatter | solution.py:71
  236.9 17.4 %collective-permute-start.1 = (bf16[128,1024]{0,1:T(8,128)(2,1)S(1)}, bf16[128,1024]{0,1:T(8,128)(2,1)}, u32[]{:S(2)}, u32[]{:S(2)}) collective-permute-start(bf16[128,1024]{0,1:T(8,128)(2,1)S(1)} %copy.16), channel_id=1, source_target_pairs={{0,8},{8,16},{16,24},{24,32},{32,40},{40,48},{48,56},{56,64},{64,7... | collective-permute-start | bytes 786440 | tf_op jit(solution)/shard_map/while/body/eval_jaxpr/ppermute | solution.py:10
  255.3 18.5 %collective-permute-start.1 = (bf16[128,1024]{0,1:T(8,128)(2,1)S(1)}, bf16[128,1024]{0,1:T(8,128)(2,1)}, u32[]{:S(2)}, u32[]{:S(2)}) collective-permute-start(bf16[128,1024]{0,1:T(8,128)(2,1)S(1)} %copy.16), channel_id=1, source_target_pairs={{0,8},{8,16},{16,24},{24,32},{32,40},{40,48},{48,56},{56,64},{64,7... | collective-permute-start | bytes 786440 | tf_op jit(solution)/shard_map/while/body/eval_jaxpr/ppermute | solution.py:10
  274.8 10.7 %collective-permute-start.1 = (bf16[128,1024]{0,1:T(8,128)(2,1)S(1)}, bf16[128,1024]{0,1:T(8,128)(2,1)}, u32[]{:S(2)}, u32[]{:S(2)}) collective-permute-start(bf16[128,1024]{0,1:T(8,128)(2,1)S(1)} %copy.16), channel_id=1, source_target_pairs={{0,8},{8,16},{16,24},{24,32},{32,40},{40,48},{48,56},{56,64},{64,7... | collective-permute-start | bytes 786440 | tf_op jit(solution)/shard_map/while/body/eval_jaxpr/ppermute | solution.py:10
  286.4 11.4 %collective-permute-start.1 = (bf16[128,1024]{0,1:T(8,128)(2,1)S(1)}, bf16[128,1024]{0,1:T(8,128)(2,1)}, u32[]{:S(2)}, u32[]{:S(2)}) collective-permute-start(bf16[128,1024]{0,1:T(8,128)(2,1)S(1)} %copy.16), channel_id=1, source_target_pairs={{0,8},{8,16},{16,24},{24,32},{32,40},{40,48},{48,56},{56,64},{64,7... | collective-permute-start | bytes 786440 | tf_op jit(solution)/shard_map/while/body/eval_jaxpr/ppermute | solution.py:10
  298.8 11.4 %collective-permute-start.1 = (bf16[128,1024]{0,1:T(8,128)(2,1)S(1)}, bf16[128,1024]{0,1:T(8,128)(2,1)}, u32[]{:S(2)}, u32[]{:S(2)}) collective-permute-start(bf16[128,1024]{0,1:T(8,128)(2,1)S(1)} %copy.16), channel_id=1, source_target_pairs={{0,8},{8,16},{16,24},{24,32},{32,40},{40,48},{48,56},{56,64},{64,7... | collective-permute-start | bytes 786440 | tf_op jit(solution)/shard_map/while/body/eval_jaxpr/ppermute | solution.py:10
  311.1 11.4 %collective-permute-start.1 = (bf16[128,1024]{0,1:T(8,128)(2,1)S(1)}, bf16[128,1024]{0,1:T(8,128)(2,1)}, u32[]{:S(2)}, u32[]{:S(2)}) collective-permute-start(bf16[128,1024]{0,1:T(8,128)(2,1)S(1)} %copy.16), channel_id=1, source_target_pairs={{0,8},{8,16},{16,24},{24,32},{32,40},{40,48},{48,56},{56,64},{64,7... | collective-permute-start | bytes 786440 | tf_op jit(solution)/shard_map/while/body/eval_jaxpr/ppermute | solution.py:10
  323.4 11.4 %collective-permute-start.1 = (bf16[128,1024]{0,1:T(8,128)(2,1)S(1)}, bf16[128,1024]{0,1:T(8,128)(2,1)}, u32[]{:S(2)}, u32[]{:S(2)}) collective-permute-start(bf16[128,1024]{0,1:T(8,128)(2,1)S(1)} %copy.16), channel_id=1, source_target_pairs={{0,8},{8,16},{16,24},{24,32},{32,40},{40,48},{48,56},{56,64},{64,7... | collective-permute-start | bytes 786440 | tf_op jit(solution)/shard_map/while/body/eval_jaxpr/ppermute | solution.py:10
  334.8 3.1 copy-start.2
  337.0 350.2 %reduce-scatter.8.cloned.1.call-start = ((), (), s32[]{:S(2)}) async-start(), calls=%async_computation.5 | async-start | bytes 532480 | tf_op jit(solution)/shard_map/reduce_scatter | solution.py:97
Sparse Core Ops, SparseCore 0:
  220.8 57.6 reduce-scatter.5
  337.1 43.9 reduce-scatter.3
  384.5 302.5 reduce-scatter.7
where the time goes:
time: 706 us; the launch traced here: 694 us
  waiting for transfers between devices  473 us (67%)
  starting transfers between devices  110 us (16%)
  blocking collectives  33.9 us (5%)
  other arithmetic  30.9 us (4%)
  local copies, waits for them, and re-layouts  18.1 us (3%)
  between operations  13.9 us (2%)
  matrix products  8.2 us (1%)
    reduce_scatter x1, waiting for transfers between devices, shards(): lax.psum_scatter(lax.dot_general(hidden_act, back_grad, (((0,), (0,)), ((...  289 us
    ppermute x20, waiting for transfers between devices, passed_along(): return lax.ppermute(value, axis, pairs)  142 us
    ppermute x20, starting transfers between devices, passed_along(): return lax.ppermute(value, axis, pairs)  110 us
    reduce_scatter x1, waiting for transfers between devices, shards(): lax.psum_scatter(output_sum.reshape(row_count, feature_width).astype(jnp....  42.2 us
    all_gather x1, blocking collectives, shards(): projected = lax.all_gather(partial_value, 'rep', axis=1, tiled=True)  19.5 us
    all_gather x1, blocking collectives, shards(): back_full = lax.all_gather(back_grad, 'rep', axis=1, tiled=True)  14.4 us
  transfers between devices with their start and end apart: 23, of which 21 were waited for; matrix products, arithmetic and copies ran while one was open for 5% of the time, Pallas kernels for 0%

commit v1 on v0

v1 whole, which is shorter than its diff:
```python
import math

import jax
import jax.numpy as jnp
from jax import lax
from jax.sharding import Mesh
from jax.sharding import PartitionSpec as P

BLK = ("by", "bx", "bz")
REP = ("rz", "rc")
EVERY = BLK + REP


def shifted_pairs(blk_count, rep_count, per_rep):
    pairs = []
    for b in range(blk_count):
        for r in range(rep_count):
            pairs.append((b * rep_count + r, ((b + per_rep * r) % blk_count) * rep_count + r))
    return pairs


def ring_pairs(count, steps):
    return [(source, (source + steps) % count) for source in range(count)]


def staged_scatter(value, axes, dim):
    sizes = [lax.axis_size(a) for a in axes]
    full = value.shape[dim]
    rest = full // math.prod(sizes)
    shape = value.shape[:dim] + tuple(sizes) + (rest,) + value.shape[dim + 1 :]
    moved = value.reshape(shape)
    order = list(range(dim)) + [dim + i for i in reversed(range(len(axes)))]
    order += list(range(dim + len(axes), len(shape)))
    moved = jnp.transpose(moved, order).reshape(value.shape)
    for a in reversed(axes):
        moved = lax.psum_scatter(moved, a, scatter_dimension=dim, tiled=True)
    return moved


def shards(hidden_pre, adj_vals, adj_cols, w_out, cotangent):
    row_count, feature_width = hidden_pre.shape
    blk_count = lax.axis_size(BLK)
    rep_count = lax.axis_size(REP)
    span = blk_count // rep_count
    blk_pos = lax.axis_index(BLK)
    rep_pos = lax.axis_index(REP)
    cols_here = feature_width // rep_count
    slots = adj_vals.shape[1]

    hidden_act = jnp.maximum(hidden_pre, 0)
    projected = jnp.dot(hidden_act, w_out, preferred_element_type=jnp.float32).astype(jnp.bfloat16)
    own_vals = adj_vals[0]
    own_cols = adj_cols[0]
    section = jnp.mod(blk_pos - own_cols, blk_count) - rep_pos * span

    visiting = lax.ppermute(projected, EVERY, shifted_pairs(blk_count, rep_count, span))
    back = shifted_pairs(blk_count, rep_count, -span)
    cot_cur = lax.ppermute(cotangent, EVERY, back)
    vals_cur = lax.ppermute(own_vals, EVERY, back)
    cols_cur = lax.ppermute(own_cols, EVERY, back)

    out_sum = jnp.zeros((row_count, feature_width), jnp.float32)
    back_sum = jnp.zeros((row_count, feature_width), jnp.float32)
    for turn in range(span):
        chosen = jnp.zeros_like(own_vals[0])
        for k in range(slots):
            chosen = chosen + jnp.where(section[k] == turn, own_vals[k], 0)
        out_sum = out_sum + jnp.dot(chosen, visiting, preferred_element_type=jnp.float32)
        chosen_back = jnp.zeros_like(own_vals[0])
        for k in range(slots):
            chosen_back = chosen_back + jnp.where(cols_cur[k] == blk_pos, vals_cur[k], 0)
        back_sum = back_sum + lax.dot_general(
            chosen_back, cot_cur, (((0,), (0,)), ((), ())), preferred_element_type=jnp.float32
        )
        if turn < span - 1:
            visiting = lax.ppermute(visiting, BLK, ring_pairs(blk_count, 1))
            cot_cur = lax.ppermute(cot_cur, BLK, ring_pairs(blk_count, -1))
            vals_cur = lax.ppermute(vals_cur, BLK, ring_pairs(blk_count, -1))
            cols_cur = lax.ppermute(cols_cur, BLK, ring_pairs(blk_count, -1))

    out_part = staged_scatter(out_sum.astype(jnp.bfloat16), REP, 1)
    back_part = staged_scatter(back_sum, REP, 1)
    back_grad = back_part.astype(jnp.bfloat16)
    term = lax.dot_general(
        hidden_act, back_grad, (((0,), (0,)), ((), ())), preferred_element_type=jnp.float32
    )
    grad_weight = staged_scatter(term, BLK, 0)
    back_full = lax.all_gather(back_grad, REP, axis=1, tiled=True)
    w_rows = lax.dynamic_slice_in_dim(w_out, rep_pos * cols_here, cols_here, 0)
    grad_in = lax.dot_general(
        back_full, w_rows, (((1,), (1,)), ((), ())), preferred_element_type=jnp.float32
    )
    pre_part = lax.dynamic_slice_in_dim(hidden_pre, rep_pos * cols_here, cols_here, 1)
    grad_pre = jnp.where(pre_part > 0, grad_in, 0.0).astype(jnp.bfloat16)
    return (out_part, grad_weight, grad_pre)


def solution(mesh):
    blk_count, rep_count = mesh.devices.shape
    fine = Mesh(mesh.devices.reshape(8, blk_count // 16, 2, rep_count // 2, 2), EVERY)
    placed = (P(BLK, None), P(BLK, REP, None, None), P(BLK, REP), P(), P(BLK, None))
    return jax.shard_map(
        shards,
        mesh=fine,
        in_specs=placed,
        out_specs=(P(BLK, REP), P(BLK, REP), P(BLK, REP)),
        check_vma=False,
    )
```

time: 706 us -> 411 us (0.58); the launches traced: 694 us -> 409 us
  waiting for transfers between devices: 473 us -> 223 us
  other arithmetic: 30.9 us -> 0.86 us
  between operations: 13.9 us -> 35.6 us
  blocking collectives: 33.9 us -> 14.6 us
    reduce_scatter x3 -> x6, waiting for transfers between devices: 331 us -> 151 us  [staged_scatter(): moved = lax.psum_scatter(moved, a, scatter_dimension=dim, tiled=True)]
    ppermute x20 -> x32, waiting for transfers between devices: 142 us -> 41 us  [the longest x7 14.6 us: shards(): visiting = lax.ppermute(visiting, BLK, ring_pairs(blk_count, 1))]
    unnamed x3 -> x8, waiting for transfers between devices: 0.05 us -> 31.7 us
    all_gather x2 -> x1, blocking collectives: 33.9 us -> 14.6 us  [shards(): back_full = lax.all_gather(back_grad, REP, axis=1, tiled=True)]
    add x7 -> x0, other arithmetic: 13.2 us -> none  [carry_step(): carried + spread_into(pick_mask(section_span - 1 - turn_index), contribut...]
    dynamic_slice x14 -> x0, local copies, waits for them, and re-layouts: 8.2 us -> none  [shards(): lax.scan(forward_step, (visiting, zero_out), jnp.arange(section_span - 1,...]
    ppermute x20 -> x32, starting transfers between devices: 110 us -> 109 us  [the longest x7 32.4 us: shards(): vals_cur = lax.ppermute(vals_cur, BLK, ring_pairs(blk_count, -1))]
  transfers between devices with their start and end apart: 23 -> 39, of which waited for: 21 -> 16; matrix products, arithmetic and copies ran while one was open for 5% -> 6% of each run, Pallas kernels for 0% -> 0%
where the time goes in v1:
time: 411 us; the launch traced here: 409 us
  waiting for transfers between devices  223 us (54%)
  starting transfers between devices  110 us (27%)
  between operations  35.6 us (9%)
  blocking collectives  14.6 us (4%)
  matrix products  12.7 us (3%)
  local copies, waits for them, and re-layouts  12.4 us (3%)
    reduce_scatter x6, waiting for transfers between devices, staged_scatter(): moved = lax.psum_scatter(moved, a, scatter_dimension=dim, tiled=True)  151 us
    ppermute x7, starting transfers between devices, shards(): vals_cur = lax.ppermute(vals_cur, BLK, ring_pairs(blk_count, -1))  32.4 us
    unnamed x8, waiting for transfers between devices  31.7 us
    ppermute x7, starting transfers between devices, shards(): cot_cur = lax.ppermute(cot_cur, BLK, ring_pairs(blk_count, -1))  28.9 us
    ppermute x7, starting transfers between devices, shards(): cols_cur = lax.ppermute(cols_cur, BLK, ring_pairs(blk_count, -1))  22.7 us
    ppermute x7, starting transfers between devices, shards(): visiting = lax.ppermute(visiting, BLK, ring_pairs(blk_count, 1))  20.2 us
    all_gather x1, blocking collectives, shards(): back_full = lax.all_gather(back_grad, REP, axis=1, tiled=True)  14.6 us
    ppermute x7, waiting for transfers between devices, shards(): visiting = lax.ppermute(visiting, BLK, ring_pairs(blk_count, 1))  14.6 us
  transfers between devices with their start and end apart: 39, of which 16 were waited for; matrix products, arithmetic and copies ran while one was open for 6% of the time, Pallas kernels for 0%

profile of v1, /device:TPU:6, one launch (start us, length us, event | category | flops | bytes accessed | tf_op | source)
XLA Modules:
  0.0 409.2 jit_solution(951404215422143867)
XLA Ops:
  13.9 4.5 %collective-permute-start.13 = (bf16[128,1024]{1,0:T(8,128)(2,1)S(1)}, bf16[128,1024]{1,0:T(8,128)(2,1)S(1)}, u32[]{:S(2)}, u32[]{:S(2)}) collective-permute-start(bf16[128,1024]{1,0:T(8,128)(2,1)S(1)} %collective-permute-done.10), channel_id=1, source_target_pairs={{0,504},{8,0},{16,8},{24,16},{32,24},{40,32},{48,40},{56,48},{64,5... | collective-permute-start | bytes 786440 | tf_op jit(solution)/shard_map/ppermute | solution.py:77
  33.3 3.9 collective-permute-start.16
  41.5 3.3 collective-permute-done.14
  49.8 5.3 %collective-permute-start.12 = (bf16[2,128,128]{2,1,0:T(8,128)(2,1)S(1)}, bf16[2,128,128]{2,1,0:T(8,128)(2,1)S(1)}, u32[]{:S(2)}, u32[]{:S(2)}) collective-permute-start(bf16[2,128,128]{2,1,0:T(8,128)(2,1)S(1)} %collective-permute-done.9), channel_id=1, source_target_pairs={{0,504},{8,0},{16,8},{24,16},{32,24},{40,32},{48,40},{56,48},{64,5... | collective-permute-start | bytes 196616 | tf_op jit(solution)/shard_map/ppermute | solution.py:78
  57.2 5.0 %collective-permute-start.20 = (s32[2]{0:T(128)S(1)}, s32[2]{0:T(128)S(1)}, u32[]{:S(2)}, u32[]{:S(2)}) collective-permute-start(s32[2]{0:T(128)S(1)} %collective-permute-done.17), channel_id=1, source_target_pairs={{0,504},{8,0},{16,8},{24,16},{32,24},{40,32},{48,40},{56,48},{64,5... | collective-permute-start | bytes 32 | tf_op jit(solution)/shard_map/ppermute | solution.py:79
  62.2 3.0 collective-permute-start.15
  68.1 3.9 collective-permute-start.19
  76.6 8.4 %collective-permute-start.18 = (bf16[2,128,128]{2,1,0:T(8,128)(2,1)}, bf16[2,128,128]{2,1,0:T(8,128)(2,1)}, u32[]{:S(2)}, u32[]{:S(2)}) collective-permute-start(bf16[2,128,128]{2,1,0:T(8,128)(2,1)} %collective-permute-done.15), channel_id=1, source_target_pairs={{0,504},{8,0},{16,8},{24,16},{32,24},{40,32},{48,40},{56,48},{64,5... | collective-permute-start | bytes 196616 | tf_op jit(solution)/shard_map/ppermute | solution.py:78
  87.1 3.9 collective-permute-start.26
  91.0 5.7 %collective-permute-start.21 = (bf16[2,128,128]{2,1,0:T(8,128)(2,1)}, bf16[2,128,128]{2,1,0:T(8,128)(2,1)}, u32[]{:S(2)}, u32[]{:S(2)}) collective-permute-start(bf16[2,128,128]{2,1,0:T(8,128)(2,1)} %collective-permute-done.18), channel_id=1, source_target_pairs={{0,504},{8,0},{16,8},{24,16},{32,24},{40,32},{48,40},{56,48},{64,5... | collective-permute-start | bytes 196616 | tf_op jit(solution)/shard_map/ppermute | solution.py:78
  98.7 3.9 collective-permute-start.29
  102.7 6.1 %collective-permute-start.24 = (bf16[2,128,128]{2,1,0:T(8,128)(2,1)}, bf16[2,128,128]{2,1,0:T(8,128)(2,1)}, u32[]{:S(2)}, u32[]{:S(2)}) collective-permute-start(bf16[2,128,128]{2,1,0:T(8,128)(2,1)} %collective-permute-done.21), channel_id=1, source_target_pairs={{0,504},{8,0},{16,8},{24,16},{32,24},{40,32},{48,40},{56,48},{64,5... | collective-permute-start | bytes 196616 | tf_op jit(solution)/shard_map/ppermute | solution.py:78
  110.8 4.8 %collective-permute-start.22 = (bf16[128,1024]{1,0:T(8,128)(2,1)}, bf16[128,1024]{1,0:T(8,128)(2,1)}, u32[]{:S(2)}, u32[]{:S(2)}) collective-permute-start(bf16[128,1024]{1,0:T(8,128)(2,1)} %collective-permute-done.19), channel_id=1, source_target_pairs={{0,504},{8,0},{16,8},{24,16},{32,24},{40,32},{48,40},{56,48},{64,5... | collective-permute-start | bytes 786440 | tf_op jit(solution)/shard_map/ppermute | solution.py:77
  119.6 9.3 %collective-permute-done.27 = bf16[2,128,128]{2,1,0:T(8,128)(2,1)S(1)} collective-permute-done((bf16[2,128,128]{2,1,0:T(8,128)(2,1)}, bf16[2,128,128]{2,1,0:T(8,128)(2,1)S(1)}, u32[]{:S(2)}, u32[]{:S(2)}) %collective-permute-start.27) | collective-permute-done | bytes 65568 | tf_op jit(solution)/shard_map/ppermute | solution.py:78
  130.8 3.9 collective-permute-start.3
  138.9 4.2 %collective-permute-done.3 = bf16[128,1024]{1,0:T(8,128)(2,1)} collective-permute-done((bf16[128,1024]{1,0:T(8,128)(2,1)}, bf16[128,1024]{1,0:T(8,128)(2,1)}, u32[]{:S(2)}, u32[]{:S(2)}) %collective-permute-start.3) | collective-permute-done | bytes 262176 | tf_op jit(solution)/shard_map/ppermute | solution.py:76
  143.1 3.1 collective-permute-start.4
  147.4 5.2 %collective-permute-start.28 = (bf16[128,1024]{1,0:T(8,128)(2,1)S(1)}, bf16[128,1024]{1,0:T(8,128)(2,1)S(1)}, u32[]{:S(2)}, u32[]{:S(2)}) collective-permute-start(bf16[128,1024]{1,0:T(8,128)(2,1)S(1)} %collective-permute-done.25), channel_id=1, source_target_pairs={{0,504},{8,0},{16,8},{24,16},{32,24},{40,32},{48,40},{56,48},{64,5... | collective-permute-start | bytes 786440 | tf_op jit(solution)/shard_map/ppermute | solution.py:77
  155.1 3.9 collective-permute-done.28
  159.0 3.7 collective-permute-start.31
  164.0 8.5 %collective-permute-done.31 = bf16[128,1024]{1,0:T(8,128)(2,1)S(1)} collective-permute-done((bf16[128,1024]{1,0:T(8,128)(2,1)S(1)}, bf16[128,1024]{1,0:T(8,128)(2,1)S(1)}, u32[]{:S(2)}, u32[]{:S(2)}) %collective-permute-start.31) | collective-permute-done | bytes 262176 | tf_op jit(solution)/shard_map/ppermute | solution.py:77
  174.6 4.5 %collective-permute-start.5 = (bf16[128,1024]{1,0:T(8,128)(2,1)}, bf16[128,1024]{1,0:T(8,128)(2,1)S(1)}, u32[]{:S(2)}, u32[]{:S(2)}) collective-permute-start(bf16[128,1024]{1,0:T(8,128)(2,1)} %collective-permute-done.4), channel_id=1, source_target_pairs={{0,8},{8,16},{16,24},{24,32},{32,40},{40,48},{48,56},{56,64},{64,7... | collective-permute-start | bytes 786440 | tf_op jit(solution)/shard_map/ppermute | solution.py:76
  180.5 5.0 %collective-permute-done.5 = bf16[128,1024]{1,0:T(8,128)(2,1)S(1)} collective-permute-done((bf16[128,1024]{1,0:T(8,128)(2,1)}, bf16[128,1024]{1,0:T(8,128)(2,1)S(1)}, u32[]{:S(2)}, u32[]{:S(2)}) %collective-permute-start.5) | collective-permute-done | bytes 262176 | tf_op jit(solution)/shard_map/ppermute | solution.py:76
  189.9 5.4 %collective-permute-done.6 = bf16[128,1024]{1,0:T(8,128)(2,1)S(1)} collective-permute-done((bf16[128,1024]{1,0:T(8,128)(2,1)S(1)}, bf16[128,1024]{1,0:T(8,128)(2,1)S(1)}, u32[]{:S(2)}, u32[]{:S(2)}) %collective-permute-start.6) | collective-permute-done | bytes 262176 | tf_op jit(solution)/shard_map/ppermute | solution.py:76
  197.2 20.1 %reduce-scatter.12.cloned.1.call-done = f32[128,512]{0,1:T(8,128)} async-done(((f32[128,1024]{0,1:T(8,128)}), f32[128,512]{0,1:T(8,128)}) %reduce-scatter.12.cloned.1.call-update) | async-done | bytes 262160 | tf_op jit(solution)/shard_map/reduce_scatter | solution.py:36
  219.3 39.4 %reduce-scatter.14.cloned.1.call-done = f32[128,128]{0,1:T(8,128)} async-done(((f32[128,512]{0,1:T(8,128)}), f32[128,128]{0,1:T(8,128)}) %reduce-scatter.14.cloned.1.call-update) | async-done | bytes 65552 | tf_op jit(solution)/shard_map/reduce_scatter | solution.py:36
  260.7 14.8 %reduce-scatter.10.cloned.1.call-done = bf16[128,512]{1,0:T(8,128)(2,1)} async-done(((bf16[128,1024]{1,0:T(8,128)(2,1)}), bf16[128,512]{1,0:T(8,128)(2,1)}) %reduce-scatter.10.cloned.1.call-update) | async-done | bytes 131088 | tf_op jit(solution)/shard_map/reduce_scatter | solution.py:36
  277.2 25.1 %reduce-scatter.16.cloned.1.call-done = f32[512,128]{1,0:T(8,128)} async-done(((f32[1024,128]{1,0:T(8,128)}), f32[512,128]{1,0:T(8,128)}) %reduce-scatter.16.cloned.1.call-update) | async-done | bytes 262160 | tf_op jit(solution)/shard_map/reduce_scatter | solution.py:36
  302.4 31.6 %reduce-scatter.22.cloned.1.call-done = bf16[128,128]{1,0:T(8,128)(2,1)} async-done(((bf16[512,128]{1,0:T(8,128)(2,1)}), bf16[128,128]{1,0:T(8,128)(2,1)}) %reduce-scatter.22.cloned.1.call-update) | async-done | bytes 32784
  335.5 14.6 %all_gather.3 = bf16[128,1024]{0,1:T(8,128)(2,1)S(1)} all-gather(bf16[128,128]{0,1:T(8,128)(2,1)S(1)} %convert_element_type.47), channel_id=1, replica_groups=mesh['by'=8,'bx'=4,'bz'=2,'rz'=4,'rc'=2] {'rz','rc'}, dimensions={1}, use_global_device_ids=true | all-gather | bytes 294912 | tf_op jit(solution)/shard_map/all_gather | solution.py:88
  350.1 9.2 %reduce-scatter.18.cloned.1.call-done = f32[128,128]{1,0:T(8,128)} async-done(((f32[512,128]{1,0:T(8,128)}), f32[128,128]{1,0:T(8,128)}) %reduce-scatter.18.cloned.1.call-update) | async-done | bytes 65552 | tf_op jit(solution)/shard_map/reduce_scatter | solution.py:36
  360.3 42.1 %reduce-scatter.20.cloned.1.call-done = f32[16,128]{1,0:T(8,128)} async-done(((f32[128,128]{1,0:T(8,128)}), f32[16,128]{1,0:T(8,128)}) %reduce-scatter.20.cloned.1.call-update) | async-done | bytes 8208 | tf_op jit(solution)/shard_map/reduce_scatter | solution.py:36
  (104 shorter events, 58.2 us)
Async XLA Ops:
  7.2 210.1 %reduce-scatter.12.cloned.1.call-start = ((), (), s32[]{:S(2)}) async-start(), calls=%async_computation.8 | async-start | bytes 786432 | tf_op jit(solution)/shard_map/reduce_scatter | solution.py:36
  7.2 22.2 %collective-permute-start.8 = (s32[2]{0:T(128)}, s32[2]{0:T(128)S(1)}, u32[]{:S(2)}, u32[]{:S(2)}) collective-permute-start(s32[2]{0:T(128)} %bitcast.119), channel_id=1, source_target_pairs={{0,0},{1,449},{2,386},{3,323},{4,260},{5,197},{6,134},{7,71},{8,8}... | collective-permute-start | bytes 32 | tf_op jit(solution)/shard_map/ppermute | solution.py:60
  10.3 39.5 %collective-permute-start.9 = (bf16[2,128,128]{2,1,0:T(8,128)(2,1)}, bf16[2,128,128]{2,1,0:T(8,128)(2,1)S(1)}, u32[]{:S(2)}, u32[]{:S(2)}) collective-permute-start(bf16[2,128,128]{2,1,0:T(8,128)(2,1)} %bitcast.115), channel_id=1, source_target_pairs={{0,0},{1,449},{2,386},{3,323},{4,260},{5,197},{6,134},{7,71},{8,8}... | collective-permute-start | bytes 196616 | tf_op jit(solution)/shard_map/ppermute | solution.py:59
  13.2 52.1 %collective-permute-start = (bf16[128,1024]{1,0:T(8,128)(2,1)S(1)}, bf16[128,1024]{1,0:T(8,128)(2,1)S(1)}, u32[]{:S(2)}, u32[]{:S(2)}) collective-permute-start(bf16[128,1024]{1,0:T(8,128)(2,1)S(1)} %convolution_convert_fusion), channel_id=1, source_target_pairs={{0,0},{1,65},{2,130},{3,195},{4,260},{5,325},{6,390},{7,455},{8,8}... | collective-permute-start | bytes 786440 | tf_op jit(solution)/shard_map/ppermute | solution.py:56
  13.9 19.4 %collective-permute-start.13 = (bf16[128,1024]{1,0:T(8,128)(2,1)S(1)}, bf16[128,1024]{1,0:T(8,128)(2,1)S(1)}, u32[]{:S(2)}, u32[]{:S(2)}) collective-permute-start(bf16[128,1024]{1,0:T(8,128)(2,1)S(1)} %collective-permute-done.10), channel_id=1, source_target_pairs={{0,504},{8,0},{16,8},{24,16},{32,24},{40,32},{48,40},{56,48},{64,5... | collective-permute-start | bytes 786440 | tf_op jit(solution)/shard_map/ppermute | solution.py:77
  33.3 34.8 %collective-permute-start.16 = (bf16[128,1024]{1,0:T(8,128)(2,1)S(1)}, bf16[128,1024]{1,0:T(8,128)(2,1)S(1)}, u32[]{:S(2)}, u32[]{:S(2)}) collective-permute-start(bf16[128,1024]{1,0:T(8,128)(2,1)S(1)} %collective-permute-done.13), channel_id=1, source_target_pairs={{0,504},{8,0},{16,8},{24,16},{32,24},{40,32},{48,40},{56,48},{64,5... | collective-permute-start | bytes 786440 | tf_op jit(solution)/shard_map/ppermute | solution.py:77
  49.8 12.4 %collective-permute-start.12 = (bf16[2,128,128]{2,1,0:T(8,128)(2,1)S(1)}, bf16[2,128,128]{2,1,0:T(8,128)(2,1)S(1)}, u32[]{:S(2)}, u32[]{:S(2)}) collective-permute-start(bf16[2,128,128]{2,1,0:T(8,128)(2,1)S(1)} %collective-permute-done.9), channel_id=1, source_target_pairs={{0,504},{8,0},{16,8},{24,16},{32,24},{40,32},{48,40},{56,48},{64,5... | collective-permute-start | bytes 196616 | tf_op jit(solution)/shard_map/ppermute | solution.py:78
  57.2 14.8 %collective-permute-start.20 = (s32[2]{0:T(128)S(1)}, s32[2]{0:T(128)S(1)}, u32[]{:S(2)}, u32[]{:S(2)}) collective-permute-start(s32[2]{0:T(128)S(1)} %collective-permute-done.17), channel_id=1, source_target_pairs={{0,504},{8,0},{16,8},{24,16},{32,24},{40,32},{48,40},{56,48},{64,5... | collective-permute-start | bytes 32 | tf_op jit(solution)/shard_map/ppermute | solution.py:79
  62.2 14.4 %collective-permute-start.15 = (bf16[2,128,128]{2,1,0:T(8,128)(2,1)S(1)}, bf16[2,128,128]{2,1,0:T(8,128)(2,1)}, u32[]{:S(2)}, u32[]{:S(2)}) collective-permute-start(bf16[2,128,128]{2,1,0:T(8,128)(2,1)S(1)} %collective-permute-done.12), channel_id=1, source_target_pairs={{0,504},{8,0},{16,8},{24,16},{32,24},{40,32},{48,40},{56,48},{64,5... | collective-permute-start | bytes 196616 | tf_op jit(solution)/shard_map/ppermute | solution.py:78
  65.3 43.6 %collective-permute-start.1 = (bf16[128,1024]{1,0:T(8,128)(2,1)S(1)}, bf16[128,1024]{1,0:T(8,128)(2,1)S(1)}, u32[]{:S(2)}, u32[]{:S(2)}) collective-permute-start(bf16[128,1024]{1,0:T(8,128)(2,1)S(1)} %collective-permute-done), channel_id=1, source_target_pairs={{0,8},{8,16},{16,24},{24,32},{32,40},{40,48},{48,56},{56,64},{64,7... | collective-permute-start | bytes 786440 | tf_op jit(solution)/shard_map/ppermute | solution.py:76
  68.1 42.7 %collective-permute-start.19 = (bf16[128,1024]{1,0:T(8,128)(2,1)S(1)}, bf16[128,1024]{1,0:T(8,128)(2,1)}, u32[]{:S(2)}, u32[]{:S(2)}) collective-permute-start(bf16[128,1024]{1,0:T(8,128)(2,1)S(1)} %collective-permute-done.16), channel_id=1, source_target_pairs={{0,504},{8,0},{16,8},{24,16},{32,24},{40,32},{48,40},{56,48},{64,5... | collective-permute-start | bytes 786440 | tf_op jit(solution)/shard_map/ppermute | solution.py:77
  74.0 11.0 %collective-permute-start.23 = (s32[2]{0:T(128)S(1)}, s32[2]{0:T(128)S(1)}, u32[]{:S(2)}, u32[]{:S(2)}) collective-permute-start(s32[2]{0:T(128)S(1)} %collective-permute-done.20), channel_id=1, source_target_pairs={{0,504},{8,0},{16,8},{24,16},{32,24},{40,32},{48,40},{56,48},{64,5... | collective-permute-start | bytes 32 | tf_op jit(solution)/shard_map/ppermute | solution.py:79
  76.6 14.4 %collective-permute-start.18 = (bf16[2,128,128]{2,1,0:T(8,128)(2,1)}, bf16[2,128,128]{2,1,0:T(8,128)(2,1)}, u32[]{:S(2)}, u32[]{:S(2)}) collective-permute-start(bf16[2,128,128]{2,1,0:T(8,128)(2,1)} %collective-permute-done.15), channel_id=1, source_target_pairs={{0,504},{8,0},{16,8},{24,16},{32,24},{40,32},{48,40},{56,48},{64,5... | collective-permute-start | bytes 196616 | tf_op jit(solution)/shard_map/ppermute | solution.py:78
  91.0 11.7 %collective-permute-start.21 = (bf16[2,128,128]{2,1,0:T(8,128)(2,1)}, bf16[2,128,128]{2,1,0:T(8,128)(2,1)}, u32[]{:S(2)}, u32[]{:S(2)}) collective-permute-start(bf16[2,128,128]{2,1,0:T(8,128)(2,1)} %collective-permute-done.18), channel_id=1, source_target_pairs={{0,504},{8,0},{16,8},{24,16},{32,24},{40,32},{48,40},{56,48},{64,5... | collective-permute-start | bytes 196616 | tf_op jit(solution)/shard_map/ppermute | solution.py:78
  98.7 16.9 %collective-permute-start.29 = (s32[2]{0:T(128)S(1)}, s32[2]{0:T(128)S(1)}, u32[]{:S(2)}, u32[]{:S(2)}) collective-permute-start(s32[2]{0:T(128)S(1)} %collective-permute-done.26), channel_id=1, source_target_pairs={{0,504},{8,0},{16,8},{24,16},{32,24},{40,32},{48,40},{56,48},{64,5... | collective-permute-start | bytes 32 | tf_op jit(solution)/shard_map/ppermute | solution.py:79
  102.7 14.8 %collective-permute-start.24 = (bf16[2,128,128]{2,1,0:T(8,128)(2,1)}, bf16[2,128,128]{2,1,0:T(8,128)(2,1)}, u32[]{:S(2)}, u32[]{:S(2)}) collective-permute-start(bf16[2,128,128]{2,1,0:T(8,128)(2,1)} %collective-permute-done.21), channel_id=1, source_target_pairs={{0,504},{8,0},{16,8},{24,16},{32,24},{40,32},{48,40},{56,48},{64,5... | collective-permute-start | bytes 196616 | tf_op jit(solution)/shard_map/ppermute | solution.py:78
  108.9 22.0 %collective-permute-start.2 = (bf16[128,1024]{1,0:T(8,128)(2,1)S(1)}, bf16[128,1024]{1,0:T(8,128)(2,1)}, u32[]{:S(2)}, u32[]{:S(2)}) collective-permute-start(bf16[128,1024]{1,0:T(8,128)(2,1)S(1)} %collective-permute-done.1), channel_id=1, source_target_pairs={{0,8},{8,16},{16,24},{24,32},{32,40},{40,48},{48,56},{56,64},{64,7... | collective-permute-start | bytes 786440 | tf_op jit(solution)/shard_map/ppermute | solution.py:76
  110.8 24.0 %collective-permute-start.22 = (bf16[128,1024]{1,0:T(8,128)(2,1)}, bf16[128,1024]{1,0:T(8,128)(2,1)}, u32[]{:S(2)}, u32[]{:S(2)}) collective-permute-start(bf16[128,1024]{1,0:T(8,128)(2,1)} %collective-permute-done.19), channel_id=1, source_target_pairs={{0,504},{8,0},{16,8},{24,16},{32,24},{40,32},{48,40},{56,48},{64,5... | collective-permute-start | bytes 786440 | tf_op jit(solution)/shard_map/ppermute | solution.py:77
  117.5 11.4 %collective-permute-start.27 = (bf16[2,128,128]{2,1,0:T(8,128)(2,1)}, bf16[2,128,128]{2,1,0:T(8,128)(2,1)S(1)}, u32[]{:S(2)}, u32[]{:S(2)}) collective-permute-start(bf16[2,128,128]{2,1,0:T(8,128)(2,1)} %collective-permute-done.24), channel_id=1, source_target_pairs={{0,504},{8,0},{16,8},{24,16},{32,24},{40,32},{48,40},{56,48},{64,5... | collective-permute-start | bytes 196616 | tf_op jit(solution)/shard_map/ppermute | solution.py:78
  128.9 35.1 %collective-permute-start.30 = (bf16[2,128,128]{2,1,0:T(8,128)(2,1)S(1)}, bf16[2,128,128]{2,1,0:T(8,128)(2,1)S(1)}, u32[]{:S(2)}, u32[]{:S(2)}) collective-permute-start(bf16[2,128,128]{2,1,0:T(8,128)(2,1)S(1)} %collective-permute-done.27), channel_id=1, source_target_pairs={{0,504},{8,0},{16,8},{24,16},{32,24},{40,32},{48,40},{56,48},{64,5... | collective-permute-start | bytes 196616 | tf_op jit(solution)/shard_map/ppermute | solution.py:78
  130.8 12.3 %collective-permute-start.3 = (bf16[128,1024]{1,0:T(8,128)(2,1)}, bf16[128,1024]{1,0:T(8,128)(2,1)}, u32[]{:S(2)}, u32[]{:S(2)}) collective-permute-start(bf16[128,1024]{1,0:T(8,128)(2,1)} %collective-permute-done.2), channel_id=1, source_target_pairs={{0,8},{8,16},{16,24},{24,32},{32,40},{40,48},{48,56},{56,64},{64,7... | collective-permute-start | bytes 786440 | tf_op jit(solution)/shard_map/ppermute | solution.py:76
  134.8 12.6 %collective-permute-start.25 = (bf16[128,1024]{1,0:T(8,128)(2,1)}, bf16[128,1024]{1,0:T(8,128)(2,1)S(1)}, u32[]{:S(2)}, u32[]{:S(2)}) collective-permute-start(bf16[128,1024]{1,0:T(8,128)(2,1)} %collective-permute-done.22), channel_id=1, source_target_pairs={{0,504},{8,0},{16,8},{24,16},{32,24},{40,32},{48,40},{56,48},{64,5... | collective-permute-start | bytes 786440 | tf_op jit(solution)/shard_map/ppermute | solution.py:77
  143.1 31.4 %collective-permute-start.4 = (bf16[128,1024]{1,0:T(8,128)(2,1)}, bf16[128,1024]{1,0:T(8,128)(2,1)}, u32[]{:S(2)}, u32[]{:S(2)}) collective-permute-start(bf16[128,1024]{1,0:T(8,128)(2,1)} %collective-permute-done.3), channel_id=1, source_target_pairs={{0,8},{8,16},{16,24},{24,32},{32,40},{40,48},{48,56},{56,64},{64,7... | collective-permute-start | bytes 786440 | tf_op jit(solution)/shard_map/ppermute | solution.py:76
  147.4 11.6 %collective-permute-start.28 = (bf16[128,1024]{1,0:T(8,128)(2,1)S(1)}, bf16[128,1024]{1,0:T(8,128)(2,1)S(1)}, u32[]{:S(2)}, u32[]{:S(2)}) collective-permute-start(bf16[128,1024]{1,0:T(8,128)(2,1)S(1)} %collective-permute-done.25), channel_id=1, source_target_pairs={{0,504},{8,0},{16,8},{24,16},{32,24},{40,32},{48,40},{56,48},{64,5... | collective-permute-start | bytes 786440 | tf_op jit(solution)/shard_map/ppermute | solution.py:77
  159.0 13.5 %collective-permute-start.31 = (bf16[128,1024]{1,0:T(8,128)(2,1)S(1)}, bf16[128,1024]{1,0:T(8,128)(2,1)S(1)}, u32[]{:S(2)}, u32[]{:S(2)}) collective-permute-start(bf16[128,1024]{1,0:T(8,128)(2,1)S(1)} %collective-permute-done.28), channel_id=1, source_target_pairs={{0,504},{8,0},{16,8},{24,16},{32,24},{40,32},{48,40},{56,48},{64,5... | collective-permute-start | bytes 786440 | tf_op jit(solution)/shard_map/ppermute | solution.py:77
  174.3 84.4 %reduce-scatter.14.cloned.1.call-start = ((), (), s32[]{:S(2)}) async-start(), calls=%async_computation.9 | async-start | bytes 327680 | tf_op jit(solution)/shard_map/reduce_scatter | solution.py:36
  195.3 22.6 %collective-permute-start.7 = (bf16[128,1024]{1,0:T(8,128)(2,1)S(1)}, bf16[128,1024]{1,0:T(8,128)(2,1)S(1)}, u32[]{:S(2)}, u32[]{:S(2)}) collective-permute-start(bf16[128,1024]{1,0:T(8,128)(2,1)S(1)} %collective-permute-done.6), channel_id=1, source_target_pairs={{0,8},{8,16},{16,24},{24,32},{32,40},{40,48},{48,56},{56,64},{64,7... | collective-permute-start | bytes 786440 | tf_op jit(solution)/shard_map/ppermute | solution.py:76
  217.3 58.1 %reduce-scatter.10.cloned.1.call-start = ((), (), s32[]{:S(2)}) async-start(), calls=%async_computation.7 | async-start | bytes 393216 | tf_op jit(solution)/shard_map/reduce_scatter | solution.py:36
  219.2 83.1 %reduce-scatter.16.cloned.1.call-start = ((), (), s32[]{:S(2)}) async-start(), calls=%async_computation.10 | async-start | bytes 786432 | tf_op jit(solution)/shard_map/reduce_scatter | solution.py:36
  260.7 73.3 %reduce-scatter.22.cloned.1.call-start = ((), (), s32[]{:S(2)}) async-start(), calls=%async_computation.13 | async-start | bytes 163840
  277.1 82.2 %reduce-scatter.18.cloned.1.call-start = ((), (), s32[]{:S(2)}) async-start(), calls=%async_computation.11 | async-start | bytes 327680 | tf_op jit(solution)/shard_map/reduce_scatter | solution.py:36
  302.3 100.0 %reduce-scatter.20.cloned.1.call-start = ((), (), s32[]{:S(2)}) async-start(), calls=%async_computation.12 | async-start | bytes 73728 | tf_op jit(solution)/shard_map/reduce_scatter | solution.py:36
  (13 other events, 174.6 us)
Sparse Core Ops, SparseCore 0:
  174.4 42.8 reduce-scatter.11
  220.3 38.2 reduce-scatter.13
  261.5 13.9 reduce-scatter.9
  278.3 23.9 reduce-scatter.15
  304.9 29.0 reduce-scatter.21
  336.9 22.4 reduce-scatter.17
  362.7 39.6 reduce-scatter.19

commit v2 on v1

--- a/solution.py
+++ b/solution.py
@@ -1,10 +1,15 @@
+import functools
 import math
 
 import jax
 import jax.numpy as jnp
 from jax import lax
+from jax.experimental import pallas as pl
+from jax.experimental.pallas import tpu as pltpu
 from jax.sharding import Mesh
 from jax.sharding import PartitionSpec as P
+
+MESH_IDS = pl.DeviceIdType.MESH
 
 BLK = ("by", "bx", "bz")
 REP = ("rz", "rc")
@@ -35,6 +40,87 @@
     for a in reversed(axes):
         moved = lax.psum_scatter(moved, a, scatter_dimension=dim, tiled=True)
     return moved
+
+
+def exchange_kernel(group, sizes, every, broadcast, src_ref, out_ref, landed, send_sem, recv_sem):
+    count = math.prod(sizes)
+    me = 0
+    for a, s in zip(group, sizes):
+        me = me * s + lax.axis_index(a)
+
+    def target(d):
+        coords = {}
+        rest = d
+        for a, s in reversed(list(zip(group, sizes))):
+            coords[a] = rest % s
+            rest = rest // s
+        return tuple(coords[a] if a in coords else lax.axis_index(a) for a in every)
+
+    def source(d):
+        return src_ref if broadcast else src_ref.at[d]
+
+    def copy_to(d, o):
+        return pltpu.make_async_remote_copy(
+            src_ref=source(d),
+            dst_ref=landed.at[me],
+            send_sem=send_sem.at[o],
+            recv_sem=recv_sem.at[me],
+            device_id=target(d),
+            device_id_type=MESH_IDS,
+        )
+
+    barrier = pltpu.get_barrier_semaphore()
+
+    def greet(o, carry):
+        pl.semaphore_signal(barrier, inc=1, device_id=target((me + o) % count), device_id_type=MESH_IDS)
+        return carry
+
+    lax.fori_loop(1, count, greet, 0)
+    pl.semaphore_wait(barrier, count - 1)
+
+    def send(o, carry):
+        copy_to((me + o) % count, o).start()
+        return carry
+
+    lax.fori_loop(1, count, send, 0)
+    out_ref[me] = src_ref[...] if broadcast else src_ref[me]
+
+    def finish(o, carry):
+        copy_to((me + o) % count, o).wait_send()
+        sender = (me + count - o) % count
+        incoming = pltpu.make_async_remote_copy(
+            src_ref=source(sender),
+            dst_ref=landed.at[sender],
+            send_sem=send_sem.at[o],
+            recv_sem=recv_sem.at[sender],
+            device_id=target(sender),
+            device_id_type=MESH_IDS,
+        )
+        incoming.wait_recv()
+        out_ref[sender] = landed[sender]
+        return carry
+
+    lax.fori_loop(1, count, finish, 0)
+
+
+def exchange(blocks, group, every, collective, broadcast=False):
+    sizes = tuple(lax.axis_size(a) for a in group)
+    count = math.prod(sizes)
+    shape = (count,) + (blocks.shape if broadcast else blocks.shape[1:])
+    size = math.prod(shape) * blocks.dtype.itemsize
+    return pl.pallas_call(
+        functools.partial(exchange_kernel, group, sizes, every, broadcast),
+        out_shape=jax.ShapeDtypeStruct(shape, blocks.dtype),
+        in_specs=[pl.BlockSpec(memory_space=pltpu.VMEM)],
+        out_specs=pl.BlockSpec(memory_space=pltpu.VMEM),
+        scratch_shapes=[
+            pltpu.VMEM(shape, blocks.dtype),
+            pltpu.SemaphoreType.DMA((count,)),
+            pltpu.SemaphoreType.DMA((count,)),
+        ],
+        compiler_params=pltpu.CompilerParams(collective_id=collective, has_side_effects=True),
+        cost_estimate=pl.CostEstimate(flops=0, transcendentals=0, bytes_accessed=3 * size),
+    )(blocks)
 
 
 def shards(hidden_pre, adj_vals, adj_cols, w_out, cotangent):
@@ -78,14 +164,17 @@
             vals_cur = lax.ppermute(vals_cur, BLK, ring_pairs(blk_count, -1))
             cols_cur = lax.ppermute(cols_cur, BLK, ring_pairs(blk_count, -1))
 
-    out_part = staged_scatter(out_sum.astype(jnp.bfloat16), REP, 1)
-    back_part = staged_scatter(back_sum, REP, 1)
-    back_grad = back_part.astype(jnp.bfloat16)
+    rows = out_sum.shape[0]
+    both = jnp.stack([out_sum, back_sum]).reshape(2, rows, rep_count, cols_here)
+    summed = exchange(jnp.transpose(both, (2, 0, 1, 3)), REP, EVERY, 0).sum(0)
+    out_part = summed[0].astype(jnp.bfloat16)
+    back_grad = summed[1].astype(jnp.bfloat16)
     term = lax.dot_general(
         hidden_act, back_grad, (((0,), (0,)), ((), ())), preferred_element_type=jnp.float32
     )
-    grad_weight = staged_scatter(term, BLK, 0)
-    back_full = lax.all_gather(back_grad, REP, axis=1, tiled=True)
+    grad_weight = exchange(term.reshape(blk_count, -1, cols_here), BLK, EVERY, 1).sum(0)
+    gathered = exchange(back_grad, REP, EVERY, 2, broadcast=True)
+    back_full = jnp.transpose(gathered, (1, 0, 2)).reshape(rows, feature_width)
     w_rows = lax.dynamic_slice_in_dim(w_out, rep_pos * cols_here, cols_here, 0)
     grad_in = lax.dot_general(
         back_full, w_rows, (((1,), (1,)), ((), ())), preferred_element_type=jnp.float32

time: 411 us -> 321 us (0.78)
  waiting for transfers between devices: 223 us -> 61 us
  Pallas kernels: 0 us -> 103 us
  blocking collectives: 14.6 us -> 0 us
  between operations: 35.6 us -> 22 us
  starting transfers between devices: 110 us -> 105 us
  other arithmetic: 0.86 us -> 5.13 us
    reduce_scatter x6 -> x0, waiting for transfers between devices: 151 us -> none  [staged_scatter(): moved = lax.psum_scatter(moved, a, scatter_dimension=dim, tiled=True)]
    pallas_call x0 -> x3, Pallas kernels: none -> 103 us  [exchange(): pl.pallas_call(functools.partial(exchange_kernel, group, sizes, every, br...]
    unnamed x8 -> x0, waiting for transfers between devices: 31.7 us -> none
    ppermute x7, waiting for transfers between devices: 3.5 us -> 19.4 us  [shards(): cols_cur = lax.ppermute(cols_cur, BLK, ring_pairs(blk_count, -1))]
    all_gather x1 -> x0, blocking collectives: 14.6 us -> none  [shards(): back_full = lax.all_gather(back_grad, REP, axis=1, tiled=True)]
    ppermute x7, waiting for transfers between devices: 13.6 us -> 26.4 us  [shards(): cot_cur = lax.ppermute(cot_cur, BLK, ring_pairs(blk_count, -1))]
    ppermute x7, starting transfers between devices: 28.9 us -> 22 us  [shards(): cot_cur = lax.ppermute(cot_cur, BLK, ring_pairs(blk_count, -1))]
    ppermute x7, starting transfers between devices: 20.2 us -> 26.5 us  [shards(): visiting = lax.ppermute(visiting, BLK, ring_pairs(blk_count, 1))]
  transfers between devices with their start and end apart: 39 -> 32, of which waited for: 16 -> 17; matrix products, arithmetic and copies ran while one was open for 6% -> 4% of each run, Pallas kernels for 0% -> 0%
where the time goes in v2:
time: 321 us; the launch traced here: 318 us
  starting transfers between devices  105 us (33%)
  Pallas kernels  103 us (32%)
  waiting for transfers between devices  61 us (19%)
  between operations  22 us (7%)
  local copies, waits for them, and re-layouts  12.1 us (4%)
  matrix products  8.83 us (3%)
  other arithmetic  5.13 us (2%)
    pallas_call x3, Pallas kernels, exchange(): pl.pallas_call(functools.partial(exchange_kernel, group, sizes, every, br...  103 us
    ppermute x7, starting transfers between devices, shards(): vals_cur = lax.ppermute(vals_cur, BLK, ring_pairs(blk_count, -1))  26.6 us
    ppermute x7, starting transfers between devices, shards(): cols_cur = lax.ppermute(cols_cur, BLK, ring_pairs(blk_count, -1))  26.5 us
    ppermute x7, starting transfers between devices, shards(): visiting = lax.ppermute(visiting, BLK, ring_pairs(blk_count, 1))  26.5 us
    ppermute x7, waiting for transfers between devices, shards(): cot_cur = lax.ppermute(cot_cur, BLK, ring_pairs(blk_count, -1))  26.4 us
    ppermute x7, starting transfers between devices, shards(): cot_cur = lax.ppermute(cot_cur, BLK, ring_pairs(blk_count, -1))  22 us
    ppermute x7, waiting for transfers between devices, shards(): cols_cur = lax.ppermute(cols_cur, BLK, ring_pairs(blk_count, -1))  19.4 us
    ppermute x7, waiting for transfers between devices, shards(): visiting = lax.ppermute(visiting, BLK, ring_pairs(blk_count, 1))  8.99 us
  transfers between devices with their start and end apart: 32, of which 17 were waited for; matrix products, arithmetic and copies ran while one was open for 4% of the time, Pallas kernels for 0%

profile of v2, /device:TPU:6, one launch (start us, length us, event | category | flops | bytes accessed | tf_op | source)
XLA Modules:
  0.0 317.6 jit_solution(53146988029241980)
XLA Ops:
  19.3 4.5 %collective-permute-start.11 = (s32[2]{0:T(128)S(1)}, s32[2]{0:T(128)S(1)}, u32[]{:S(2)}, u32[]{:S(2)}) collective-permute-start(s32[2]{0:T(128)S(1)} %collective-permute-done.8), channel_id=1, source_target_pairs={{0,504},{8,0},{16,8},{24,16},{32,24},{40,32},{48,40},{56,48},{64,5... | collective-permute-start | bytes 32 | tf_op jit(solution)/shard_map/ppermute | solution.py:165
  27.0 5.1 %collective-permute-start.14 = (s32[2]{0:T(128)S(1)}, s32[2]{0:T(128)S(1)}, u32[]{:S(2)}, u32[]{:S(2)}) collective-permute-start(s32[2]{0:T(128)S(1)} %collective-permute-done.11), channel_id=1, source_target_pairs={{0,504},{8,0},{16,8},{24,16},{32,24},{40,32},{48,40},{56,48},{64,5... | collective-permute-start | bytes 32 | tf_op jit(solution)/shard_map/ppermute | solution.py:165
  32.1 3.4 %collective-permute-done.14 = s32[2]{0:T(128)S(1)} collective-permute-done((s32[2]{0:T(128)S(1)}, s32[2]{0:T(128)S(1)}, u32[]{:S(2)}, u32[]{:S(2)}) %collective-permute-start.14) | collective-permute-done | bytes 40 | tf_op jit(solution)/shard_map/ppermute | solution.py:165
  37.3 3.0 collective-permute-start.17
  40.3 5.5 %collective-permute-done.17 = s32[2]{0:T(128)S(1)} collective-permute-done((s32[2]{0:T(128)S(1)}, s32[2]{0:T(128)S(1)}, u32[]{:S(2)}, u32[]{:S(2)}) %collective-permute-start.17) | collective-permute-done | bytes 40 | tf_op jit(solution)/shard_map/ppermute | solution.py:165
  51.5 4.6 %collective-permute-done.20 = s32[2]{0:T(128)S(1)} collective-permute-done((s32[2]{0:T(128)S(1)}, s32[2]{0:T(128)S(1)}, u32[]{:S(2)}, u32[]{:S(2)}) %collective-permute-start.20) | collective-permute-done | bytes 40 | tf_op jit(solution)/shard_map/ppermute | solution.py:165
  61.9 4.6 %collective-permute-done.23 = s32[2]{0:T(128)S(1)} collective-permute-done((s32[2]{0:T(128)S(1)}, s32[2]{0:T(128)S(1)}, u32[]{:S(2)}, u32[]{:S(2)}) %collective-permute-start.23) | collective-permute-done | bytes 40 | tf_op jit(solution)/shard_map/ppermute | solution.py:165
  70.3 6.3 %collective-permute-start.18 = (bf16[2,128,128]{2,1,0:T(8,128)(2,1)S(1)}, bf16[2,128,128]{2,1,0:T(8,128)(2,1)S(1)}, u32[]{:S(2)}, u32[]{:S(2)}) collective-permute-start(bf16[2,128,128]{2,1,0:T(8,128)(2,1)S(1)} %collective-permute-done.15), channel_id=1, source_target_pairs={{0,504},{8,0},{16,8},{24,16},{32,24},{40,32},{48,40},{56,48},{64,5... | collective-permute-start | bytes 196616 | tf_op jit(solution)/shard_map/ppermute | solution.py:164
  78.7 8.2 %collective-permute-start.29 = (s32[2]{0:T(128)S(1)}, s32[2]{0:T(128)S(1)}, u32[]{:S(2)}, u32[]{:S(2)}) collective-permute-start(s32[2]{0:T(128)S(1)} %collective-permute-done.26), channel_id=1, source_target_pairs={{0,504},{8,0},{16,8},{24,16},{32,24},{40,32},{48,40},{56,48},{64,5... | collective-permute-start | bytes 32 | tf_op jit(solution)/shard_map/ppermute | solution.py:165
  90.7 5.2 %collective-permute-start.1 = (bf16[128,1024]{1,0:T(8,128)(2,1)S(1)}, bf16[128,1024]{1,0:T(8,128)(2,1)S(1)}, u32[]{:S(2)}, u32[]{:S(2)}) collective-permute-start(bf16[128,1024]{1,0:T(8,128)(2,1)S(1)} %collective-permute-done), channel_id=1, source_target_pairs={{0,8},{8,16},{16,24},{24,32},{32,40},{40,48},{48,56},{56,64},{64,7... | collective-permute-start | bytes 786440 | tf_op jit(solution)/shard_map/ppermute | solution.py:162
  95.9 4.4 %collective-permute-start.13 = (bf16[128,1024]{1,0:T(8,128)(2,1)S(1)}, bf16[128,1024]{1,0:T(8,128)(2,1)S(1)}, u32[]{:S(2)}, u32[]{:S(2)}) collective-permute-start(bf16[128,1024]{1,0:T(8,128)(2,1)S(1)} %collective-permute-done.10), channel_id=1, source_target_pairs={{0,504},{8,0},{16,8},{24,16},{32,24},{40,32},{48,40},{56,48},{64,5... | collective-permute-start | bytes 786440 | tf_op jit(solution)/shard_map/ppermute | solution.py:163
  100.3 3.9 %collective-permute-start.24 = (bf16[2,128,128]{2,1,0:T(8,128)(2,1)S(1)}, bf16[2,128,128]{2,1,0:T(8,128)(2,1)S(1)}, u32[]{:S(2)}, u32[]{:S(2)}) collective-permute-start(bf16[2,128,128]{2,1,0:T(8,128)(2,1)S(1)} %collective-permute-done.21), channel_id=1, source_target_pairs={{0,504},{8,0},{16,8},{24,16},{32,24},{40,32},{48,40},{56,48},{64,5... | collective-permute-start | bytes 196616 | tf_op jit(solution)/shard_map/ppermute | solution.py:164
  104.5 4.5 %collective-permute-done.24 = bf16[2,128,128]{2,1,0:T(8,128)(2,1)S(1)} collective-permute-done((bf16[2,128,128]{2,1,0:T(8,128)(2,1)S(1)}, bf16[2,128,128]{2,1,0:T(8,128)(2,1)S(1)}, u32[]{:S(2)}, u32[]{:S(2)}) %collective-permute-start.24) | collective-permute-done | bytes 65568 | tf_op jit(solution)/shard_map/ppermute | solution.py:164
  109.0 5.3 %collective-permute-start.27 = (bf16[2,128,128]{2,1,0:T(8,128)(2,1)S(1)}, bf16[2,128,128]{2,1,0:T(8,128)(2,1)}, u32[]{:S(2)}, u32[]{:S(2)}) collective-permute-start(bf16[2,128,128]{2,1,0:T(8,128)(2,1)S(1)} %collective-permute-done.24), channel_id=1, source_target_pairs={{0,504},{8,0},{16,8},{24,16},{32,24},{40,32},{48,40},{56,48},{64,5... | collective-permute-start | bytes 196616 | tf_op jit(solution)/shard_map/ppermute | solution.py:164
  116.2 5.4 %collective-permute-start.30 = (bf16[2,128,128]{2,1,0:T(8,128)(2,1)}, bf16[2,128,128]{2,1,0:T(8,128)(2,1)S(1)}, u32[]{:S(2)}, u32[]{:S(2)}) collective-permute-start(bf16[2,128,128]{2,1,0:T(8,128)(2,1)} %collective-permute-done.27), channel_id=1, source_target_pairs={{0,504},{8,0},{16,8},{24,16},{32,24},{40,32},{48,40},{56,48},{64,5... | collective-permute-start | bytes 196616 | tf_op jit(solution)/shard_map/ppermute | solution.py:164
  124.4 4.0 %collective-permute-start.16 = (bf16[128,1024]{1,0:T(8,128)(2,1)S(1)}, bf16[128,1024]{1,0:T(8,128)(2,1)S(1)}, u32[]{:S(2)}, u32[]{:S(2)}) collective-permute-start(bf16[128,1024]{1,0:T(8,128)(2,1)S(1)} %collective-permute-done.13), channel_id=1, source_target_pairs={{0,504},{8,0},{16,8},{24,16},{32,24},{40,32},{48,40},{56,48},{64,5... | collective-permute-start | bytes 786440 | tf_op jit(solution)/shard_map/ppermute | solution.py:163
  128.9 4.8 %collective-permute-done.2 = bf16[128,1024]{1,0:T(8,128)(2,1)S(1)} collective-permute-done((bf16[128,1024]{1,0:T(8,128)(2,1)S(1)}, bf16[128,1024]{1,0:T(8,128)(2,1)S(1)}, u32[]{:S(2)}, u32[]{:S(2)}) %collective-permute-start.2) | collective-permute-done | bytes 262176 | tf_op jit(solution)/shard_map/ppermute | solution.py:162
  133.7 3.2 %collective-permute-start.3 = (bf16[128,1024]{1,0:T(8,128)(2,1)S(1)}, bf16[128,1024]{1,0:T(8,128)(2,1)S(1)}, u32[]{:S(2)}, u32[]{:S(2)}) collective-permute-start(bf16[128,1024]{1,0:T(8,128)(2,1)S(1)} %collective-permute-done.2), channel_id=1, source_target_pairs={{0,8},{8,16},{16,24},{24,32},{32,40},{40,48},{48,56},{56,64},{64,7... | collective-permute-start | bytes 786440 | tf_op jit(solution)/shard_map/ppermute | solution.py:162
  137.3 3.8 %collective-permute-start.19 = (bf16[128,1024]{1,0:T(8,128)(2,1)S(1)}, bf16[128,1024]{1,0:T(8,128)(2,1)S(1)}, u32[]{:S(2)}, u32[]{:S(2)}) collective-permute-start(bf16[128,1024]{1,0:T(8,128)(2,1)S(1)} %collective-permute-done.16), channel_id=1, source_target_pairs={{0,504},{8,0},{16,8},{24,16},{32,24},{40,32},{48,40},{56,48},{64,5... | collective-permute-start | bytes 786440 | tf_op jit(solution)/shard_map/ppermute | solution.py:163
  141.6 3.6 %collective-permute-done.3 = bf16[128,1024]{1,0:T(8,128)(2,1)S(1)} collective-permute-done((bf16[128,1024]{1,0:T(8,128)(2,1)S(1)}, bf16[128,1024]{1,0:T(8,128)(2,1)S(1)}, u32[]{:S(2)}, u32[]{:S(2)}) %collective-permute-start.3) | collective-permute-done | bytes 262176 | tf_op jit(solution)/shard_map/ppermute | solution.py:162
  145.2 3.8 %collective-permute-start.4 = (bf16[128,1024]{1,0:T(8,128)(2,1)S(1)}, bf16[128,1024]{1,0:T(8,128)(2,1)S(1)}, u32[]{:S(2)}, u32[]{:S(2)}) collective-permute-start(bf16[128,1024]{1,0:T(8,128)(2,1)S(1)} %collective-permute-done.3), channel_id=1, source_target_pairs={{0,8},{8,16},{16,24},{24,32},{32,40},{40,48},{48,56},{56,64},{64,7... | collective-permute-start | bytes 786440 | tf_op jit(solution)/shard_map/ppermute | solution.py:162
  149.0 4.6 %collective-permute-done.19 = bf16[128,1024]{1,0:T(8,128)(2,1)S(1)} collective-permute-done((bf16[128,1024]{1,0:T(8,128)(2,1)S(1)}, bf16[128,1024]{1,0:T(8,128)(2,1)S(1)}, u32[]{:S(2)}, u32[]{:S(2)}) %collective-permute-start.19) | collective-permute-done | bytes 262176 | tf_op jit(solution)/shard_map/ppermute | solution.py:163
  156.6 3.7 %collective-permute-start.5 = (bf16[128,1024]{1,0:T(8,128)(2,1)S(1)}, bf16[128,1024]{1,0:T(8,128)(2,1)S(1)}, u32[]{:S(2)}, u32[]{:S(2)}) collective-permute-start(bf16[128,1024]{1,0:T(8,128)(2,1)S(1)} %collective-permute-done.4), channel_id=1, source_target_pairs={{0,8},{8,16},{16,24},{24,32},{32,40},{40,48},{48,56},{56,64},{64,7... | collective-permute-start | bytes 786440 | tf_op jit(solution)/shard_map/ppermute | solution.py:162
  160.3 8.5 %collective-permute-done.22 = bf16[128,1024]{1,0:T(8,128)(2,1)S(1)} collective-permute-done((bf16[128,1024]{1,0:T(8,128)(2,1)S(1)}, bf16[128,1024]{1,0:T(8,128)(2,1)S(1)}, u32[]{:S(2)}, u32[]{:S(2)}) %collective-permute-start.22) | collective-permute-done | bytes 262176 | tf_op jit(solution)/shard_map/ppermute | solution.py:163
  171.3 3.9 %collective-permute-start.6 = (bf16[128,1024]{1,0:T(8,128)(2,1)S(1)}, bf16[128,1024]{1,0:T(8,128)(2,1)S(1)}, u32[]{:S(2)}, u32[]{:S(2)}) collective-permute-start(bf16[128,1024]{1,0:T(8,128)(2,1)S(1)} %collective-permute-done.5), channel_id=1, source_target_pairs={{0,8},{8,16},{16,24},{24,32},{32,40},{40,48},{48,56},{56,64},{64,7... | collective-permute-start | bytes 786440 | tf_op jit(solution)/shard_map/ppermute | solution.py:162
  175.2 5.9 %collective-permute-done.25 = bf16[128,1024]{1,0:T(8,128)(2,1)S(1)} collective-permute-done((bf16[128,1024]{1,0:T(8,128)(2,1)S(1)}, bf16[128,1024]{1,0:T(8,128)(2,1)S(1)}, u32[]{:S(2)}, u32[]{:S(2)}) %collective-permute-start.25) | collective-permute-done | bytes 262176 | tf_op jit(solution)/shard_map/ppermute | solution.py:163
  183.5 3.9 %collective-permute-start.7 = (bf16[128,1024]{1,0:T(8,128)(2,1)S(1)}, bf16[128,1024]{1,0:T(8,128)(2,1)S(1)}, u32[]{:S(2)}, u32[]{:S(2)}) collective-permute-start(bf16[128,1024]{1,0:T(8,128)(2,1)S(1)} %collective-permute-done.6), channel_id=1, source_target_pairs={{0,8},{8,16},{16,24},{24,32},{32,40},{40,48},{48,56},{56,64},{64,7... | collective-permute-start | bytes 786440 | tf_op jit(solution)/shard_map/ppermute | solution.py:162
  189.7 4.2 %collective-permute-start.31 = (bf16[128,1024]{1,0:T(8,128)(2,1)}, bf16[128,1024]{1,0:T(8,128)(2,1)}, u32[]{:S(2)}, u32[]{:S(2)}) collective-permute-start(bf16[128,1024]{1,0:T(8,128)(2,1)} %collective-permute-done.28), channel_id=1, source_target_pairs={{0,504},{8,0},{16,8},{24,16},{32,24},{40,32},{48,40},{56,48},{64,5... | collective-permute-start | bytes 786440 | tf_op jit(solution)/shard_map/ppermute | solution.py:163
  198.6 4.6 %collective-permute-done.31 = bf16[128,1024]{1,0:T(8,128)(2,1)} collective-permute-done((bf16[128,1024]{1,0:T(8,128)(2,1)}, bf16[128,1024]{1,0:T(8,128)(2,1)}, u32[]{:S(2)}, u32[]{:S(2)}) %collective-permute-start.31) | collective-permute-done | bytes 262176 | tf_op jit(solution)/shard_map/ppermute | solution.py:163
  206.9 51.2 %shard_map.76 = f32[8,2,128,128]{3,2,1,0:T(8,128)} custom-call(f32[8,2,128,128]{3,2,1,0:T(8,128)} %maximum_bitcast_fusion.src_ref), custom_call_target="tpu_custom_call" | custom-call | bytes 3145728 | tf_op jit(solution)/shard_map/pallas_call | solution.py:111
  261.1 40.1 %shard_map.77 = f32[64,16,128]{2,1,0:T(8,128)} custom-call(f32[64,16,128]{2,1,0:T(8,128)} %fusion.28.src_ref), custom_call_target="tpu_custom_call" | custom-call | bytes 1572864 | tf_op jit(solution)/shard_map/pallas_call | solution.py:111
  302.8 12.0 %shard_map.78 = bf16[8,128,128]{2,1,0:T(8,128)(2,1)} custom-call(bf16[128,128]{1,0:T(8,128)(2,1)} %get-tuple-element.3.src_ref), custom_call_target="tpu_custom_call" | custom-call | bytes 786432 | tf_op jit(solution)/shard_map/pallas_call | solution.py:111
  (81 shorter events, 56.1 us)
Async XLA Ops:
  2.8 87.9 %collective-permute-start = (bf16[128,1024]{1,0:T(8,128)(2,1)S(1)}, bf16[128,1024]{1,0:T(8,128)(2,1)S(1)}, u32[]{:S(2)}, u32[]{:S(2)}) collective-permute-start(bf16[128,1024]{1,0:T(8,128)(2,1)S(1)} %convolution_convert_fusion), channel_id=1, source_target_pairs={{0,0},{1,65},{2,130},{3,195},{4,260},{5,325},{6,390},{7,455},{8,8}... | collective-permute-start | bytes 786440 | tf_op jit(solution)/shard_map/ppermute | solution.py:142
  3.5 14.0 %collective-permute-start.8 = (s32[2]{0:T(128)S(1)}, s32[2]{0:T(128)S(1)}, u32[]{:S(2)}, u32[]{:S(2)}) collective-permute-start(s32[2]{0:T(128)S(1)} %bitcast.124), channel_id=1, source_target_pairs={{0,0},{1,449},{2,386},{3,323},{4,260},{5,197},{6,134},{7,71},{8,8}... | collective-permute-start | bytes 32 | tf_op jit(solution)/shard_map/ppermute | solution.py:146
  4.1 91.8 %collective-permute-start.10 = (bf16[128,1024]{1,0:T(8,128)(2,1)}, bf16[128,1024]{1,0:T(8,128)(2,1)S(1)}, u32[]{:S(2)}, u32[]{:S(2)}) collective-permute-start(bf16[128,1024]{1,0:T(8,128)(2,1)} %param.9), channel_id=1, source_target_pairs={{0,0},{1,449},{2,386},{3,323},{4,260},{5,197},{6,134},{7,71},{8,8}... | collective-permute-start | bytes 786440 | tf_op jit(solution)/shard_map/ppermute | solution.py:144
  5.8 43.8 %collective-permute-start.9 = (bf16[2,128,128]{2,1,0:T(8,128)(2,1)S(1)}, bf16[2,128,128]{2,1,0:T(8,128)(2,1)S(1)}, u32[]{:S(2)}, u32[]{:S(2)}) collective-permute-start(bf16[2,128,128]{2,1,0:T(8,128)(2,1)S(1)} %bitcast.120), channel_id=1, source_target_pairs={{0,0},{1,449},{2,386},{3,323},{4,260},{5,197},{6,134},{7,71},{8,8}... | collective-permute-start | bytes 196616 | tf_op jit(solution)/shard_map/ppermute | solution.py:145
  19.3 5.8 %collective-permute-start.11 = (s32[2]{0:T(128)S(1)}, s32[2]{0:T(128)S(1)}, u32[]{:S(2)}, u32[]{:S(2)}) collective-permute-start(s32[2]{0:T(128)S(1)} %collective-permute-done.8), channel_id=1, source_target_pairs={{0,504},{8,0},{16,8},{24,16},{32,24},{40,32},{48,40},{56,48},{64,5... | collective-permute-start | bytes 32 | tf_op jit(solution)/shard_map/ppermute | solution.py:165
  27.0 8.4 %collective-permute-start.14 = (s32[2]{0:T(128)S(1)}, s32[2]{0:T(128)S(1)}, u32[]{:S(2)}, u32[]{:S(2)}) collective-permute-start(s32[2]{0:T(128)S(1)} %collective-permute-done.11), channel_id=1, source_target_pairs={{0,504},{8,0},{16,8},{24,16},{32,24},{40,32},{48,40},{56,48},{64,5... | collective-permute-start | bytes 32 | tf_op jit(solution)/shard_map/ppermute | solution.py:165
  37.3 8.4 %collective-permute-start.17 = (s32[2]{0:T(128)S(1)}, s32[2]{0:T(128)S(1)}, u32[]{:S(2)}, u32[]{:S(2)}) collective-permute-start(s32[2]{0:T(128)S(1)} %collective-permute-done.14), channel_id=1, source_target_pairs={{0,504},{8,0},{16,8},{24,16},{32,24},{40,32},{48,40},{56,48},{64,5... | collective-permute-start | bytes 32 | tf_op jit(solution)/shard_map/ppermute | solution.py:165
  47.7 8.4 %collective-permute-start.20 = (s32[2]{0:T(128)S(1)}, s32[2]{0:T(128)S(1)}, u32[]{:S(2)}, u32[]{:S(2)}) collective-permute-start(s32[2]{0:T(128)S(1)} %collective-permute-done.17), channel_id=1, source_target_pairs={{0,504},{8,0},{16,8},{24,16},{32,24},{40,32},{48,40},{56,48},{64,5... | collective-permute-start | bytes 32 | tf_op jit(solution)/shard_map/ppermute | solution.py:165
  49.6 10.3 %collective-permute-start.12 = (bf16[2,128,128]{2,1,0:T(8,128)(2,1)S(1)}, bf16[2,128,128]{2,1,0:T(8,128)(2,1)S(1)}, u32[]{:S(2)}, u32[]{:S(2)}) collective-permute-start(bf16[2,128,128]{2,1,0:T(8,128)(2,1)S(1)} %collective-permute-done.9), channel_id=1, source_target_pairs={{0,504},{8,0},{16,8},{24,16},{32,24},{40,32},{48,40},{56,48},{64,5... | collective-permute-start | bytes 196616 | tf_op jit(solution)/shard_map/ppermute | solution.py:164
  58.0 8.4 %collective-permute-start.23 = (s32[2]{0:T(128)S(1)}, s32[2]{0:T(128)S(1)}, u32[]{:S(2)}, u32[]{:S(2)}) collective-permute-start(s32[2]{0:T(128)S(1)} %collective-permute-done.20), channel_id=1, source_target_pairs={{0,504},{8,0},{16,8},{24,16},{32,24},{40,32},{48,40},{56,48},{64,5... | collective-permute-start | bytes 32 | tf_op jit(solution)/shard_map/ppermute | solution.py:165
  59.9 10.3 %collective-permute-start.15 = (bf16[2,128,128]{2,1,0:T(8,128)(2,1)S(1)}, bf16[2,128,128]{2,1,0:T(8,128)(2,1)S(1)}, u32[]{:S(2)}, u32[]{:S(2)}) collective-permute-start(bf16[2,128,128]{2,1,0:T(8,128)(2,1)S(1)} %collective-permute-done.12), channel_id=1, source_target_pairs={{0,504},{8,0},{16,8},{24,16},{32,24},{40,32},{48,40},{56,48},{64,5... | collective-permute-start | bytes 196616 | tf_op jit(solution)/shard_map/ppermute | solution.py:164
  68.3 8.4 %collective-permute-start.26 = (s32[2]{0:T(128)S(1)}, s32[2]{0:T(128)S(1)}, u32[]{:S(2)}, u32[]{:S(2)}) collective-permute-start(s32[2]{0:T(128)S(1)} %collective-permute-done.23), channel_id=1, source_target_pairs={{0,504},{8,0},{16,8},{24,16},{32,24},{40,32},{48,40},{56,48},{64,5... | collective-permute-start | bytes 32 | tf_op jit(solution)/shard_map/ppermute | solution.py:165
  70.3 16.6 %collective-permute-start.18 = (bf16[2,128,128]{2,1,0:T(8,128)(2,1)S(1)}, bf16[2,128,128]{2,1,0:T(8,128)(2,1)S(1)}, u32[]{:S(2)}, u32[]{:S(2)}) collective-permute-start(bf16[2,128,128]{2,1,0:T(8,128)(2,1)S(1)} %collective-permute-done.15), channel_id=1, source_target_pairs={{0,504},{8,0},{16,8},{24,16},{32,24},{40,32},{48,40},{56,48},{64,5... | collective-permute-start | bytes 196616 | tf_op jit(solution)/shard_map/ppermute | solution.py:164
  78.7 10.1 %collective-permute-start.29 = (s32[2]{0:T(128)S(1)}, s32[2]{0:T(128)S(1)}, u32[]{:S(2)}, u32[]{:S(2)}) collective-permute-start(s32[2]{0:T(128)S(1)} %collective-permute-done.26), channel_id=1, source_target_pairs={{0,504},{8,0},{16,8},{24,16},{32,24},{40,32},{48,40},{56,48},{64,5... | collective-permute-start | bytes 32 | tf_op jit(solution)/shard_map/ppermute | solution.py:165
  86.8 13.5 %collective-permute-start.21 = (bf16[2,128,128]{2,1,0:T(8,128)(2,1)S(1)}, bf16[2,128,128]{2,1,0:T(8,128)(2,1)S(1)}, u32[]{:S(2)}, u32[]{:S(2)}) collective-permute-start(bf16[2,128,128]{2,1,0:T(8,128)(2,1)S(1)} %collective-permute-done.18), channel_id=1, source_target_pairs={{0,504},{8,0},{16,8},{24,16},{32,24},{40,32},{48,40},{56,48},{64,5... | collective-permute-start | bytes 196616 | tf_op jit(solution)/shard_map/ppermute | solution.py:164
  90.7 30.9 %collective-permute-start.1 = (bf16[128,1024]{1,0:T(8,128)(2,1)S(1)}, bf16[128,1024]{1,0:T(8,128)(2,1)S(1)}, u32[]{:S(2)}, u32[]{:S(2)}) collective-permute-start(bf16[128,1024]{1,0:T(8,128)(2,1)S(1)} %collective-permute-done), channel_id=1, source_target_pairs={{0,8},{8,16},{16,24},{24,32},{32,40},{40,48},{48,56},{56,64},{64,7... | collective-permute-start | bytes 786440 | tf_op jit(solution)/shard_map/ppermute | solution.py:162
  95.9 28.4 %collective-permute-start.13 = (bf16[128,1024]{1,0:T(8,128)(2,1)S(1)}, bf16[128,1024]{1,0:T(8,128)(2,1)S(1)}, u32[]{:S(2)}, u32[]{:S(2)}) collective-permute-start(bf16[128,1024]{1,0:T(8,128)(2,1)S(1)} %collective-permute-done.10), channel_id=1, source_target_pairs={{0,504},{8,0},{16,8},{24,16},{32,24},{40,32},{48,40},{56,48},{64,5... | collective-permute-start | bytes 786440 | tf_op jit(solution)/shard_map/ppermute | solution.py:163
  100.3 8.7 %collective-permute-start.24 = (bf16[2,128,128]{2,1,0:T(8,128)(2,1)S(1)}, bf16[2,128,128]{2,1,0:T(8,128)(2,1)S(1)}, u32[]{:S(2)}, u32[]{:S(2)}) collective-permute-start(bf16[2,128,128]{2,1,0:T(8,128)(2,1)S(1)} %collective-permute-done.21), channel_id=1, source_target_pairs={{0,504},{8,0},{16,8},{24,16},{32,24},{40,32},{48,40},{56,48},{64,5... | collective-permute-start | bytes 196616 | tf_op jit(solution)/shard_map/ppermute | solution.py:164
  109.0 7.2 %collective-permute-start.27 = (bf16[2,128,128]{2,1,0:T(8,128)(2,1)S(1)}, bf16[2,128,128]{2,1,0:T(8,128)(2,1)}, u32[]{:S(2)}, u32[]{:S(2)}) collective-permute-start(bf16[2,128,128]{2,1,0:T(8,128)(2,1)S(1)} %collective-permute-done.24), channel_id=1, source_target_pairs={{0,504},{8,0},{16,8},{24,16},{32,24},{40,32},{48,40},{56,48},{64,5... | collective-permute-start | bytes 196616 | tf_op jit(solution)/shard_map/ppermute | solution.py:164
  116.2 82.4 %collective-permute-start.30 = (bf16[2,128,128]{2,1,0:T(8,128)(2,1)}, bf16[2,128,128]{2,1,0:T(8,128)(2,1)S(1)}, u32[]{:S(2)}, u32[]{:S(2)}) collective-permute-start(bf16[2,128,128]{2,1,0:T(8,128)(2,1)} %collective-permute-done.27), channel_id=1, source_target_pairs={{0,504},{8,0},{16,8},{24,16},{32,24},{40,32},{48,40},{56,48},{64,5... | collective-permute-start | bytes 196616 | tf_op jit(solution)/shard_map/ppermute | solution.py:164
  121.6 12.0 %collective-permute-start.2 = (bf16[128,1024]{1,0:T(8,128)(2,1)S(1)}, bf16[128,1024]{1,0:T(8,128)(2,1)S(1)}, u32[]{:S(2)}, u32[]{:S(2)}) collective-permute-start(bf16[128,1024]{1,0:T(8,128)(2,1)S(1)} %collective-permute-done.1), channel_id=1, source_target_pairs={{0,8},{8,16},{16,24},{24,32},{32,40},{40,48},{48,56},{56,64},{64,7... | collective-permute-start | bytes 786440 | tf_op jit(solution)/shard_map/ppermute | solution.py:162
  124.4 12.9 %collective-permute-start.16 = (bf16[128,1024]{1,0:T(8,128)(2,1)S(1)}, bf16[128,1024]{1,0:T(8,128)(2,1)S(1)}, u32[]{:S(2)}, u32[]{:S(2)}) collective-permute-start(bf16[128,1024]{1,0:T(8,128)(2,1)S(1)} %collective-permute-done.13), channel_id=1, source_target_pairs={{0,504},{8,0},{16,8},{24,16},{32,24},{40,32},{48,40},{56,48},{64,5... | collective-permute-start | bytes 786440 | tf_op jit(solution)/shard_map/ppermute | solution.py:163
  133.7 11.6 %collective-permute-start.3 = (bf16[128,1024]{1,0:T(8,128)(2,1)S(1)}, bf16[128,1024]{1,0:T(8,128)(2,1)S(1)}, u32[]{:S(2)}, u32[]{:S(2)}) collective-permute-start(bf16[128,1024]{1,0:T(8,128)(2,1)S(1)} %collective-permute-done.2), channel_id=1, source_target_pairs={{0,8},{8,16},{16,24},{24,32},{32,40},{40,48},{48,56},{56,64},{64,7... | collective-permute-start | bytes 786440 | tf_op jit(solution)/shard_map/ppermute | solution.py:162
  137.3 16.3 %collective-permute-start.19 = (bf16[128,1024]{1,0:T(8,128)(2,1)S(1)}, bf16[128,1024]{1,0:T(8,128)(2,1)S(1)}, u32[]{:S(2)}, u32[]{:S(2)}) collective-permute-start(bf16[128,1024]{1,0:T(8,128)(2,1)S(1)} %collective-permute-done.16), channel_id=1, source_target_pairs={{0,504},{8,0},{16,8},{24,16},{32,24},{40,32},{48,40},{56,48},{64,5... | collective-permute-start | bytes 786440 | tf_op jit(solution)/shard_map/ppermute | solution.py:163
  145.2 11.4 %collective-permute-start.4 = (bf16[128,1024]{1,0:T(8,128)(2,1)S(1)}, bf16[128,1024]{1,0:T(8,128)(2,1)S(1)}, u32[]{:S(2)}, u32[]{:S(2)}) collective-permute-start(bf16[128,1024]{1,0:T(8,128)(2,1)S(1)} %collective-permute-done.3), channel_id=1, source_target_pairs={{0,8},{8,16},{16,24},{24,32},{32,40},{40,48},{48,56},{56,64},{64,7... | collective-permute-start | bytes 786440 | tf_op jit(solution)/shard_map/ppermute | solution.py:162
  153.6 15.2 %collective-permute-start.22 = (bf16[128,1024]{1,0:T(8,128)(2,1)S(1)}, bf16[128,1024]{1,0:T(8,128)(2,1)S(1)}, u32[]{:S(2)}, u32[]{:S(2)}) collective-permute-start(bf16[128,1024]{1,0:T(8,128)(2,1)S(1)} %collective-permute-done.19), channel_id=1, source_target_pairs={{0,504},{8,0},{16,8},{24,16},{32,24},{40,32},{48,40},{56,48},{64,5... | collective-permute-start | bytes 786440 | tf_op jit(solution)/shard_map/ppermute | solution.py:163
  156.6 14.7 %collective-permute-start.5 = (bf16[128,1024]{1,0:T(8,128)(2,1)S(1)}, bf16[128,1024]{1,0:T(8,128)(2,1)S(1)}, u32[]{:S(2)}, u32[]{:S(2)}) collective-permute-start(bf16[128,1024]{1,0:T(8,128)(2,1)S(1)} %collective-permute-done.4), channel_id=1, source_target_pairs={{0,8},{8,16},{16,24},{24,32},{32,40},{40,48},{48,56},{56,64},{64,7... | collective-permute-start | bytes 786440 | tf_op jit(solution)/shard_map/ppermute | solution.py:162
  168.8 12.2 %collective-permute-start.25 = (bf16[128,1024]{1,0:T(8,128)(2,1)S(1)}, bf16[128,1024]{1,0:T(8,128)(2,1)S(1)}, u32[]{:S(2)}, u32[]{:S(2)}) collective-permute-start(bf16[128,1024]{1,0:T(8,128)(2,1)S(1)} %collective-permute-done.22), channel_id=1, source_target_pairs={{0,504},{8,0},{16,8},{24,16},{32,24},{40,32},{48,40},{56,48},{64,5... | collective-permute-start | bytes 786440 | tf_op jit(solution)/shard_map/ppermute | solution.py:163
  171.3 12.2 %collective-permute-start.6 = (bf16[128,1024]{1,0:T(8,128)(2,1)S(1)}, bf16[128,1024]{1,0:T(8,128)(2,1)S(1)}, u32[]{:S(2)}, u32[]{:S(2)}) collective-permute-start(bf16[128,1024]{1,0:T(8,128)(2,1)S(1)} %collective-permute-done.5), channel_id=1, source_target_pairs={{0,8},{8,16},{16,24},{24,32},{32,40},{40,48},{48,56},{56,64},{64,7... | collective-permute-start | bytes 786440 | tf_op jit(solution)/shard_map/ppermute | solution.py:162
  181.1 8.6 %collective-permute-start.28 = (bf16[128,1024]{1,0:T(8,128)(2,1)S(1)}, bf16[128,1024]{1,0:T(8,128)(2,1)}, u32[]{:S(2)}, u32[]{:S(2)}) collective-permute-start(bf16[128,1024]{1,0:T(8,128)(2,1)S(1)} %collective-permute-done.25), channel_id=1, source_target_pairs={{0,504},{8,0},{16,8},{24,16},{32,24},{40,32},{48,40},{56,48},{64,5... | collective-permute-start | bytes 786440 | tf_op jit(solution)/shard_map/ppermute | solution.py:163
  183.5 11.8 %collective-permute-start.7 = (bf16[128,1024]{1,0:T(8,128)(2,1)S(1)}, bf16[128,1024]{1,0:T(8,128)(2,1)S(1)}, u32[]{:S(2)}, u32[]{:S(2)}) collective-permute-start(bf16[128,1024]{1,0:T(8,128)(2,1)S(1)} %collective-permute-done.6), channel_id=1, source_target_pairs={{0,8},{8,16},{16,24},{24,32},{32,40},{40,48},{48,56},{56,64},{64,7... | collective-permute-start | bytes 786440 | tf_op jit(solution)/shard_map/ppermute | solution.py:162
  189.7 13.5 %collective-permute-start.31 = (bf16[128,1024]{1,0:T(8,128)(2,1)}, bf16[128,1024]{1,0:T(8,128)(2,1)}, u32[]{:S(2)}, u32[]{:S(2)}) collective-permute-start(bf16[128,1024]{1,0:T(8,128)(2,1)} %collective-permute-done.28), channel_id=1, source_target_pairs={{0,504},{8,0},{16,8},{24,16},{32,24},{40,32},{48,40},{56,48},{64,5... | collective-permute-start | bytes 786440 | tf_op jit(solution)/shard_map/ppermute | solution.py:163
  (3 other events, 9.6 us)

commit v3 on v2

--- a/solution.py
+++ b/solution.py
@@ -123,6 +123,136 @@
     )(blocks)
 
 
+def window_kernel(blk_sizes, rep_sizes, every, proj_ref, cot_ref, chosen_ref, sent_ref, out_ref, back_ref,
+                  p_got, cot_got, ch_got, send_sem, recv_sem, local_sem):
+    blk_count = math.prod(blk_sizes)
+    span = chosen_ref.shape[0]
+    blk_axes, rep_axes = every[: len(blk_sizes)], every[len(blk_sizes) :]
+    b = 0
+    for a, s in zip(blk_axes, blk_sizes):
+        b = b * s + lax.axis_index(a)
+    r = 0
+    for a, s in zip(rep_axes, rep_sizes):
+        r = r * s + lax.axis_index(a)
+
+    def target(j):
+        coords = []
+        rest = j
+        for s in reversed(blk_sizes):
+            coords.append(rest % s)
+            rest = rest // s
+        return tuple(reversed(coords)) + tuple(lax.axis_index(a) for a in rep_axes)
+
+    def copies(t):
+        ahead = target((b + span * r + t) % blk_count)
+        behind = target((b + blk_count - span * r - t) % blk_count)
+        return (
+            pltpu.make_async_remote_copy(proj_ref, p_got.at[t], send_sem.at[0, t], recv_sem.at[0, t],
+                                         device_id=ahead, device_id_type=MESH_IDS),
+            pltpu.make_async_remote_copy(cot_ref, cot_got.at[t], send_sem.at[1, t], recv_sem.at[1, t],
+                                         device_id=behind, device_id_type=MESH_IDS),
+            pltpu.make_async_remote_copy(sent_ref.at[t], ch_got.at[t], send_sem.at[2, t], recv_sem.at[2, t],
+                                         device_id=behind, device_id_type=MESH_IDS),
+        )
+
+    def local_copies():
+        return (
+            pltpu.make_async_copy(proj_ref, p_got.at[0], local_sem.at[0]),
+            pltpu.make_async_copy(cot_ref, cot_got.at[0], local_sem.at[1]),
+            pltpu.make_async_copy(sent_ref.at[0], ch_got.at[0], local_sem.at[2]),
+        )
+
+    barrier = pltpu.get_barrier_semaphore()
+    for t in range(span):
+        ahead = target((b + span * r + t) % blk_count)
+        behind = target((b + blk_count - span * r - t) % blk_count)
+
+        def greet(ahead=ahead, behind=behind):
+            pl.semaphore_signal(barrier, inc=1, device_id=ahead, device_id_type=MESH_IDS)
+            pl.semaphore_signal(barrier, inc=1, device_id=behind, device_id_type=MESH_IDS)
+
+        if t == 0:
+            pl.when(r != 0)(greet)
+        else:
+            greet()
+
+    @pl.when(r != 0)
+    def _():
+        pl.semaphore_wait(barrier, 2 * span)
+        for c in copies(0):
+            c.start()
+
+    @pl.when(r == 0)
+    def _():
+        pl.semaphore_wait(barrier, 2 * span - 2)
+        for c in local_copies():
+            c.start()
+
+    for t in range(1, span):
+        for c in copies(t):
+            c.start()
+
+    @pl.when(r != 0)
+    def _():
+        for c in copies(0):
+            c.wait_recv()
+
+    @pl.when(r == 0)
+    def _():
+        for c in local_copies():
+            c.wait()
+
+    for t in range(span):
+        if t > 0:
+            for c in copies(t):
+                c.wait_recv()
+        part = jnp.dot(chosen_ref[t], p_got[t], preferred_element_type=jnp.float32)
+        back = jnp.dot(ch_got[t], cot_got[t], preferred_element_type=jnp.float32)
+        if t == 0:
+            out_ref[...] = part
+            back_ref[...] = back
+        else:
+            out_ref[...] += part
+            back_ref[...] += back
+
+    @pl.when(r != 0)
+    def _():
+        for c in copies(0):
+            c.wait_send()
+
+    for t in range(1, span):
+        for c in copies(t):
+            c.wait_send()
+
+
+def window(projected, cotangent, chosen, chosen_t, blk_sizes, rep_sizes, every, collective):
+    span = chosen.shape[0]
+    rows, width = projected.shape
+    vmem = pl.BlockSpec(memory_space=pltpu.VMEM)
+    moved = (2 * rows * width * 2 + rows * rows * 2) * span
+    return pl.pallas_call(
+        functools.partial(window_kernel, blk_sizes, rep_sizes, every),
+        out_shape=(
+            jax.ShapeDtypeStruct((rows, width), jnp.float32),
+            jax.ShapeDtypeStruct((rows, width), jnp.float32),
+        ),
+        in_specs=[vmem, vmem, vmem, vmem],
+        out_specs=(vmem, vmem),
+        scratch_shapes=[
+            pltpu.VMEM((span, rows, width), projected.dtype),
+            pltpu.VMEM((span, rows, width), cotangent.dtype),
+            pltpu.VMEM((span, rows, rows), chosen.dtype),
+            pltpu.SemaphoreType.DMA((3, span)),
+            pltpu.SemaphoreType.DMA((3, span)),
+            pltpu.SemaphoreType.DMA((3,)),
+        ],
+        compiler_params=pltpu.CompilerParams(collective_id=collective, has_side_effects=True),
+        cost_estimate=pl.CostEstimate(
+            flops=4 * span * rows * rows * width, transcendentals=0, bytes_accessed=2 * moved
+        ),
+    )(projected, cotangent, chosen, chosen_t)
+
+
 def shards(hidden_pre, adj_vals, adj_cols, w_out, cotangent):
     row_count, feature_width = hidden_pre.shape
     blk_count = lax.axis_size(BLK)
@@ -139,30 +269,17 @@
     own_cols = adj_cols[0]
     section = jnp.mod(blk_pos - own_cols, blk_count) - rep_pos * span
 
-    visiting = lax.ppermute(projected, EVERY, shifted_pairs(blk_count, rep_count, span))
-    back = shifted_pairs(blk_count, rep_count, -span)
-    cot_cur = lax.ppermute(cotangent, EVERY, back)
-    vals_cur = lax.ppermute(own_vals, EVERY, back)
-    cols_cur = lax.ppermute(own_cols, EVERY, back)
-
-    out_sum = jnp.zeros((row_count, feature_width), jnp.float32)
-    back_sum = jnp.zeros((row_count, feature_width), jnp.float32)
-    for turn in range(span):
-        chosen = jnp.zeros_like(own_vals[0])
-        for k in range(slots):
-            chosen = chosen + jnp.where(section[k] == turn, own_vals[k], 0)
-        out_sum = out_sum + jnp.dot(chosen, visiting, preferred_element_type=jnp.float32)
-        chosen_back = jnp.zeros_like(own_vals[0])
-        for k in range(slots):
-            chosen_back = chosen_back + jnp.where(cols_cur[k] == blk_pos, vals_cur[k], 0)
-        back_sum = back_sum + lax.dot_general(
-            chosen_back, cot_cur, (((0,), (0,)), ((), ())), preferred_element_type=jnp.float32
-        )
-        if turn < span - 1:
-            visiting = lax.ppermute(visiting, BLK, ring_pairs(blk_count, 1))
-            cot_cur = lax.ppermute(cot_cur, BLK, ring_pairs(blk_count, -1))
-            vals_cur = lax.ppermute(vals_cur, BLK, ring_pairs(blk_count, -1))
-            cols_cur = lax.ppermute(cols_cur, BLK, ring_pairs(blk_count, -1))
+    chosen = jnp.stack(
+        [
+            sum(jnp.where(section[k] == turn, own_vals[k], 0) for k in range(slots))
+            for turn in range(span)
+        ]
+    )
+    blk_sizes = tuple(lax.axis_size(a) for a in BLK)
+    rep_sizes = tuple(lax.axis_size(a) for a in REP)
+    out_sum, back_sum = window(
+        projected, cotangent, chosen, jnp.transpose(chosen, (0, 2, 1)), blk_sizes, rep_sizes, EVERY, 3
+    )
 
     rows = out_sum.shape[0]
     both = jnp.stack([out_sum, back_sum]).reshape(2, rows, rep_count, cols_here)

time: 321 us -> 287 us (0.89)
  Pallas kernels: 103 us -> 253 us
  starting transfers between devices: 105 us -> 0 us
  waiting for transfers between devices: 61 us -> 0 us
  between operations: 22 us -> 11.1 us
  matrix products: 8.83 us -> 3.83 us
    ppermute x32 -> x0, starting transfers between devices: 105 us -> none  [the longest x7 26.6 us: shards(): vals_cur = lax.ppermute(vals_cur, BLK, ring_pairs(blk_count, -1))]
    pallas_call x0 -> x1, Pallas kernels: none -> 83.4 us  [window(): pl.pallas_call(functools.partial(window_kernel, blk_sizes, rep_sizes, eve...]
    pallas_call x3, Pallas kernels: 103 us -> 169 us  [exchange(): pl.pallas_call(functools.partial(exchange_kernel, group, sizes, every, br...]
    ppermute x32 -> x0, waiting for transfers between devices: 61 us -> none  [the longest x7 26.4 us: shards(): cot_cur = lax.ppermute(cot_cur, BLK, ring_pairs(blk_count, -1))]
    dot_general x16 -> x0, matrix products: 5.72 us -> none  [the longest x8 3.96 us: shards(): lax.dot_general(chosen_back, cot_cur, (((0,), (0,)), ((), ())), preferred...]
    slice x9 -> x2, local copies, waits for them, and re-layouts: 5.24 us -> 1.37 us  [the longest x1 0.78 us: shards(): own_vals[k]]
  transfers between devices with their start and end apart: 32 -> 0, of which waited for: 17 -> 0; matrix products, arithmetic and copies ran while one was open for 4% -> 0% of each run, Pallas kernels for 0% -> 0%
where the time goes in v3:
time: 287 us; the launch traced here: 283 us
  Pallas kernels  253 us (88%)
  between operations  11.1 us (4%)
  local copies, waits for them, and re-layouts  9.13 us (3%)
  other arithmetic  6.15 us (2%)
  matrix products  3.83 us (1%)
    pallas_call x3, Pallas kernels, exchange(): pl.pallas_call(functools.partial(exchange_kernel, group, sizes, every, br...  169 us
    pallas_call x1, Pallas kernels, window(): pl.pallas_call(functools.partial(window_kernel, blk_sizes, rep_sizes, eve...  83.4 us

profile of v3, /device:TPU:6, one launch (start us, length us, event | category | flops | bytes accessed | tf_op | source)
XLA Modules:
  0.0 283.0 jit_solution(12665303852563946275)
XLA Ops:
  0.6 0.0 copy-start
  0.7 0.8 fusion.6
  1.5 0.6 fusion.10
  12.4 0.8 fusion.9
  13.2 0.1 copy.21
  13.3 0.1 copy.22
  13.7 0.0 copy-start.1
  13.7 1.2 copy.12
  14.9 0.0 copy-done
  14.9 1.2 convolution_convert_fusion.proj_ref
  16.1 0.9 copy.15.chosen_ref
  17.0 0.0 copy-done.1
  17.0 83.4 %shard_map.76 = (f32[128,1024]{1,0:T(8,128)}, f32[128,1024]{1,0:T(8,128)}) custom-call(bf16[128,1024]{1,0:T(8,128)(2,1)} %convolution_convert_fusion.proj_ref, bf16[128,1024]{1,0:T(8,128)(2,1)} %cot_ref.1, bf16[8,128,128]{2,1,0:T(8,128)(2,1)} %copy.15.chosen_ref, bf16[8,128,128]{2,1,0:T(8,128)(2,1)} %bitcast.59), custom_call_target="tpu_custom_call" | custom-call | flops 536870912 | bytes 8912896 | tf_op jit(solution)/shard_map/pallas_call | solution.py:233
  100.5 1.2 copy.16
  101.7 0.2 copy.18
  101.9 1.2 copy.17
  103.1 1.0 copy.19
  104.2 2.1 maximum_bitcast_fusion.src_ref
  106.3 122.4 %shard_map.77 = f32[8,2,128,128]{3,2,1,0:T(8,128)} custom-call(f32[8,2,128,128]{3,2,1,0:T(8,128)} %maximum_bitcast_fusion.src_ref), custom_call_target="tpu_custom_call" | custom-call | bytes 3145728 | tf_op jit(solution)/shard_map/pallas_call | solution.py:111
  228.7 1.3 reduce_sum.18
  230.0 0.6 fusion.5
  230.6 1.0 fusion.3.src_ref
  231.6 35.1 %shard_map.78 = f32[64,16,128]{2,1,0:T(8,128)} custom-call(f32[64,16,128]{2,1,0:T(8,128)} %fusion.3.src_ref), custom_call_target="tpu_custom_call" | custom-call | bytes 1572864 | tf_op jit(solution)/shard_map/pallas_call | solution.py:111
  266.7 1.7 reduce_sum.19
  268.4 11.8 %shard_map.79 = bf16[8,128,128]{2,1,0:T(8,128)(2,1)} custom-call(bf16[128,128]{1,0:T(8,128)(2,1)} %get-tuple-element.7.src_ref), custom_call_target="tpu_custom_call" | custom-call | bytes 786432 | tf_op jit(solution)/shard_map/pallas_call | solution.py:111
  280.2 1.1 copy.20
  281.4 1.7 fusion
  (9 shorter events, 0.2 us)
Async XLA Ops:
  0.6 14.3 %copy-start = (bf16[1024,1024]{1,0:T(8,128)(2,1)S(1)}, bf16[1024,1024]{1,0:T(8,128)(2,1)}, u32[]{:S(2)}) copy-start(bf16[1024,1024]{1,0:T(8,128)(2,1)} %param.8) | copy-start | bytes 6291460
  13.7 3.3 %copy-start.1 = (bf16[8,128,128]{1,2,0:T(8,128)(2,1)}, bf16[8,128,128]{1,2,0:T(8,128)(2,1)S(1)}, u32[]{:S(2)}) copy-start(bf16[8,128,128]{1,2,0:T(8,128)(2,1)S(1)} %bitcast_dynamic-update-slice_fusion) | copy-start | bytes 786436

commit v4 on v3

--- a/solution.py
+++ b/solution.py
@@ -134,78 +134,89 @@
     r = 0
     for a, s in zip(rep_axes, rep_sizes):
         r = r * s + lax.axis_index(a)
-
-    def target(j):
+    far = span * r
+
+    def target(offset):
+        rest = (b + offset + blk_count) % blk_count
         coords = []
-        rest = j
         for s in reversed(blk_sizes):
             coords.append(rest % s)
             rest = rest // s
         return tuple(reversed(coords)) + tuple(lax.axis_index(a) for a in rep_axes)
 
-    def copies(t):
-        ahead = target((b + span * r + t) % blk_count)
-        behind = target((b + blk_count - span * r - t) % blk_count)
+    def remote(src, dst, kind, t, offset):
+        return pltpu.make_async_remote_copy(src, dst, send_sem.at[kind, t], recv_sem.at[kind, t],
+                                            device_id=target(offset), device_id_type=MESH_IDS)
+
+    def relay_moves():
         return (
-            pltpu.make_async_remote_copy(proj_ref, p_got.at[t], send_sem.at[0, t], recv_sem.at[0, t],
-                                         device_id=ahead, device_id_type=MESH_IDS),
-            pltpu.make_async_remote_copy(cot_ref, cot_got.at[t], send_sem.at[1, t], recv_sem.at[1, t],
-                                         device_id=behind, device_id_type=MESH_IDS),
-            pltpu.make_async_remote_copy(sent_ref.at[t], ch_got.at[t], send_sem.at[2, t], recv_sem.at[2, t],
-                                         device_id=behind, device_id_type=MESH_IDS),
-        )
-
-    def local_copies():
+            remote(proj_ref, p_got.at[0], 0, 0, far),
+            remote(cot_ref, cot_got.at[0], 1, 0, -far),
+            remote(sent_ref.at[0], ch_got.at[0], 2, 0, -far),
+        )
+
+    def local_moves():
         return (
             pltpu.make_async_copy(proj_ref, p_got.at[0], local_sem.at[0]),
             pltpu.make_async_copy(cot_ref, cot_got.at[0], local_sem.at[1]),
             pltpu.make_async_copy(sent_ref.at[0], ch_got.at[0], local_sem.at[2]),
         )
 
+    def chosen_move(t):
+        return remote(sent_ref.at[t], ch_got.at[t], 2, t, -far - t)
+
+    def forwards(t):
+        return (
+            remote(p_got.at[0], p_got.at[t], 0, t, t),
+            remote(cot_got.at[0], cot_got.at[t], 1, t, -t),
+        )
+
     barrier = pltpu.get_barrier_semaphore()
-    for t in range(span):
-        ahead = target((b + span * r + t) % blk_count)
-        behind = target((b + blk_count - span * r - t) % blk_count)
-
-        def greet(ahead=ahead, behind=behind):
-            pl.semaphore_signal(barrier, inc=1, device_id=ahead, device_id_type=MESH_IDS)
-            pl.semaphore_signal(barrier, inc=1, device_id=behind, device_id_type=MESH_IDS)
-
-        if t == 0:
-            pl.when(r != 0)(greet)
-        else:
-            greet()
+
+    def greet(offset):
+        pl.semaphore_signal(barrier, inc=1, device_id=target(offset), device_id_type=MESH_IDS)
+        pl.semaphore_signal(barrier, inc=1, device_id=target(-offset), device_id_type=MESH_IDS)
+
+    for t in range(1, span):
+        greet(far + t)
+        greet(t)
 
     @pl.when(r != 0)
     def _():
-        pl.semaphore_wait(barrier, 2 * span)
-        for c in copies(0):
+        greet(far)
+        greet(far)
+        pl.semaphore_wait(barrier, 4 * span)
+        for c in relay_moves():
             c.start()
 
     @pl.when(r == 0)
     def _():
-        pl.semaphore_wait(barrier, 2 * span - 2)
-        for c in local_copies():
+        pl.semaphore_wait(barrier, 4 * span - 4)
+        for c in local_moves():
             c.start()
 
     for t in range(1, span):
-        for c in copies(t):
+        chosen_move(t).start()
+
+    @pl.when(r != 0)
+    def _():
+        for c in relay_moves():
+            c.wait_recv()
+
+    @pl.when(r == 0)
+    def _():
+        for c in local_moves():
+            c.wait()
+
+    for t in range(1, span):
+        for c in forwards(t):
             c.start()
-
-    @pl.when(r != 0)
-    def _():
-        for c in copies(0):
-            c.wait_recv()
-
-    @pl.when(r == 0)
-    def _():
-        for c in local_copies():
-            c.wait()
 
     for t in range(span):
         if t > 0:
-            for c in copies(t):
+            for c in forwards(t):
                 c.wait_recv()
+            chosen_move(t).wait_recv()
         part = jnp.dot(chosen_ref[t], p_got[t], preferred_element_type=jnp.float32)
         back = jnp.dot(ch_got[t], cot_got[t], preferred_element_type=jnp.float32)
         if t == 0:
@@ -217,11 +228,12 @@
 
     @pl.when(r != 0)
     def _():
-        for c in copies(0):
+        for c in relay_moves():
             c.wait_send()
 
     for t in range(1, span):
-        for c in copies(t):
+        chosen_move(t).wait_send()
+        for c in forwards(t):
             c.wait_send()
 
 

time: 287 us -> 215 us (0.75)
  Pallas kernels: 253 us -> 181 us
    pallas_call x3, Pallas kernels: 169 us -> 112 us  [exchange(): pl.pallas_call(functools.partial(exchange_kernel, group, sizes, every, br...]
    pallas_call x1, Pallas kernels: 83.4 us -> 69.3 us  [window(): pl.pallas_call(functools.partial(window_kernel, blk_sizes, rep_sizes, eve...]
where the time goes in v4:
time: 215 us; the launch traced here: 211 us
  Pallas kernels  181 us (84%)
  between operations  11.1 us (5%)
  local copies, waits for them, and re-layouts  9.13 us (4%)
  other arithmetic  6.15 us (3%)
  matrix products  3.84 us (2%)
    pallas_call x3, Pallas kernels, exchange(): pl.pallas_call(functools.partial(exchange_kernel, group, sizes, every, br...  112 us
    pallas_call x1, Pallas kernels, window(): pl.pallas_call(functools.partial(window_kernel, blk_sizes, rep_sizes, eve...  69.3 us

profile of v4, /device:TPU:6, one launch (start us, length us, event | category | flops | bytes accessed | tf_op | source)
XLA Modules:
  0.0 211.4 jit_solution(13857392169404101454)
XLA Ops:
  0.6 0.0 copy-start
  0.7 0.8 fusion.6
  1.5 0.6 fusion.10
  12.4 0.8 fusion.9
  13.2 0.1 copy.21
  13.3 0.1 copy.22
  13.7 0.0 copy-start.1
  13.7 1.2 copy.12
  14.9 0.0 copy-done
  14.9 1.2 convolution_convert_fusion.proj_ref
  16.1 0.9 copy.15.chosen_ref
  17.0 0.0 copy-done.1
  17.0 69.3 %shard_map.76 = (f32[128,1024]{1,0:T(8,128)}, f32[128,1024]{1,0:T(8,128)}) custom-call(bf16[128,1024]{1,0:T(8,128)(2,1)} %convolution_convert_fusion.proj_ref, bf16[128,1024]{1,0:T(8,128)(2,1)} %cot_ref.1, bf16[8,128,128]{2,1,0:T(8,128)(2,1)} %copy.15.chosen_ref, bf16[8,128,128]{2,1,0:T(8,128)(2,1)} %bitcast.59), custom_call_target="tpu_custom_call" | custom-call | flops 536870912 | bytes 8912896 | tf_op jit(solution)/shard_map/pallas_call | solution.py:245
  86.3 1.2 copy.16
  87.5 0.2 copy.18
  87.8 1.2 copy.17
  89.0 1.0 copy.19
  90.0 2.1 maximum_bitcast_fusion.src_ref
  92.1 55.4 %shard_map.77 = f32[8,2,128,128]{3,2,1,0:T(8,128)} custom-call(f32[8,2,128,128]{3,2,1,0:T(8,128)} %maximum_bitcast_fusion.src_ref), custom_call_target="tpu_custom_call" | custom-call | bytes 3145728 | tf_op jit(solution)/shard_map/pallas_call | solution.py:111
  147.6 1.3 reduce_sum.18
  148.9 0.6 fusion.5
  149.5 1.0 fusion.3.src_ref
  150.5 42.0 %shard_map.78 = f32[64,16,128]{2,1,0:T(8,128)} custom-call(f32[64,16,128]{2,1,0:T(8,128)} %fusion.3.src_ref), custom_call_target="tpu_custom_call" | custom-call | bytes 1572864 | tf_op jit(solution)/shard_map/pallas_call | solution.py:111
  192.5 1.7 reduce_sum.19
  194.2 14.5 %shard_map.79 = bf16[8,128,128]{2,1,0:T(8,128)(2,1)} custom-call(bf16[128,128]{1,0:T(8,128)(2,1)} %get-tuple-element.7.src_ref), custom_call_target="tpu_custom_call" | custom-call | bytes 786432 | tf_op jit(solution)/shard_map/pallas_call | solution.py:111
  208.7 1.1 copy.20
  209.8 1.7 fusion
  (9 shorter events, 0.2 us)
Async XLA Ops:
  0.6 14.3 %copy-start = (bf16[1024,1024]{1,0:T(8,128)(2,1)S(1)}, bf16[1024,1024]{1,0:T(8,128)(2,1)}, u32[]{:S(2)}) copy-start(bf16[1024,1024]{1,0:T(8,128)(2,1)} %param.8) | copy-start | bytes 6291460
  13.7 3.3 %copy-start.1 = (bf16[8,128,128]{1,2,0:T(8,128)(2,1)}, bf16[8,128,128]{1,2,0:T(8,128)(2,1)S(1)}, u32[]{:S(2)}) copy-start(bf16[8,128,128]{1,2,0:T(8,128)(2,1)S(1)} %bitcast_dynamic-update-slice_fusion) | copy-start | bytes 786436

commit v5 on v4

--- a/solution.py
+++ b/solution.py
@@ -42,13 +42,20 @@
     return moved
 
 
-def exchange_kernel(group, sizes, every, broadcast, src_ref, out_ref, landed, send_sem, recv_sem):
-    count = math.prod(sizes)
-    me = 0
-    for a, s in zip(group, sizes):
-        me = me * s + lax.axis_index(a)
-
-    def target(d):
+def exchange_kernel(plans, every, *refs):
+    count_of = [math.prod(sizes) for _, sizes, _ in plans]
+    n = len(plans)
+    srcs, outs = refs[:n], refs[n : 2 * n]
+    landed, send_sems, recv_sems = refs[2 * n : 3 * n], refs[3 * n : 4 * n], refs[4 * n : 5 * n]
+    barrier = pltpu.get_barrier_semaphore()
+
+    def position(group, sizes):
+        me = 0
+        for a, s in zip(group, sizes):
+            me = me * s + lax.axis_index(a)
+        return me
+
+    def target(group, sizes, d):
         coords = {}
         rest = d
         for a, s in reversed(list(zip(group, sizes))):
@@ -56,71 +63,76 @@
             rest = rest // s
         return tuple(coords[a] if a in coords else lax.axis_index(a) for a in every)
 
-    def source(d):
-        return src_ref if broadcast else src_ref.at[d]
-
-    def copy_to(d, o):
+    def copy(i, d, slot, o):
+        group, sizes, broadcast = plans[i]
         return pltpu.make_async_remote_copy(
-            src_ref=source(d),
-            dst_ref=landed.at[me],
-            send_sem=send_sem.at[o],
-            recv_sem=recv_sem.at[me],
-            device_id=target(d),
+            src_ref=srcs[i] if broadcast else srcs[i].at[d],
+            dst_ref=landed[i].at[slot],
+            send_sem=send_sems[i].at[o],
+            recv_sem=recv_sems[i].at[slot],
+            device_id=target(group, sizes, d),
             device_id_type=MESH_IDS,
         )
 
-    barrier = pltpu.get_barrier_semaphore()
-
-    def greet(o, carry):
-        pl.semaphore_signal(barrier, inc=1, device_id=target((me + o) % count), device_id_type=MESH_IDS)
-        return carry
-
-    lax.fori_loop(1, count, greet, 0)
-    pl.semaphore_wait(barrier, count - 1)
-
-    def send(o, carry):
-        copy_to((me + o) % count, o).start()
-        return carry
-
-    lax.fori_loop(1, count, send, 0)
-    out_ref[me] = src_ref[...] if broadcast else src_ref[me]
-
-    def finish(o, carry):
-        copy_to((me + o) % count, o).wait_send()
-        sender = (me + count - o) % count
-        incoming = pltpu.make_async_remote_copy(
-            src_ref=source(sender),
-            dst_ref=landed.at[sender],
-            send_sem=send_sem.at[o],
-            recv_sem=recv_sem.at[sender],
-            device_id=target(sender),
-            device_id_type=MESH_IDS,
-        )
-        incoming.wait_recv()
-        out_ref[sender] = landed[sender]
-        return carry
-
-    lax.fori_loop(1, count, finish, 0)
+    for i, (group, sizes, _) in enumerate(plans):
+        me, count = position(group, sizes), count_of[i]
+
+        def greet(o, carry, group=group, sizes=sizes, me=me, count=count):
+            pl.semaphore_signal(barrier, inc=1, device_id=target(group, sizes, (me + o) % count),
+                                device_id_type=MESH_IDS)
+            return carry
+
+        lax.fori_loop(1, count, greet, 0)
+    pl.semaphore_wait(barrier, sum(count_of) - n)
+
+    for i, (group, sizes, broadcast) in enumerate(plans):
+        me, count = position(group, sizes), count_of[i]
+
+        def send(o, carry, i=i, me=me, count=count):
+            copy(i, (me + o) % count, me, o).start()
+            return carry
+
+        lax.fori_loop(1, count, send, 0)
+        outs[i][me] = srcs[i][...] if broadcast else srcs[i][me]
+
+    for i, (group, sizes, broadcast) in enumerate(plans):
+        me, count = position(group, sizes), count_of[i]
+
+        def finish(o, carry, i=i, me=me, count=count):
+            copy(i, (me + o) % count, me, o).wait_send()
+            sender = (me + count - o) % count
+            copy(i, sender, sender, o).wait_recv()
+            outs[i][sender] = landed[i][sender]
+            return carry
+
+        lax.fori_loop(1, count, finish, 0)
+
+
+def exchange_many(items, every, collective):
+    plans, shapes, total = [], [], 0
+    for blocks, group, broadcast in items:
+        sizes = tuple(lax.axis_size(a) for a in group)
+        count = math.prod(sizes)
+        shape = (count,) + (blocks.shape if broadcast else blocks.shape[1:])
+        plans.append((group, sizes, broadcast))
+        shapes.append(jax.ShapeDtypeStruct(shape, blocks.dtype))
+        total += math.prod(shape) * blocks.dtype.itemsize
+    vmem = pl.BlockSpec(memory_space=pltpu.VMEM)
+    return pl.pallas_call(
+        functools.partial(exchange_kernel, tuple(plans), every),
+        out_shape=tuple(shapes),
+        in_specs=[vmem] * len(items),
+        out_specs=tuple([vmem] * len(items)),
+        scratch_shapes=[pltpu.VMEM(x.shape, x.dtype) for x in shapes]
+        + [pltpu.SemaphoreType.DMA((x.shape[0],)) for x in shapes]
+        + [pltpu.SemaphoreType.DMA((x.shape[0],)) for x in shapes],
+        compiler_params=pltpu.CompilerParams(collective_id=collective, has_side_effects=True),
+        cost_estimate=pl.CostEstimate(flops=0, transcendentals=0, bytes_accessed=3 * total),
+    )(*[blocks for blocks, _, _ in items])
 
 
 def exchange(blocks, group, every, collective, broadcast=False):
-    sizes = tuple(lax.axis_size(a) for a in group)
-    count = math.prod(sizes)
-    shape = (count,) + (blocks.shape if broadcast else blocks.shape[1:])
-    size = math.prod(shape) * blocks.dtype.itemsize
-    return pl.pallas_call(
-        functools.partial(exchange_kernel, group, sizes, every, broadcast),
-        out_shape=jax.ShapeDtypeStruct(shape, blocks.dtype),
-        in_specs=[pl.BlockSpec(memory_space=pltpu.VMEM)],
-        out_specs=pl.BlockSpec(memory_space=pltpu.VMEM),
-        scratch_shapes=[
-            pltpu.VMEM(shape, blocks.dtype),
-            pltpu.SemaphoreType.DMA((count,)),
-            pltpu.SemaphoreType.DMA((count,)),
-        ],
-        compiler_params=pltpu.CompilerParams(collective_id=collective, has_side_effects=True),
-        cost_estimate=pl.CostEstimate(flops=0, transcendentals=0, bytes_accessed=3 * size),
-    )(blocks)
+    return exchange_many([(blocks, group, broadcast)], every, collective)[0]
 
 
 def window_kernel(blk_sizes, rep_sizes, every, proj_ref, cot_ref, chosen_ref, sent_ref, out_ref, back_ref,
@@ -301,8 +313,10 @@
     term = lax.dot_general(
         hidden_act, back_grad, (((0,), (0,)), ((), ())), preferred_element_type=jnp.float32
     )
-    grad_weight = exchange(term.reshape(blk_count, -1, cols_here), BLK, EVERY, 1).sum(0)
-    gathered = exchange(back_grad, REP, EVERY, 2, broadcast=True)
+    weight_parts, gathered = exchange_many(
+        [(term.reshape(blk_count, -1, cols_here), BLK, False), (back_grad, REP, True)], EVERY, 1
+    )
+    grad_weight = weight_parts.sum(0)
     back_full = jnp.transpose(gathered, (1, 0, 2)).reshape(rows, feature_width)
     w_rows = lax.dynamic_slice_in_dim(w_out, rep_pos * cols_here, cols_here, 0)
     grad_in = lax.dot_general(

time: 215 us -> 201 us (0.935)
  Pallas kernels: 181 us -> 167 us
    pallas_call x3 -> x2, Pallas kernels: 112 us -> 97.6 us  [exchange_many(): pl.pallas_call(functools.partial(exchange_kernel, tuple(plans), every), o...]
where the time goes in v5:
time: 201 us; the launch traced here: 197 us
  Pallas kernels  167 us (83%)
  between operations  11.1 us (6%)
  local copies, waits for them, and re-layouts  9.11 us (5%)
  other arithmetic  6.14 us (3%)
  matrix products  3.84 us (2%)
    pallas_call x2, Pallas kernels, exchange_many(): pl.pallas_call(functools.partial(exchange_kernel, tuple(plans), every), o...  97.6 us
    pallas_call x1, Pallas kernels, window(): pl.pallas_call(functools.partial(window_kernel, blk_sizes, rep_sizes, eve...  69.3 us

profile of v5, /device:TPU:6, one launch (start us, length us, event | category | flops | bytes accessed | tf_op | source)
XLA Modules:
  0.0 197.1 jit_solution(16401436990033497893)
XLA Ops:
  0.6 0.0 copy-start
  0.7 0.8 fusion.6
  1.5 0.6 fusion.10
  12.4 0.8 fusion.9
  13.2 0.1 copy.21
  13.3 0.1 copy.22
  13.7 0.0 copy-start.1
  13.7 1.2 copy.12
  14.9 0.0 copy-done
  14.9 1.2 convolution_convert_fusion.proj_ref
  16.1 0.9 copy.15.chosen_ref
  17.0 0.0 copy-done.1
  17.0 69.3 %shard_map.76 = (f32[128,1024]{1,0:T(8,128)}, f32[128,1024]{1,0:T(8,128)}) custom-call(bf16[128,1024]{1,0:T(8,128)(2,1)} %convolution_convert_fusion.proj_ref, bf16[128,1024]{1,0:T(8,128)(2,1)} %cot_ref.1, bf16[8,128,128]{2,1,0:T(8,128)(2,1)} %copy.15.chosen_ref, bf16[8,128,128]{2,1,0:T(8,128)(2,1)} %bitcast.58), custom_call_target="tpu_custom_call" | custom-call | flops 536870912 | bytes 8912896 | tf_op jit(solution)/shard_map/pallas_call | solution.py:257
  86.3 1.2 copy.16
  87.5 0.2 copy.18
  87.8 1.2 copy.17
  89.0 1.0 copy.19
  90.0 2.1 %maximum_bitcast_fusion.refs_0_ = f32[8,2,128,128]{3,2,1,0:T(8,128)} fusion(f32[1,128,8,128]{3,1,0,2:T(8,128)} %copy.19, f32[1,128,8,128]{3,1,0,2:T(8,128)S(1)} %copy.18), kind=kLoop, calls=%fused_computation.3 | loop fusion | flops 262144 | bytes 2097152 | tf_op jit(solution)/shard_map/transpose | solution.py:310
  92.1 55.4 %shard_map.77 = f32[8,2,128,128]{3,2,1,0:T(8,128)} custom-call(f32[8,2,128,128]{3,2,1,0:T(8,128)} %maximum_bitcast_fusion.refs_0_), custom_call_target="tpu_custom_call" | custom-call | bytes 3145728 | tf_op jit(solution)/shard_map/pallas_call | solution.py:121
  147.5 1.3 reduce_sum.18
  148.8 0.6 fusion.5
  149.5 1.0 fusion.3.refs_0_
  150.4 42.2 %shard_map.78 = (f32[64,16,128]{2,1,0:T(8,128)}, bf16[8,128,128]{2,1,0:T(8,128)(2,1)}) custom-call(f32[64,16,128]{2,1,0:T(8,128)} %fusion.3.refs_0_, bf16[128,128]{1,0:T(8,128)(2,1)} %get-tuple-element.11.refs_1_), custom_call_target="tpu_custom_call" | custom-call | bytes 2359296 | tf_op jit(solution)/shard_map/pallas_call | solution.py:121
  192.6 1.7 reduce_sum.19
  194.3 1.1 copy.20
  195.5 1.7 fusion
  (9 shorter events, 0.2 us)
Async XLA Ops:
  0.6 14.3 %copy-start = (bf16[1024,1024]{1,0:T(8,128)(2,1)S(1)}, bf16[1024,1024]{1,0:T(8,128)(2,1)}, u32[]{:S(2)}) copy-start(bf16[1024,1024]{1,0:T(8,128)(2,1)} %param.8) | copy-start | bytes 6291460
  13.7 3.3 %copy-start.1 = (bf16[8,128,128]{1,2,0:T(8,128)(2,1)}, bf16[8,128,128]{1,2,0:T(8,128)(2,1)S(1)}, u32[]{:S(2)}) copy-start(bf16[8,128,128]{1,2,0:T(8,128)(2,1)S(1)} %bitcast_dynamic-update-slice_fusion) | copy-start | bytes 786436

commit v6 on v5

--- a/solution.py
+++ b/solution.py
@@ -47,6 +47,7 @@
     n = len(plans)
     srcs, outs = refs[:n], refs[n : 2 * n]
     landed, send_sems, recv_sems = refs[2 * n : 3 * n], refs[3 * n : 4 * n], refs[4 * n : 5 * n]
+    totals = refs[5 * n : 6 * n]
     barrier = pltpu.get_barrier_semaphore()
 
     def position(group, sizes):
@@ -64,7 +65,8 @@
         return tuple(coords[a] if a in coords else lax.axis_index(a) for a in every)
 
     def copy(i, d, slot, o):
-        group, sizes, broadcast = plans[i]
+        group, sizes, mode = plans[i]
+        broadcast = mode == "concat"
         return pltpu.make_async_remote_copy(
             src_ref=srcs[i] if broadcast else srcs[i].at[d],
             dst_ref=landed[i].at[slot],
@@ -85,7 +87,7 @@
         lax.fori_loop(1, count, greet, 0)
     pl.semaphore_wait(barrier, sum(count_of) - n)
 
-    for i, (group, sizes, broadcast) in enumerate(plans):
+    for i, (group, sizes, mode) in enumerate(plans):
         me, count = position(group, sizes), count_of[i]
 
         def send(o, carry, i=i, me=me, count=count):
@@ -93,46 +95,60 @@
             return carry
 
         lax.fori_loop(1, count, send, 0)
-        outs[i][me] = srcs[i][...] if broadcast else srcs[i][me]
-
-    for i, (group, sizes, broadcast) in enumerate(plans):
+        if mode == "concat":
+            width = srcs[i].shape[-1]
+            outs[i][:, pl.ds(pl.multiple_of(me * width, width), width)] = srcs[i][...]
+        else:
+            totals[i][...] = srcs[i][me].astype(jnp.float32)
+
+    for i, (group, sizes, mode) in enumerate(plans):
         me, count = position(group, sizes), count_of[i]
 
-        def finish(o, carry, i=i, me=me, count=count):
+        def finish(o, carry, i=i, me=me, count=count, mode=mode):
             copy(i, (me + o) % count, me, o).wait_send()
             sender = (me + count - o) % count
             copy(i, sender, sender, o).wait_recv()
-            outs[i][sender] = landed[i][sender]
+            if mode == "concat":
+                width = srcs[i].shape[-1]
+                outs[i][:, pl.ds(pl.multiple_of(sender * width, width), width)] = landed[i][sender]
+            else:
+                totals[i][...] += landed[i][sender].astype(jnp.float32)
             return carry
 
         lax.fori_loop(1, count, finish, 0)
+        if mode != "concat":
+            outs[i][...] = totals[i][...].astype(outs[i].dtype)
 
 
 def exchange_many(items, every, collective):
-    plans, shapes, total = [], [], 0
-    for blocks, group, broadcast in items:
+    plans, shapes, landings, totals, counts, total = [], [], [], [], [], 0
+    for blocks, group, mode, dtype in items:
         sizes = tuple(lax.axis_size(a) for a in group)
         count = math.prod(sizes)
-        shape = (count,) + (blocks.shape if broadcast else blocks.shape[1:])
-        plans.append((group, sizes, broadcast))
-        shapes.append(jax.ShapeDtypeStruct(shape, blocks.dtype))
-        total += math.prod(shape) * blocks.dtype.itemsize
+        if mode == "concat":
+            slot_shape = blocks.shape
+            shapes.append(jax.ShapeDtypeStruct(blocks.shape[:-1] + (count * blocks.shape[-1],), dtype))
+        else:
+            slot_shape = blocks.shape[1:]
+            shapes.append(jax.ShapeDtypeStruct(slot_shape, dtype))
+        plans.append((group, sizes, mode))
+        counts.append(count)
+        landings.append(pltpu.VMEM((count,) + slot_shape, blocks.dtype))
+        totals.append(pltpu.VMEM(slot_shape, jnp.float32))
+        total += count * math.prod(slot_shape) * blocks.dtype.itemsize
     vmem = pl.BlockSpec(memory_space=pltpu.VMEM)
     return pl.pallas_call(
         functools.partial(exchange_kernel, tuple(plans), every),
         out_shape=tuple(shapes),
         in_specs=[vmem] * len(items),
         out_specs=tuple([vmem] * len(items)),
-        scratch_shapes=[pltpu.VMEM(x.shape, x.dtype) for x in shapes]
-        + [pltpu.SemaphoreType.DMA((x.shape[0],)) for x in shapes]
-        + [pltpu.SemaphoreType.DMA((x.shape[0],)) for x in shapes],
+        scratch_shapes=landings
+        + [pltpu.SemaphoreType.DMA((c,)) for c in counts]
+        + [pltpu.SemaphoreType.DMA((c,)) for c in counts]
+        + totals,
         compiler_params=pltpu.CompilerParams(collective_id=collective, has_side_effects=True),
         cost_estimate=pl.CostEstimate(flops=0, transcendentals=0, bytes_accessed=3 * total),
-    )(*[blocks for blocks, _, _ in items])
-
-
-def exchange(blocks, group, every, collective, broadcast=False):
-    return exchange_many([(blocks, group, broadcast)], every, collective)[0]
+    )(*[item[0] for item in items])
 
 
 def window_kernel(blk_sizes, rep_sizes, every, proj_ref, cot_ref, chosen_ref, sent_ref, out_ref, back_ref,
@@ -231,12 +247,15 @@
             chosen_move(t).wait_recv()
         part = jnp.dot(chosen_ref[t], p_got[t], preferred_element_type=jnp.float32)
         back = jnp.dot(ch_got[t], cot_got[t], preferred_element_type=jnp.float32)
-        if t == 0:
-            out_ref[...] = part
-            back_ref[...] = back
-        else:
-            out_ref[...] += part
-            back_ref[...] += back
+        width = out_ref.shape[-1]
+        for q in range(out_ref.shape[0]):
+            columns = slice(q * width, (q + 1) * width)
+            if t == 0:
+                out_ref[q] = part[:, columns]
+                back_ref[q] = back[:, columns]
+            else:
+                out_ref[q] += part[:, columns]
+                back_ref[q] += back[:, columns]
 
     @pl.when(r != 0)
     def _():
@@ -250,6 +269,7 @@
 
 
 def window(projected, cotangent, chosen, chosen_t, blk_sizes, rep_sizes, every, collective):
+    pieces = math.prod(rep_sizes)
     span = chosen.shape[0]
     rows, width = projected.shape
     vmem = pl.BlockSpec(memory_space=pltpu.VMEM)
@@ -257,8 +277,8 @@
     return pl.pallas_call(
         functools.partial(window_kernel, blk_sizes, rep_sizes, every),
         out_shape=(
-            jax.ShapeDtypeStruct((rows, width), jnp.float32),
-            jax.ShapeDtypeStruct((rows, width), jnp.float32),
+            jax.ShapeDtypeStruct((pieces, rows, width // pieces), jnp.float32),
+            jax.ShapeDtypeStruct((pieces, rows, width // pieces), jnp.float32),
         ),
         in_specs=[vmem, vmem, vmem, vmem],
         out_specs=(vmem, vmem),
@@ -305,19 +325,21 @@
         projected, cotangent, chosen, jnp.transpose(chosen, (0, 2, 1)), blk_sizes, rep_sizes, EVERY, 3
     )
 
-    rows = out_sum.shape[0]
-    both = jnp.stack([out_sum, back_sum]).reshape(2, rows, rep_count, cols_here)
-    summed = exchange(jnp.transpose(both, (2, 0, 1, 3)), REP, EVERY, 0).sum(0)
-    out_part = summed[0].astype(jnp.bfloat16)
-    back_grad = summed[1].astype(jnp.bfloat16)
+    rows = projected.shape[0]
+    out_part, back_grad = exchange_many(
+        [(out_sum, REP, "sum", jnp.bfloat16), (back_sum, REP, "sum", jnp.bfloat16)], EVERY, 0
+    )
     term = lax.dot_general(
         hidden_act, back_grad, (((0,), (0,)), ((), ())), preferred_element_type=jnp.float32
     )
-    weight_parts, gathered = exchange_many(
-        [(term.reshape(blk_count, -1, cols_here), BLK, False), (back_grad, REP, True)], EVERY, 1
-    )
-    grad_weight = weight_parts.sum(0)
-    back_full = jnp.transpose(gathered, (1, 0, 2)).reshape(rows, feature_width)
+    grad_weight, back_full = exchange_many(
+        [
+            (term.reshape(blk_count, -1, cols_here), BLK, "sum", jnp.float32),
+            (back_grad, REP, "concat", jnp.bfloat16),
+        ],
+        EVERY,
+        1,
+    )
     w_rows = lax.dynamic_slice_in_dim(w_out, rep_pos * cols_here, cols_here, 0)
     grad_in = lax.dot_general(
         back_full, w_rows, (((1,), (1,)), ((), ())), preferred_element_type=jnp.float32

time: 201 us -> 194 us (0.965)
  other arithmetic: 6.14 us -> 1.04 us
  local copies, waits for them, and re-layouts: 9.11 us -> 5.12 us
    reduce_sum x2 -> x0, other arithmetic: 2.99 us -> none  [the longest x1 1.71 us: shards(): grad_weight = weight_parts.sum(0)]
    pallas_call x2 -> x0, local copies, waits for them, and re-layouts: 2.46 us -> none  [window(): pl.pallas_call(functools.partial(window_kernel, blk_sizes, rep_sizes, eve...]
    transpose x1 -> x0, other arithmetic: 2.09 us -> none  [shards(): summed = exchange(jnp.transpose(both, (2, 0, 1, 3)), REP, EVERY, 0).sum(0)]
where the time goes in v6:
time: 194 us; the launch traced here: 192 us
  Pallas kernels  169 us (87%)
  between operations  11.1 us (6%)
  matrix products  5.72 us (3%)
  local copies, waits for them, and re-layouts  5.12 us (3%)
    pallas_call x2, Pallas kernels, exchange_many(): pl.pallas_call(functools.partial(exchange_kernel, tuple(plans), every), o...  99.6 us
    pallas_call x1, Pallas kernels, window(): pl.pallas_call(functools.partial(window_kernel, blk_sizes, rep_sizes, eve...  69.4 us

profile of v6, /device:TPU:6, one launch (start us, length us, event | category | flops | bytes accessed | tf_op | source)
XLA Modules:
  0.0 191.9 jit_solution(8184716318876849737)
XLA Ops:
  0.6 0.0 copy-start
  0.7 0.8 fusion.7
  1.5 0.6 fusion.13
  12.4 0.8 fusion.12
  13.2 0.1 copy.11
  13.3 0.1 copy.12
  13.7 0.0 copy-start.2
  13.7 0.8 copy.10.chosen_ref
  14.5 0.0 copy-done
  14.5 2.1 %convolution_convert_fusion.proj_ref = bf16[128,1024]{1,0:T(8,128)(2,1)} fusion(bf16[1024,1024]{1,0:T(8,128)(2,1)S(1)} %copy-done, bf16[128,1024]{1,0:T(8,128)(2,1)} %param.5), kind=kOutput, calls=%fused_computation | convolution fusion | flops 268697600 | bytes 2621440 | tf_op jit(solution)/shard_map/dot_general | solution.py:311
  16.6 0.0 copy-done.2
  16.6 0.0 copy-start.1
  16.6 69.4 %shard_map.76 = (f32[8,128,128]{2,1,0:T(8,128)}, f32[8,128,128]{2,1,0:T(8,128)}) custom-call(bf16[128,1024]{1,0:T(8,128)(2,1)} %convolution_convert_fusion.proj_ref, bf16[128,1024]{1,0:T(8,128)(2,1)} %cot_ref.1, bf16[8,128,128]{2,1,0:T(8,128)(2,1)} %copy.10.chosen_ref, bf16[8,128,128]{2,1,0:T(8,128)(2,1)} %bitcast.40), custom_call_target="tpu_custom_call" | custom-call | flops 536870912 | bytes 8912896 | tf_op jit(solution)/shard_map/pallas_call | solution.py:277
  86.1 56.7 %shard_map.77 = (bf16[128,128]{1,0:T(8,128)(2,1)}, bf16[128,128]{1,0:T(8,128)(2,1)}) custom-call(f32[8,128,128]{2,1,0:T(8,128)} %get-tuple-element.9.refs_0_, f32[8,128,128]{2,1,0:T(8,128)} %get-tuple-element.10.refs_1_), custom_call_target="tpu_custom_call" | custom-call | bytes 3145728 | tf_op jit(solution)/shard_map/pallas_call | solution.py:140
  142.8 0.0 copy-done.1
  142.8 1.8 fusion.2
  144.6 42.9 %shard_map.78 = (f32[16,128]{1,0:T(8,128)}, bf16[128,1024]{1,0:T(8,128)(2,1)}) custom-call(f32[64,16,128]{2,1,0:T(8,128)} %bitcast.39, bf16[128,128]{1,0:T(8,128)(2,1)} %get-tuple-element.12.refs_1_), custom_call_target="tpu_custom_call" | custom-call | bytes 2359296 | tf_op jit(solution)/shard_map/pallas_call | solution.py:140
  187.5 1.8 fusion
  189.3 1.4 copy.22
  190.6 1.3 copy.23
  (8 shorter events, 0.2 us)
Async XLA Ops:
  0.6 13.9 %copy-start = (bf16[1024,1024]{1,0:T(8,128)(2,1)S(1)}, bf16[1024,1024]{1,0:T(8,128)(2,1)}, u32[]{:S(2)}) copy-start(bf16[1024,1024]{1,0:T(8,128)(2,1)} %param.8) | copy-start | bytes 6291460
  13.7 3.0 %copy-start.2 = (bf16[8,128,128]{1,2,0:T(8,128)(2,1)}, bf16[8,128,128]{1,2,0:T(8,128)(2,1)S(1)}, u32[]{:S(2)}) copy-start(bf16[8,128,128]{1,2,0:T(8,128)(2,1)S(1)} %bitcast_dynamic-update-slice_fusion) | copy-start | bytes 786436
  16.6 126.1 %copy-start.1 = (bf16[128,1024]{1,0:T(8,128)(2,1)S(1)}, bf16[128,1024]{1,0:T(8,128)(2,1)}, u32[]{:S(2)}) copy-start(bf16[128,1024]{1,0:T(8,128)(2,1)} %param.5) | copy-start | bytes 786436

commit v7 on v6

--- a/solution.py
+++ b/solution.py
@@ -172,31 +172,40 @@
             rest = rest // s
         return tuple(reversed(coords)) + tuple(lax.axis_index(a) for a in rep_axes)
 
-    def remote(src, dst, kind, t, offset):
-        return pltpu.make_async_remote_copy(src, dst, send_sem.at[kind, t], recv_sem.at[kind, t],
+    def remote(src, dst, kind, h, t, offset):
+        return pltpu.make_async_remote_copy(src, dst, send_sem.at[kind, h, t], recv_sem.at[kind, h, t],
                                             device_id=target(offset), device_id_type=MESH_IDS)
 
-    def relay_moves():
+    half = proj_ref.shape[0] // 2
+
+    def rows(h):
+        return pl.ds(h * half, half)
+
+    def relay_moves(h):
+        moves = (
+            remote(proj_ref.at[rows(h)], p_got.at[0, rows(h)], 0, h, 0, far),
+            remote(cot_ref.at[rows(h)], cot_got.at[0, rows(h)], 1, h, 0, -far),
+        )
+        if h == 0:
+            moves += (remote(sent_ref.at[0], ch_got.at[0], 2, 0, 0, -far),)
+        return moves
+
+    def local_moves(h):
+        moves = (
+            pltpu.make_async_copy(proj_ref.at[rows(h)], p_got.at[0, rows(h)], local_sem.at[0, h]),
+            pltpu.make_async_copy(cot_ref.at[rows(h)], cot_got.at[0, rows(h)], local_sem.at[1, h]),
+        )
+        if h == 0:
+            moves += (pltpu.make_async_copy(sent_ref.at[0], ch_got.at[0], local_sem.at[2, 0]),)
+        return moves
+
+    def chosen_move(t):
+        return remote(sent_ref.at[t], ch_got.at[t], 2, 0, t, -far - t)
+
+    def forwards(t, h):
         return (
-            remote(proj_ref, p_got.at[0], 0, 0, far),
-            remote(cot_ref, cot_got.at[0], 1, 0, -far),
-            remote(sent_ref.at[0], ch_got.at[0], 2, 0, -far),
-        )
-
-    def local_moves():
-        return (
-            pltpu.make_async_copy(proj_ref, p_got.at[0], local_sem.at[0]),
-            pltpu.make_async_copy(cot_ref, cot_got.at[0], local_sem.at[1]),
-            pltpu.make_async_copy(sent_ref.at[0], ch_got.at[0], local_sem.at[2]),
-        )
-
-    def chosen_move(t):
-        return remote(sent_ref.at[t], ch_got.at[t], 2, t, -far - t)
-
-    def forwards(t):
-        return (
-            remote(p_got.at[0], p_got.at[t], 0, t, t),
-            remote(cot_got.at[0], cot_got.at[t], 1, t, -t),
+            remote(p_got.at[0, rows(h)], p_got.at[t, rows(h)], 0, h, t, t),
+            remote(cot_got.at[0, rows(h)], cot_got.at[t, rows(h)], 1, h, t, -t),
         )
 
     barrier = pltpu.get_barrier_semaphore()
@@ -214,36 +223,41 @@
         greet(far)
         greet(far)
         pl.semaphore_wait(barrier, 4 * span)
-        for c in relay_moves():
-            c.start()
+        for h in range(2):
+            for c in relay_moves(h):
+                c.start()
 
     @pl.when(r == 0)
     def _():
         pl.semaphore_wait(barrier, 4 * span - 4)
-        for c in local_moves():
-            c.start()
+        for h in range(2):
+            for c in local_moves(h):
+                c.start()
 
     for t in range(1, span):
         chosen_move(t).start()
 
-    @pl.when(r != 0)
-    def _():
-        for c in relay_moves():
-            c.wait_recv()
-
-    @pl.when(r == 0)
-    def _():
-        for c in local_moves():
-            c.wait()
-
-    for t in range(1, span):
-        for c in forwards(t):
-            c.start()
+    for h in range(2):
+
+        @pl.when(r != 0)
+        def _():
+            for c in relay_moves(h):
+                c.wait_recv()
+
+        @pl.when(r == 0)
+        def _():
+            for c in local_moves(h):
+                c.wait()
+
+        for t in range(1, span):
+            for c in forwards(t, h):
+                c.start()
 
     for t in range(span):
         if t > 0:
-            for c in forwards(t):
-                c.wait_recv()
+            for h in range(2):
+                for c in forwards(t, h):
+                    c.wait_recv()
             chosen_move(t).wait_recv()
         part = jnp.dot(chosen_ref[t], p_got[t], preferred_element_type=jnp.float32)
         back = jnp.dot(ch_got[t], cot_got[t], preferred_element_type=jnp.float32)
@@ -259,13 +273,15 @@
 
     @pl.when(r != 0)
     def _():
-        for c in relay_moves():
-            c.wait_send()
+        for h in range(2):
+            for c in relay_moves(h):
+                c.wait_send()
 
     for t in range(1, span):
         chosen_move(t).wait_send()
-        for c in forwards(t):
-            c.wait_send()
+        for h in range(2):
+            for c in forwards(t, h):
+                c.wait_send()
 
 
 def window(projected, cotangent, chosen, chosen_t, blk_sizes, rep_sizes, every, collective):
@@ -286,9 +302,9 @@
             pltpu.VMEM((span, rows, width), projected.dtype),
             pltpu.VMEM((span, rows, width), cotangent.dtype),
             pltpu.VMEM((span, rows, rows), chosen.dtype),
-            pltpu.SemaphoreType.DMA((3, span)),
-            pltpu.SemaphoreType.DMA((3, span)),
-            pltpu.SemaphoreType.DMA((3,)),
+            pltpu.SemaphoreType.DMA((3, 2, span)),
+            pltpu.SemaphoreType.DMA((3, 2, span)),
+            pltpu.SemaphoreType.DMA((3, 2)),
         ],
         compiler_params=pltpu.CompilerParams(collective_id=collective, has_side_effects=True),
         cost_estimate=pl.CostEstimate(

time: 194 us -> 173 us (0.89)
  Pallas kernels: 169 us -> 150 us
    pallas_call x2, Pallas kernels: 99.6 us -> 82.4 us  [exchange_many(): pl.pallas_call(functools.partial(exchange_kernel, tuple(plans), every), o...]
    pallas_call x1, Pallas kernels: 69.4 us -> 67.3 us  [window(): pl.pallas_call(functools.partial(window_kernel, blk_sizes, rep_sizes, eve...]
where the time goes in v7:
time: 173 us
  Pallas kernels  150 us (87%)
  between operations  11.1 us (6%)
  matrix products  5.72 us (3%)
  local copies, waits for them, and re-layouts  5.12 us (3%)
    pallas_call x2, Pallas kernels, exchange_many(): pl.pallas_call(functools.partial(exchange_kernel, tuple(plans), every), o...  82.4 us
    pallas_call x1, Pallas kernels, window(): pl.pallas_call(functools.partial(window_kernel, blk_sizes, rep_sizes, eve...  67.3 us

profile of v7, /device:TPU:6, one launch (start us, length us, event | category | flops | bytes accessed | tf_op | source)
XLA Modules:
  0.0 172.6 jit_solution(8732815219542758209)
XLA Ops:
  0.6 0.0 copy-start
  0.7 0.8 fusion.7
  1.5 0.6 fusion.13
  12.4 0.8 fusion.12
  13.2 0.1 copy.11
  13.3 0.1 copy.12
  13.7 0.0 copy-start.2
  13.7 0.8 copy.10.chosen_ref
  14.5 0.0 copy-done
  14.5 2.1 %convolution_convert_fusion.proj_ref = bf16[128,1024]{1,0:T(8,128)(2,1)} fusion(bf16[1024,1024]{1,0:T(8,128)(2,1)S(1)} %copy-done, bf16[128,1024]{1,0:T(8,128)(2,1)} %param.5), kind=kOutput, calls=%fused_computation | convolution fusion | flops 268697600 | bytes 2621440 | tf_op jit(solution)/shard_map/dot_general | solution.py:327
  16.6 0.0 copy-done.2
  16.6 0.0 copy-start.1
  16.6 67.3 %shard_map.76 = (f32[8,128,128]{2,1,0:T(8,128)}, f32[8,128,128]{2,1,0:T(8,128)}) custom-call(bf16[128,1024]{1,0:T(8,128)(2,1)} %convolution_convert_fusion.proj_ref, bf16[128,1024]{1,0:T(8,128)(2,1)} %cot_ref.1, bf16[8,128,128]{2,1,0:T(8,128)(2,1)} %copy.10.chosen_ref, bf16[8,128,128]{2,1,0:T(8,128)(2,1)} %bitcast.40), custom_call_target="tpu_custom_call" | custom-call | flops 536870912 | bytes 8912896 | tf_op jit(solution)/shard_map/pallas_call | solution.py:293
  83.9 52.6 %shard_map.77 = (bf16[128,128]{1,0:T(8,128)(2,1)}, bf16[128,128]{1,0:T(8,128)(2,1)}) custom-call(f32[8,128,128]{2,1,0:T(8,128)} %get-tuple-element.9.refs_0_, f32[8,128,128]{2,1,0:T(8,128)} %get-tuple-element.10.refs_1_), custom_call_target="tpu_custom_call" | custom-call | bytes 3145728 | tf_op jit(solution)/shard_map/pallas_call | solution.py:140
  136.5 0.0 copy-done.1
  136.5 1.8 %fusion.2 = f32[1024,128]{1,0:T(8,128)} fusion(bf16[128,128]{1,0:T(8,128)(2,1)} %get-tuple-element.12.refs_1_, bf16[128,1024]{1,0:T(8,128)(2,1)S(1)} %copy-done.1), kind=kOutput, calls=%fused_computation.4 | convolution fusion | flops 33685504 | bytes 819200 | tf_op jit(solution)/shard_map/dot_general | solution.py:348
  138.4 29.8 %shard_map.78 = (f32[16,128]{1,0:T(8,128)}, bf16[128,1024]{1,0:T(8,128)(2,1)}) custom-call(f32[64,16,128]{2,1,0:T(8,128)} %bitcast.39, bf16[128,128]{1,0:T(8,128)(2,1)} %get-tuple-element.12.refs_1_), custom_call_target="tpu_custom_call" | custom-call | bytes 2359296 | tf_op jit(solution)/shard_map/pallas_call | solution.py:140
  168.1 1.8 %fusion = bf16[128,128]{1,0:T(8,128)(2,1)} fusion(bf16[128,1024]{1,0:T(8,128)(2,1)} %get-tuple-element.14, bf16[1024,1024]{1,0:T(8,128)(2,1)S(1)} %copy-done, s32[]{:T(128)S(6)} %select_n.274, bf16[128,1024]{1,0:T(8,128)(2,1)S(1)} %copy-done.1), kind=kOutput, calls=%fused_computation.2 | convolution fusion | flops 33636352 | bytes 590848 | tf_op jit(solution)/shard_map/dot_general | solution.py:360
  169.9 1.4 copy.22
  171.3 1.3 copy.23
  (8 shorter events, 0.2 us)
Async XLA Ops:
  0.6 13.9 %copy-start = (bf16[1024,1024]{1,0:T(8,128)(2,1)S(1)}, bf16[1024,1024]{1,0:T(8,128)(2,1)}, u32[]{:S(2)}) copy-start(bf16[1024,1024]{1,0:T(8,128)(2,1)} %param.8) | copy-start | bytes 6291460
  13.7 3.0 %copy-start.2 = (bf16[8,128,128]{1,2,0:T(8,128)(2,1)}, bf16[8,128,128]{1,2,0:T(8,128)(2,1)S(1)}, u32[]{:S(2)}) copy-start(bf16[8,128,128]{1,2,0:T(8,128)(2,1)S(1)} %bitcast_dynamic-update-slice_fusion) | copy-start | bytes 786436
  16.6 119.9 %copy-start.1 = (bf16[128,1024]{1,0:T(8,128)(2,1)S(1)}, bf16[128,1024]{1,0:T(8,128)(2,1)}, u32[]{:S(2)}) copy-start(bf16[128,1024]{1,0:T(8,128)(2,1)} %param.5) | copy-start | bytes 786436

commit v8 on v7

--- a/solution.py
+++ b/solution.py
@@ -176,7 +176,8 @@
         return pltpu.make_async_remote_copy(src, dst, send_sem.at[kind, h, t], recv_sem.at[kind, h, t],
                                             device_id=target(offset), device_id_type=MESH_IDS)
 
-    half = proj_ref.shape[0] // 2
+    splits = 4
+    half = proj_ref.shape[0] // splits
 
     def rows(h):
         return pl.ds(h * half, half)
@@ -223,21 +224,21 @@
         greet(far)
         greet(far)
         pl.semaphore_wait(barrier, 4 * span)
-        for h in range(2):
+        for h in range(splits):
             for c in relay_moves(h):
                 c.start()
 
     @pl.when(r == 0)
     def _():
         pl.semaphore_wait(barrier, 4 * span - 4)
-        for h in range(2):
+        for h in range(splits):
             for c in local_moves(h):
                 c.start()
 
     for t in range(1, span):
         chosen_move(t).start()
 
-    for h in range(2):
+    for h in range(splits):
 
         @pl.when(r != 0)
         def _():
@@ -255,7 +256,7 @@
 
     for t in range(span):
         if t > 0:
-            for h in range(2):
+            for h in range(splits):
                 for c in forwards(t, h):
                     c.wait_recv()
             chosen_move(t).wait_recv()
@@ -273,13 +274,13 @@
 
     @pl.when(r != 0)
     def _():
-        for h in range(2):
+        for h in range(splits):
             for c in relay_moves(h):
                 c.wait_send()
 
     for t in range(1, span):
         chosen_move(t).wait_send()
-        for h in range(2):
+        for h in range(splits):
             for c in forwards(t, h):
                 c.wait_send()
 
@@ -302,9 +303,9 @@
             pltpu.VMEM((span, rows, width), projected.dtype),
             pltpu.VMEM((span, rows, width), cotangent.dtype),
             pltpu.VMEM((span, rows, rows), chosen.dtype),
-            pltpu.SemaphoreType.DMA((3, 2, span)),
-            pltpu.SemaphoreType.DMA((3, 2, span)),
-            pltpu.SemaphoreType.DMA((3, 2)),
+            pltpu.SemaphoreType.DMA((3, 4, span)),
+            pltpu.SemaphoreType.DMA((3, 4, span)),
+            pltpu.SemaphoreType.DMA((3, 4)),
         ],
         compiler_params=pltpu.CompilerParams(collective_id=collective, has_side_effects=True),
         cost_estimate=pl.CostEstimate(

time: 173 us -> 172 us (level)
  Pallas kernels: 150 us -> 147 us
    pallas_call x2, Pallas kernels: 82.4 us -> 76.8 us  [exchange_many(): pl.pallas_call(functools.partial(exchange_kernel, tuple(plans), every), o...]
    pallas_call x1, Pallas kernels: 67.3 us -> 70.6 us  [window(): pl.pallas_call(functools.partial(window_kernel, blk_sizes, rep_sizes, eve...]
where the time goes in v8:
time: 172 us; the launch traced here: 170 us
  Pallas kernels  147 us (85%)
  between operations  11.1 us (6%)
  matrix products  5.72 us (3%)
  local copies, waits for them, and re-layouts  5.12 us (3%)
    pallas_call x2, Pallas kernels, exchange_many(): pl.pallas_call(functools.partial(exchange_kernel, tuple(plans), every), o...  76.8 us
    pallas_call x1, Pallas kernels, window(): pl.pallas_call(functools.partial(window_kernel, blk_sizes, rep_sizes, eve...  70.6 us

profile of v8, /device:TPU:6, one launch (start us, length us, event | category | flops | bytes accessed | tf_op | source)
XLA Modules:
  0.0 170.3 jit_solution(12253791371611125843)
XLA Ops:
  0.6 0.0 copy-start
  0.7 0.8 fusion.7
  1.5 0.6 fusion.13
  12.4 0.8 fusion.12
  13.2 0.1 copy.11
  13.3 0.1 copy.12
  13.7 0.0 copy-start.2
  13.7 0.8 copy.10.chosen_ref
  14.5 0.0 copy-done
  14.5 2.1 %convolution_convert_fusion.proj_ref = bf16[128,1024]{1,0:T(8,128)(2,1)} fusion(bf16[1024,1024]{1,0:T(8,128)(2,1)S(1)} %copy-done, bf16[128,1024]{1,0:T(8,128)(2,1)} %param.5), kind=kOutput, calls=%fused_computation | convolution fusion | flops 268697600 | bytes 2621440 | tf_op jit(solution)/shard_map/dot_general | solution.py:328
  16.6 0.0 copy-done.2
  16.6 0.0 copy-start.1
  16.6 70.6 %shard_map.76 = (f32[8,128,128]{2,1,0:T(8,128)}, f32[8,128,128]{2,1,0:T(8,128)}) custom-call(bf16[128,1024]{1,0:T(8,128)(2,1)} %convolution_convert_fusion.proj_ref, bf16[128,1024]{1,0:T(8,128)(2,1)} %cot_ref.1, bf16[8,128,128]{2,1,0:T(8,128)(2,1)} %copy.10.chosen_ref, bf16[8,128,128]{2,1,0:T(8,128)(2,1)} %bitcast.40), custom_call_target="tpu_custom_call" | custom-call | flops 536870912 | bytes 8912896 | tf_op jit(solution)/shard_map/pallas_call | solution.py:294
  87.2 49.6 %shard_map.77 = (bf16[128,128]{1,0:T(8,128)(2,1)}, bf16[128,128]{1,0:T(8,128)(2,1)}) custom-call(f32[8,128,128]{2,1,0:T(8,128)} %get-tuple-element.9.refs_0_, f32[8,128,128]{2,1,0:T(8,128)} %get-tuple-element.10.refs_1_), custom_call_target="tpu_custom_call" | custom-call | bytes 3145728 | tf_op jit(solution)/shard_map/pallas_call | solution.py:140
  136.9 0.0 copy-done.1
  136.9 1.8 %fusion.2 = f32[1024,128]{1,0:T(8,128)} fusion(bf16[128,128]{1,0:T(8,128)(2,1)} %get-tuple-element.12.refs_1_, bf16[128,1024]{1,0:T(8,128)(2,1)S(1)} %copy-done.1), kind=kOutput, calls=%fused_computation.4 | convolution fusion | flops 33685504 | bytes 819200 | tf_op jit(solution)/shard_map/dot_general | solution.py:349
  138.7 27.2 %shard_map.78 = (f32[16,128]{1,0:T(8,128)}, bf16[128,1024]{1,0:T(8,128)(2,1)}) custom-call(f32[64,16,128]{2,1,0:T(8,128)} %bitcast.39, bf16[128,128]{1,0:T(8,128)(2,1)} %get-tuple-element.12.refs_1_), custom_call_target="tpu_custom_call" | custom-call | bytes 2359296 | tf_op jit(solution)/shard_map/pallas_call | solution.py:140
  165.9 1.8 %fusion = bf16[128,128]{1,0:T(8,128)(2,1)} fusion(bf16[128,1024]{1,0:T(8,128)(2,1)} %get-tuple-element.14, bf16[1024,1024]{1,0:T(8,128)(2,1)S(1)} %copy-done, s32[]{:T(128)S(6)} %select_n.274, bf16[128,1024]{1,0:T(8,128)(2,1)S(1)} %copy-done.1), kind=kOutput, calls=%fused_computation.2 | convolution fusion | flops 33636352 | bytes 590848 | tf_op jit(solution)/shard_map/dot_general | solution.py:361
  167.7 1.4 copy.22
  169.0 1.3 copy.23
  (8 shorter events, 0.2 us)
Async XLA Ops:
  0.6 13.9 %copy-start = (bf16[1024,1024]{1,0:T(8,128)(2,1)S(1)}, bf16[1024,1024]{1,0:T(8,128)(2,1)}, u32[]{:S(2)}) copy-start(bf16[1024,1024]{1,0:T(8,128)(2,1)} %param.8) | copy-start | bytes 6291460
  13.7 3.0 %copy-start.2 = (bf16[8,128,128]{1,2,0:T(8,128)(2,1)}, bf16[8,128,128]{1,2,0:T(8,128)(2,1)S(1)}, u32[]{:S(2)}) copy-start(bf16[8,128,128]{1,2,0:T(8,128)(2,1)S(1)} %bitcast_dynamic-update-slice_fusion) | copy-start | bytes 786436
  16.6 120.2 %copy-start.1 = (bf16[128,1024]{1,0:T(8,128)(2,1)S(1)}, bf16[128,1024]{1,0:T(8,128)(2,1)}, u32[]{:S(2)}) copy-start(bf16[128,1024]{1,0:T(8,128)(2,1)} %param.5) | copy-start | bytes 786436

commit v9 on v8

--- a/solution.py
+++ b/solution.py
@@ -152,7 +152,7 @@
 
 
 def window_kernel(blk_sizes, rep_sizes, every, proj_ref, cot_ref, chosen_ref, sent_ref, out_ref, back_ref,
-                  p_got, cot_got, ch_got, send_sem, recv_sem, local_sem):
+                  p_got, cot_got, ch_got, send_sem, recv_sem, local_sem, acc):
     blk_count = math.prod(blk_sizes)
     span = chosen_ref.shape[0]
     blk_axes, rep_axes = every[: len(blk_sizes)], every[len(blk_sizes) :]
@@ -262,15 +262,18 @@
             chosen_move(t).wait_recv()
         part = jnp.dot(chosen_ref[t], p_got[t], preferred_element_type=jnp.float32)
         back = jnp.dot(ch_got[t], cot_got[t], preferred_element_type=jnp.float32)
-        width = out_ref.shape[-1]
-        for q in range(out_ref.shape[0]):
-            columns = slice(q * width, (q + 1) * width)
-            if t == 0:
-                out_ref[q] = part[:, columns]
-                back_ref[q] = back[:, columns]
-            else:
-                out_ref[q] += part[:, columns]
-                back_ref[q] += back[:, columns]
+        if t == 0:
+            acc[0] = part
+            acc[1] = back
+        else:
+            acc[0] += part
+            acc[1] += back
+
+    width = out_ref.shape[-1]
+    for q in range(out_ref.shape[0]):
+        columns = pl.ds(q * width, width)
+        out_ref[q] = acc[0, :, columns].astype(out_ref.dtype)
+        back_ref[q] = acc[1, :, columns].astype(back_ref.dtype)
 
     @pl.when(r != 0)
     def _():
@@ -294,8 +297,8 @@
     return pl.pallas_call(
         functools.partial(window_kernel, blk_sizes, rep_sizes, every),
         out_shape=(
-            jax.ShapeDtypeStruct((pieces, rows, width // pieces), jnp.float32),
-            jax.ShapeDtypeStruct((pieces, rows, width // pieces), jnp.float32),
+            jax.ShapeDtypeStruct((pieces, rows, width // pieces), jnp.bfloat16),
+            jax.ShapeDtypeStruct((pieces, rows, width // pieces), jnp.bfloat16),
         ),
         in_specs=[vmem, vmem, vmem, vmem],
         out_specs=(vmem, vmem),
@@ -306,6 +309,7 @@
             pltpu.SemaphoreType.DMA((3, 4, span)),
             pltpu.SemaphoreType.DMA((3, 4, span)),
             pltpu.SemaphoreType.DMA((3, 4)),
+            pltpu.VMEM((2, rows, width), jnp.float32),
         ],
         compiler_params=pltpu.CompilerParams(collective_id=collective, has_side_effects=True),
         cost_estimate=pl.CostEstimate(

time: 172 us -> 160 us (0.930)
  Pallas kernels: 147 us -> 136 us
    pallas_call x2, Pallas kernels: 76.8 us -> 66 us  [exchange_many(): pl.pallas_call(functools.partial(exchange_kernel, tuple(plans), every), o...]
where the time goes in v9:
time: 160 us; the launch traced here: 159 us
  Pallas kernels  136 us (85%)
  between operations  11.1 us (7%)
  matrix products  5.79 us (4%)
  local copies, waits for them, and re-layouts  5.12 us (3%)
    pallas_call x1, Pallas kernels, window(): pl.pallas_call(functools.partial(window_kernel, blk_sizes, rep_sizes, eve...  70.3 us
    pallas_call x2, Pallas kernels, exchange_many(): pl.pallas_call(functools.partial(exchange_kernel, tuple(plans), every), o...  66 us

profile of v9, /device:TPU:6, one launch (start us, length us, event | category | flops | bytes accessed | tf_op | source)
XLA Modules:
  0.0 159.4 jit_solution(6824550651510765906)
XLA Ops:
  0.6 0.0 copy-start
  0.7 0.8 fusion.7
  1.5 0.6 fusion.13
  12.4 0.8 fusion.12
  13.2 0.1 copy.11
  13.3 0.1 copy.12
  13.7 0.0 copy-start.2
  13.7 0.8 copy.10.chosen_ref
  14.5 0.0 copy-done
  14.5 0.0 copy-start.1
  14.5 2.2 %convolution_convert_fusion.proj_ref = bf16[128,1024]{1,0:T(8,128)(2,1)} fusion(bf16[1024,1024]{1,0:T(8,128)(2,1)S(1)} %copy-done, bf16[128,1024]{1,0:T(8,128)(2,1)} %param.5), kind=kOutput, calls=%fused_computation | convolution fusion | flops 268697600 | bytes 2621440 | tf_op jit(solution)/shard_map/dot_general | solution.py:332
  16.7 0.0 copy-done.2
  16.7 70.3 %shard_map.76 = (bf16[8,128,128]{2,1,0:T(8,128)(2,1)}, bf16[8,128,128]{2,1,0:T(8,128)(2,1)}) custom-call(bf16[128,1024]{1,0:T(8,128)(2,1)} %convolution_convert_fusion.proj_ref, bf16[128,1024]{1,0:T(8,128)(2,1)} %cot_ref.1, bf16[8,128,128]{2,1,0:T(8,128)(2,1)} %copy.10.chosen_ref, bf16[8,128,128]{2,1,0:T(8,128)(2,1)} %bitcast.40), custom_call_target="tpu_custom_call" | custom-call | flops 536870912 | bytes 8912896 | tf_op jit(solution)/shard_map/pallas_call | solution.py:297
  87.0 39.3 %shard_map.77 = (bf16[128,128]{1,0:T(8,128)(2,1)}, bf16[128,128]{1,0:T(8,128)(2,1)}) custom-call(bf16[8,128,128]{2,1,0:T(8,128)(2,1)} %get-tuple-element.9.refs_0_, bf16[8,128,128]{2,1,0:T(8,128)(2,1)} %get-tuple-element.10.refs_1_), custom_call_target="tpu_custom_call" | custom-call | bytes 1572864 | tf_op jit(solution)/shard_map/pallas_call | solution.py:140
  126.3 0.0 copy-done.1
  126.3 1.8 %fusion.2 = f32[1024,128]{1,0:T(8,128)} fusion(bf16[128,128]{1,0:T(8,128)(2,1)} %get-tuple-element.12.refs_1_, bf16[128,1024]{1,0:T(8,128)(2,1)S(1)} %copy-done.1), kind=kOutput, calls=%fused_computation.4 | convolution fusion | flops 33685504 | bytes 819200 | tf_op jit(solution)/shard_map/dot_general | solution.py:353
  128.1 26.7 %shard_map.78 = (f32[16,128]{1,0:T(8,128)}, bf16[128,1024]{1,0:T(8,128)(2,1)}) custom-call(f32[64,16,128]{2,1,0:T(8,128)} %bitcast.39, bf16[128,128]{1,0:T(8,128)(2,1)} %get-tuple-element.12.refs_1_), custom_call_target="tpu_custom_call" | custom-call | bytes 2359296 | tf_op jit(solution)/shard_map/pallas_call | solution.py:140
  154.9 1.8 %fusion = bf16[128,128]{1,0:T(8,128)(2,1)} fusion(bf16[128,1024]{1,0:T(8,128)(2,1)} %get-tuple-element.14, bf16[1024,1024]{1,0:T(8,128)(2,1)S(1)} %copy-done, s32[]{:T(128)S(6)} %select_n.274, bf16[128,1024]{1,0:T(8,128)(2,1)S(1)} %copy-done.1), kind=kOutput, calls=%fused_computation.2 | convolution fusion | flops 33636352 | bytes 590848 | tf_op jit(solution)/shard_map/dot_general | solution.py:365
  156.7 1.4 copy.22
  158.1 1.3 copy.23
  (8 shorter events, 0.2 us)
Async XLA Ops:
  0.6 13.9 %copy-start = (bf16[1024,1024]{1,0:T(8,128)(2,1)S(1)}, bf16[1024,1024]{1,0:T(8,128)(2,1)}, u32[]{:S(2)}) copy-start(bf16[1024,1024]{1,0:T(8,128)(2,1)} %param.8) | copy-start | bytes 6291460
  13.7 3.0 %copy-start.2 = (bf16[8,128,128]{1,2,0:T(8,128)(2,1)}, bf16[8,128,128]{1,2,0:T(8,128)(2,1)S(1)}, u32[]{:S(2)}) copy-start(bf16[8,128,128]{1,2,0:T(8,128)(2,1)S(1)} %bitcast_dynamic-update-slice_fusion) | copy-start | bytes 786436
  14.5 111.8 %copy-start.1 = (bf16[128,1024]{1,0:T(8,128)(2,1)S(1)}, bf16[128,1024]{1,0:T(8,128)(2,1)}, u32[]{:S(2)}) copy-start(bf16[128,1024]{1,0:T(8,128)(2,1)} %param.5) | copy-start | bytes 786436

commit v10 on v9

--- a/solution.py
+++ b/solution.py
@@ -334,16 +334,13 @@
     own_cols = adj_cols[0]
     section = jnp.mod(blk_pos - own_cols, blk_count) - rep_pos * span
 
-    chosen = jnp.stack(
-        [
-            sum(jnp.where(section[k] == turn, own_vals[k], 0) for k in range(slots))
-            for turn in range(span)
-        ]
-    )
+    picks = (section[None, :] == jnp.arange(span, dtype=section.dtype)[:, None]).astype(own_vals.dtype)
+    chosen = jnp.einsum("tk,kab->tab", picks, own_vals, preferred_element_type=jnp.float32).astype(own_vals.dtype)
+    chosen_t = jnp.einsum("tk,kab->tba", picks, own_vals, preferred_element_type=jnp.float32).astype(own_vals.dtype)
     blk_sizes = tuple(lax.axis_size(a) for a in BLK)
     rep_sizes = tuple(lax.axis_size(a) for a in REP)
     out_sum, back_sum = window(
-        projected, cotangent, chosen, jnp.transpose(chosen, (0, 2, 1)), blk_sizes, rep_sizes, EVERY, 3
+        projected, cotangent, chosen, chosen_t, blk_sizes, rep_sizes, EVERY, 3
     )
 
     rows = projected.shape[0]

time: 160 us -> 149 us (0.931)
  between operations: 11.1 us -> 0.71 us
where the time goes in v10:
time: 149 us; the launch traced here: 148 us
  Pallas kernels  136 us (91%)
  matrix products  6.94 us (5%)
  local copies, waits for them, and re-layouts  3.76 us (3%)
    pallas_call x1, Pallas kernels, window(): pl.pallas_call(functools.partial(window_kernel, blk_sizes, rep_sizes, eve...  70.4 us
    pallas_call x2, Pallas kernels, exchange_many(): pl.pallas_call(functools.partial(exchange_kernel, tuple(plans), every), o...  65.8 us

profile of v10, /device:TPU:6, one launch (start us, length us, event | category | flops | bytes accessed | tf_op | source)
XLA Modules:
  0.0 148.5 jit_solution(13382569808140813746)
XLA Ops:
  0.6 0.0 copy-start
  0.7 0.8 fusion.13
  1.5 1.2 fusion.7
  2.6 0.2 copy.9
  2.9 0.0 copy-start.2
  2.9 0.9 copy.10.chosen_ref
  3.7 0.0 copy-done
  3.7 0.0 copy-start.1
  3.7 2.2 %convolution_convert_fusion.proj_ref = bf16[128,1024]{1,0:T(8,128)(2,1)} fusion(bf16[1024,1024]{1,0:T(8,128)(2,1)S(1)} %copy-done, bf16[128,1024]{1,0:T(8,128)(2,1)} %param.5), kind=kOutput, calls=%fused_computation | convolution fusion | flops 268697600 | bytes 2621440 | tf_op jit(solution)/shard_map/dot_general | solution.py:332
  5.9 0.0 copy-done.2
  5.9 70.4 %shard_map.76 = (bf16[8,128,128]{2,1,0:T(8,128)(2,1)}, bf16[8,128,128]{2,1,0:T(8,128)(2,1)}) custom-call(bf16[128,1024]{1,0:T(8,128)(2,1)} %convolution_convert_fusion.proj_ref, bf16[128,1024]{1,0:T(8,128)(2,1)} %cot_ref.1, bf16[8,128,128]{2,1,0:T(8,128)(2,1)} %copy.10.chosen_ref, bf16[8,128,128]{2,1,0:T(8,128)(2,1)} %bitcast.12), custom_call_target="tpu_custom_call" | custom-call | flops 536870912 | bytes 8912896 | tf_op jit(solution)/shard_map/pallas_call | solution.py:297
  76.3 39.1 %shard_map.77 = (bf16[128,128]{1,0:T(8,128)(2,1)}, bf16[128,128]{1,0:T(8,128)(2,1)}) custom-call(bf16[8,128,128]{2,1,0:T(8,128)(2,1)} %get-tuple-element.9.refs_0_, bf16[8,128,128]{2,1,0:T(8,128)(2,1)} %get-tuple-element.10.refs_1_), custom_call_target="tpu_custom_call" | custom-call | bytes 1572864 | tf_op jit(solution)/shard_map/pallas_call | solution.py:140
  115.4 0.0 copy-done.1
  115.4 1.8 %fusion.2 = f32[1024,128]{1,0:T(8,128)} fusion(bf16[128,128]{1,0:T(8,128)(2,1)} %get-tuple-element.12.refs_1_, bf16[128,1024]{1,0:T(8,128)(2,1)S(1)} %copy-done.1), kind=kOutput, calls=%fused_computation.4 | convolution fusion | flops 33685504 | bytes 819200 | tf_op jit(solution)/shard_map/dot_general | solution.py:350
  117.2 26.8 %shard_map.78 = (f32[16,128]{1,0:T(8,128)}, bf16[128,1024]{1,0:T(8,128)(2,1)}) custom-call(f32[64,16,128]{2,1,0:T(8,128)} %bitcast.11, bf16[128,128]{1,0:T(8,128)(2,1)} %get-tuple-element.12.refs_1_), custom_call_target="tpu_custom_call" | custom-call | bytes 2359296 | tf_op jit(solution)/shard_map/pallas_call | solution.py:140
  144.0 1.8 %fusion = bf16[128,128]{1,0:T(8,128)(2,1)} fusion(bf16[128,1024]{1,0:T(8,128)(2,1)} %get-tuple-element.14, bf16[1024,1024]{1,0:T(8,128)(2,1)S(1)} %copy-done, s32[]{:T(128)S(6)} %select_n.17, bf16[128,1024]{1,0:T(8,128)(2,1)S(1)} %copy-done.1), kind=kOutput, calls=%fused_computation.2 | convolution fusion | flops 33636352 | bytes 590848 | tf_op jit(solution)/shard_map/dot_general | solution.py:362
  145.8 1.4 copy.15
  147.2 1.3 copy.16
Async XLA Ops:
  0.6 3.1 %copy-start = (bf16[1024,1024]{1,0:T(8,128)(2,1)S(1)}, bf16[1024,1024]{1,0:T(8,128)(2,1)}, u32[]{:S(2)}) copy-start(bf16[1024,1024]{1,0:T(8,128)(2,1)} %param.8) | copy-start | bytes 6291460
  2.9 3.0 %copy-start.2 = (bf16[8,128,128]{1,2,0:T(8,128)(2,1)}, bf16[8,128,128]{1,2,0:T(8,128)(2,1)S(1)}, u32[]{:S(2)}) copy-start(bf16[8,128,128]{1,2,0:T(8,128)(2,1)S(1)} %copy.9) | copy-start | bytes 786436
  3.7 111.7 %copy-start.1 = (bf16[128,1024]{1,0:T(8,128)(2,1)S(1)}, bf16[128,1024]{1,0:T(8,128)(2,1)}, u32[]{:S(2)}) copy-start(bf16[128,1024]{1,0:T(8,128)(2,1)} %param.5) | copy-start | bytes 786436

commit v11 on v10

--- a/solution.py
+++ b/solution.py
@@ -176,7 +176,7 @@
         return pltpu.make_async_remote_copy(src, dst, send_sem.at[kind, h, t], recv_sem.at[kind, h, t],
                                             device_id=target(offset), device_id_type=MESH_IDS)
 
-    splits = 4
+    splits = 8
     half = proj_ref.shape[0] // splits
 
     def rows(h):
@@ -306,9 +306,9 @@
             pltpu.VMEM((span, rows, width), projected.dtype),
             pltpu.VMEM((span, rows, width), cotangent.dtype),
             pltpu.VMEM((span, rows, rows), chosen.dtype),
-            pltpu.SemaphoreType.DMA((3, 4, span)),
-            pltpu.SemaphoreType.DMA((3, 4, span)),
-            pltpu.SemaphoreType.DMA((3, 4)),
+            pltpu.SemaphoreType.DMA((3, 8, span)),
+            pltpu.SemaphoreType.DMA((3, 8, span)),
+            pltpu.SemaphoreType.DMA((3, 8)),
             pltpu.VMEM((2, rows, width), jnp.float32),
         ],
         compiler_params=pltpu.CompilerParams(collective_id=collective, has_side_effects=True),

time: 149 us -> 150 us (level)
    pallas_call x2, Pallas kernels: 65.8 us -> 70 us  [exchange_many(): pl.pallas_call(functools.partial(exchange_kernel, tuple(plans), every), o...]
    pallas_call x1, Pallas kernels: 70.4 us -> 67.3 us  [window(): pl.pallas_call(functools.partial(window_kernel, blk_sizes, rep_sizes, eve...]
where the time goes in v11:
time: 150 us
  Pallas kernels  137 us (91%)
  matrix products  6.94 us (5%)
  local copies, waits for them, and re-layouts  3.76 us (3%)
    pallas_call x2, Pallas kernels, exchange_many(): pl.pallas_call(functools.partial(exchange_kernel, tuple(plans), every), o...  70 us
    pallas_call x1, Pallas kernels, window(): pl.pallas_call(functools.partial(window_kernel, blk_sizes, rep_sizes, eve...  67.3 us

profile of v11, /device:TPU:6, one launch (start us, length us, event | category | flops | bytes accessed | tf_op | source)
XLA Modules:
  0.0 149.5 jit_solution(12980458556368754651)
XLA Ops:
  0.6 0.0 copy-start
  0.7 0.8 fusion.13
  1.5 1.2 fusion.7
  2.6 0.2 copy.9
  2.9 0.0 copy-start.2
  2.9 0.9 copy.10.chosen_ref
  3.7 0.0 copy-done
  3.7 0.0 copy-start.1
  3.7 2.2 %convolution_convert_fusion.proj_ref = bf16[128,1024]{1,0:T(8,128)(2,1)} fusion(bf16[1024,1024]{1,0:T(8,128)(2,1)S(1)} %copy-done, bf16[128,1024]{1,0:T(8,128)(2,1)} %param.5), kind=kOutput, calls=%fused_computation | convolution fusion | flops 268697600 | bytes 2621440 | tf_op jit(solution)/shard_map/dot_general | solution.py:332
  5.9 0.0 copy-done.2
  5.9 67.3 %shard_map.76 = (bf16[8,128,128]{2,1,0:T(8,128)(2,1)}, bf16[8,128,128]{2,1,0:T(8,128)(2,1)}) custom-call(bf16[128,1024]{1,0:T(8,128)(2,1)} %convolution_convert_fusion.proj_ref, bf16[128,1024]{1,0:T(8,128)(2,1)} %cot_ref.1, bf16[8,128,128]{2,1,0:T(8,128)(2,1)} %copy.10.chosen_ref, bf16[8,128,128]{2,1,0:T(8,128)(2,1)} %bitcast.12), custom_call_target="tpu_custom_call" | custom-call | flops 536870912 | bytes 8912896 | tf_op jit(solution)/shard_map/pallas_call | solution.py:297
  73.2 42.5 %shard_map.77 = (bf16[128,128]{1,0:T(8,128)(2,1)}, bf16[128,128]{1,0:T(8,128)(2,1)}) custom-call(bf16[8,128,128]{2,1,0:T(8,128)(2,1)} %get-tuple-element.9.refs_0_, bf16[8,128,128]{2,1,0:T(8,128)(2,1)} %get-tuple-element.10.refs_1_), custom_call_target="tpu_custom_call" | custom-call | bytes 1572864 | tf_op jit(solution)/shard_map/pallas_call | solution.py:140
  115.7 0.0 copy-done.1
  115.8 1.8 %fusion.2 = f32[1024,128]{1,0:T(8,128)} fusion(bf16[128,128]{1,0:T(8,128)(2,1)} %get-tuple-element.12.refs_1_, bf16[128,1024]{1,0:T(8,128)(2,1)S(1)} %copy-done.1), kind=kOutput, calls=%fused_computation.4 | convolution fusion | flops 33685504 | bytes 819200 | tf_op jit(solution)/shard_map/dot_general | solution.py:350
  117.6 27.5 %shard_map.78 = (f32[16,128]{1,0:T(8,128)}, bf16[128,1024]{1,0:T(8,128)(2,1)}) custom-call(f32[64,16,128]{2,1,0:T(8,128)} %bitcast.11, bf16[128,128]{1,0:T(8,128)(2,1)} %get-tuple-element.12.refs_1_), custom_call_target="tpu_custom_call" | custom-call | bytes 2359296 | tf_op jit(solution)/shard_map/pallas_call | solution.py:140
  145.0 1.8 %fusion = bf16[128,128]{1,0:T(8,128)(2,1)} fusion(bf16[128,1024]{1,0:T(8,128)(2,1)} %get-tuple-element.14, bf16[1024,1024]{1,0:T(8,128)(2,1)S(1)} %copy-done, s32[]{:T(128)S(6)} %select_n.17, bf16[128,1024]{1,0:T(8,128)(2,1)S(1)} %copy-done.1), kind=kOutput, calls=%fused_computation.2 | convolution fusion | flops 33636352 | bytes 590848 | tf_op jit(solution)/shard_map/dot_general | solution.py:362
  146.9 1.4 copy.15
  148.2 1.3 copy.16
Async XLA Ops:
  0.6 3.1 %copy-start = (bf16[1024,1024]{1,0:T(8,128)(2,1)S(1)}, bf16[1024,1024]{1,0:T(8,128)(2,1)}, u32[]{:S(2)}) copy-start(bf16[1024,1024]{1,0:T(8,128)(2,1)} %param.8) | copy-start | bytes 6291460
  2.9 3.0 %copy-start.2 = (bf16[8,128,128]{1,2,0:T(8,128)(2,1)}, bf16[8,128,128]{1,2,0:T(8,128)(2,1)S(1)}, u32[]{:S(2)}) copy-start(bf16[8,128,128]{1,2,0:T(8,128)(2,1)S(1)} %copy.9) | copy-start | bytes 786436
  3.7 112.0 %copy-start.1 = (bf16[128,1024]{1,0:T(8,128)(2,1)S(1)}, bf16[128,1024]{1,0:T(8,128)(2,1)}, u32[]{:S(2)}) copy-start(bf16[128,1024]{1,0:T(8,128)(2,1)} %param.5) | copy-start | bytes 786436

commit v12 on v10

--- a/solution.py
+++ b/solution.py
@@ -318,6 +318,126 @@
     )(projected, cotangent, chosen, chosen_t)
 
 
+def tail_kernel(rep_sizes, blk_sizes, every, out_c, back_c, act_t, out_ref, weight_ref, full_ref,
+                land_o, land_b, land_w, land_g, bg_s, term_s, tot_o, tot_b, tot_w, sends, recvs):
+    rep_axes, blk_axes = every[len(blk_sizes) :], every[: len(blk_sizes)]
+    groups = {"rep": (rep_axes, rep_sizes), "blk": (blk_axes, blk_sizes)}
+    barrier = pltpu.get_barrier_semaphore()
+
+    def position(name):
+        axes, sizes = groups[name]
+        me = 0
+        for a, s in zip(axes, sizes):
+            me = me * s + lax.axis_index(a)
+        return me
+
+    def target(name, d):
+        axes, sizes = groups[name]
+        coords = {}
+        rest = d
+        for a, s in reversed(list(zip(axes, sizes))):
+            coords[a] = rest % s
+            rest = rest // s
+        return tuple(coords[a] if a in coords else lax.axis_index(a) for a in every)
+
+    def count(name):
+        return math.prod(groups[name][1])
+
+    for name in ("rep", "blk"):
+        me, n = position(name), count(name)
+
+        def greet(o, carry, name=name, me=me, n=n):
+            pl.semaphore_signal(barrier, inc=1, device_id=target(name, (me + o) % n), device_id_type=MESH_IDS)
+            return carry
+
+        lax.fori_loop(1, n, greet, 0)
+    pl.semaphore_wait(barrier, count("rep") + count("blk") - 2)
+
+    def run(plans):
+        for k, name, source, land, total, out in plans:
+            me, n = position(name), count(name)
+
+            def send(o, carry, k=k, name=name, source=source, land=land, me=me, n=n):
+                d = (me + o) % n
+                pltpu.make_async_remote_copy(source(d), land.at[me], sends.at[k, o], recvs.at[k, me],
+                                             device_id=target(name, d), device_id_type=MESH_IDS).start()
+                return carry
+
+            lax.fori_loop(1, n, send, 0)
+            if total is not None:
+                total[...] = source(me)[...].astype(jnp.float32)
+            else:
+                width = land.shape[-1]
+                out[:, pl.ds(pl.multiple_of(me * width, width), width)] = source(me)[...]
+        for k, name, source, land, total, out in plans:
+            me, n = position(name), count(name)
+
+            def finish(o, carry, k=k, name=name, source=source, land=land, total=total, out=out, me=me, n=n):
+                d = (me + o) % n
+                pltpu.make_async_remote_copy(source(d), land.at[me], sends.at[k, o], recvs.at[k, me],
+                                             device_id=target(name, d), device_id_type=MESH_IDS).wait_send()
+                sender = (me + n - o) % n
+                pltpu.make_async_remote_copy(source(sender), land.at[sender], sends.at[k, o], recvs.at[k, sender],
+                                             device_id=target(name, sender), device_id_type=MESH_IDS).wait_recv()
+                if total is not None:
+                    total[...] += land[sender].astype(jnp.float32)
+                else:
+                    width = land.shape[-1]
+                    out[:, pl.ds(pl.multiple_of(sender * width, width), width)] = land[sender]
+                return carry
+
+            lax.fori_loop(1, n, finish, 0)
+
+    run([
+        (0, "rep", lambda d: out_c.at[d], land_o, tot_o, None),
+        (1, "rep", lambda d: back_c.at[d], land_b, tot_b, None),
+    ])
+    out_ref[...] = tot_o[...].astype(out_ref.dtype)
+    bg_s[...] = tot_b[...].astype(bg_s.dtype)
+    term = jnp.dot(act_t[...], bg_s[...], preferred_element_type=jnp.float32)
+    term_s[...] = term.reshape(term_s.shape)
+    run([
+        (2, "blk", lambda d: term_s.at[d], land_w, tot_w, None),
+        (3, "rep", lambda d: bg_s, land_g, None, full_ref),
+    ])
+    weight_ref[...] = tot_w[...]
+
+
+def tail(out_c, back_c, act_t, blk_sizes, rep_sizes, every, collective):
+    reps, blks = math.prod(rep_sizes), math.prod(blk_sizes)
+    _, rows, cols = back_c.shape
+    vmem = pl.BlockSpec(memory_space=pltpu.VMEM)
+    most = max(reps, blks)
+    return pl.pallas_call(
+        functools.partial(tail_kernel, rep_sizes, blk_sizes, every),
+        out_shape=(
+            jax.ShapeDtypeStruct((rows, cols), jnp.bfloat16),
+            jax.ShapeDtypeStruct((act_t.shape[0] // blks, cols), jnp.float32),
+            jax.ShapeDtypeStruct((rows, cols * reps), jnp.bfloat16),
+        ),
+        in_specs=[vmem, vmem, vmem],
+        out_specs=(vmem, vmem, vmem),
+        scratch_shapes=[
+            pltpu.VMEM((reps, rows, cols), out_c.dtype),
+            pltpu.VMEM((reps, rows, cols), back_c.dtype),
+            pltpu.VMEM((blks, act_t.shape[0] // blks, cols), jnp.float32),
+            pltpu.VMEM((reps, rows, cols), jnp.bfloat16),
+            pltpu.VMEM((rows, cols), jnp.bfloat16),
+            pltpu.VMEM((blks, act_t.shape[0] // blks, cols), jnp.float32),
+            pltpu.VMEM((rows, cols), jnp.float32),
+            pltpu.VMEM((rows, cols), jnp.float32),
+            pltpu.VMEM((act_t.shape[0] // blks, cols), jnp.float32),
+            pltpu.SemaphoreType.DMA((4, most)),
+            pltpu.SemaphoreType.DMA((4, most)),
+        ],
+        compiler_params=pltpu.CompilerParams(collective_id=collective, has_side_effects=True),
+        cost_estimate=pl.CostEstimate(
+            flops=2 * act_t.shape[0] * rows * cols, transcendentals=0,
+            bytes_accessed=3 * (2 * reps * rows * cols * 2 + act_t.shape[0] * cols * 4 + reps * rows * cols * 2),
+        ),
+    )(out_c, back_c, act_t)
+
+
 def shards(hidden_pre, adj_vals, adj_cols, w_out, cotangent):
     row_count, feature_width = hidden_pre.shape
     blk_count = lax.axis_size(BLK)
@@ -344,19 +464,8 @@
     )
 
     rows = projected.shape[0]
-    out_part, back_grad = exchange_many(
-        [(out_sum, REP, "sum", jnp.bfloat16), (back_sum, REP, "sum", jnp.bfloat16)], EVERY, 0
-    )
-    term = lax.dot_general(
-        hidden_act, back_grad, (((0,), (0,)), ((), ())), preferred_element_type=jnp.float32
-    )
-    grad_weight, back_full = exchange_many(
-        [
-            (term.reshape(blk_count, -1, cols_here), BLK, "sum", jnp.float32),
-            (back_grad, REP, "concat", jnp.bfloat16),
-        ],
-        EVERY,
-        1,
+    out_part, grad_weight, back_full = tail(
+        out_sum, back_sum, jnp.transpose(hidden_act), blk_sizes, rep_sizes, EVERY, 0
     )
     w_rows = lax.dynamic_slice_in_dim(w_out, rep_pos * cols_here, cols_here, 0)
     grad_in = lax.dot_general(

time: 149 us -> 147 us (0.987)
  matrix products: 6.94 us -> 4.15 us
    dot_general x1 -> x0, matrix products: 1.8 us -> none  [shards(): lax.dot_general(hidden_act, back_grad, (((0,), (0,)), ((), ())), preferre...]
    unnamed x8 -> x7, local copies, waits for them, and re-layouts: 2.69 us -> 3.9 us
    pallas_call x2 -> x1, Pallas kernels: 65.8 us -> 64.8 us  [tail(): pl.pallas_call(functools.partial(tail_kernel, rep_sizes, blk_sizes, every...]
where the time goes in v12:
time: 147 us; the launch traced here: 146 us
  Pallas kernels  135 us (92%)
  local copies, waits for them, and re-layouts  4.99 us (3%)
  matrix products  4.15 us (3%)
  other arithmetic  1.53 us (1%)
    pallas_call x1, Pallas kernels, window(): pl.pallas_call(functools.partial(window_kernel, blk_sizes, rep_sizes, eve...  70.4 us
    pallas_call x1, Pallas kernels, tail(): pl.pallas_call(functools.partial(tail_kernel, rep_sizes, blk_sizes, every...  64.8 us
    unnamed x7, local copies, waits for them, and re-layouts  3.9 us

profile of v12, /device:TPU:6, one launch (start us, length us, event | category | flops | bytes accessed | tf_op | source)
XLA Modules:
  0.0 146.5 jit_solution(7487021075011380273)
XLA Ops:
  0.6 0.0 copy-start
  0.7 0.8 fusion.10
  1.5 1.2 fusion.4
  2.6 0.2 copy.10
  2.9 0.0 copy-start.1
  2.9 1.2 copy.8
  4.1 0.7 maximum_bitcast_fusion.act_t
  4.8 0.0 copy-done
  4.8 1.2 convolution_convert_fusion.proj_ref
  6.0 0.9 copy.11.chosen_ref
  6.9 0.0 copy-done.1
  6.9 70.4 %shard_map.76 = (bf16[8,128,128]{2,1,0:T(8,128)(2,1)}, bf16[8,128,128]{2,1,0:T(8,128)(2,1)}) custom-call(bf16[128,1024]{1,0:T(8,128)(2,1)} %convolution_convert_fusion.proj_ref, bf16[128,1024]{1,0:T(8,128)(2,1)} %cot_ref.1, bf16[8,128,128]{2,1,0:T(8,128)(2,1)} %copy.11.chosen_ref, bf16[8,128,128]{2,1,0:T(8,128)(2,1)} %bitcast.11), custom_call_target="tpu_custom_call" | custom-call | flops 536870912 | bytes 8912896 | tf_op jit(solution)/shard_map/pallas_call | solution.py:297
  77.2 64.8 %shard_map.77 = (bf16[128,128]{1,0:T(8,128)(2,1)}, f32[16,128]{1,0:T(8,128)}, bf16[128,1024]{1,0:T(8,128)(2,1)}) custom-call(bf16[8,128,128]{2,1,0:T(8,128)(2,1)} %get-tuple-element.8.out_c, bf16[8,128,128]{2,1,0:T(8,128)(2,1)} %get-tuple-element.9.back_c, bf16[1024,128]{1,0:T(8,128)(2,1)} %maximum_bitcast_fusion.act_t), custom_call_target="tpu_custom_call" | custom-call | flops 33554432 | bytes 3932160 | tf_op jit(solution)/shard_map/pallas_call | solution.py:411
  142.0 1.8 %fusion = bf16[128,128]{1,0:T(8,128)(2,1)} fusion(bf16[128,1024]{1,0:T(8,128)(2,1)} %get-tuple-element.12, bf16[1024,1024]{1,0:T(8,128)(2,1)S(1)} %copy-done, s32[]{:T(128)S(6)} %select_n.17, bf16[128,1024]{1,0:T(8,128)(2,1)} %param.5), kind=kOutput, calls=%fused_computation.2 | convolution fusion | flops 33636352 | bytes 590848 | tf_op jit(solution)/shard_map/dot_general | solution.py:471
  143.8 1.4 copy.16
  145.2 1.3 copy.17
Async XLA Ops:
  0.6 4.2 %copy-start = (bf16[1024,1024]{1,0:T(8,128)(2,1)S(1)}, bf16[1024,1024]{1,0:T(8,128)(2,1)}, u32[]{:S(2)}) copy-start(bf16[1024,1024]{1,0:T(8,128)(2,1)} %param.8) | copy-start | bytes 6291460
  2.9 4.0 %copy-start.1 = (bf16[8,128,128]{1,2,0:T(8,128)(2,1)}, bf16[8,128,128]{1,2,0:T(8,128)(2,1)S(1)}, u32[]{:S(2)}) copy-start(bf16[8,128,128]{1,2,0:T(8,128)(2,1)S(1)} %copy.10) | copy-start | bytes 786436

commit v13 on v12

--- a/solution.py
+++ b/solution.py
@@ -152,7 +152,7 @@
 
 
 def window_kernel(blk_sizes, rep_sizes, every, proj_ref, cot_ref, chosen_ref, sent_ref, out_ref, back_ref,
-                  p_got, cot_got, ch_got, send_sem, recv_sem, local_sem, acc):
+                  p_got, cot_got, ch_got, send_sem, recv_sem, local_sem, acc, greeted=False):
     blk_count = math.prod(blk_sizes)
     span = chosen_ref.shape[0]
     blk_axes, rep_axes = every[: len(blk_sizes)], every[len(blk_sizes) :]
@@ -215,22 +215,25 @@
         pl.semaphore_signal(barrier, inc=1, device_id=target(offset), device_id_type=MESH_IDS)
         pl.semaphore_signal(barrier, inc=1, device_id=target(-offset), device_id_type=MESH_IDS)
 
-    for t in range(1, span):
-        greet(far + t)
-        greet(t)
+    if not greeted:
+        for t in range(1, span):
+            greet(far + t)
+            greet(t)
 
     @pl.when(r != 0)
     def _():
-        greet(far)
-        greet(far)
-        pl.semaphore_wait(barrier, 4 * span)
+        if not greeted:
+            greet(far)
+            greet(far)
+            pl.semaphore_wait(barrier, 4 * span)
         for h in range(splits):
             for c in relay_moves(h):
                 c.start()
 
     @pl.when(r == 0)
     def _():
-        pl.semaphore_wait(barrier, 4 * span - 4)
+        if not greeted:
+            pl.semaphore_wait(barrier, 4 * span - 4)
         for h in range(splits):
             for c in local_moves(h):
                 c.start()
@@ -319,7 +322,7 @@
 
 
 def tail_kernel(rep_sizes, blk_sizes, every, out_c, back_c, act_t, out_ref, weight_ref, full_ref,
-                land_o, land_b, land_w, land_g, bg_s, term_s, tot_o, tot_b, tot_w, sends, recvs):
+                land_o, land_b, land_w, land_g, bg_s, term_s, tot_o, tot_b, tot_w, sends, recvs, greeted=False):
     rep_axes, blk_axes = every[len(blk_sizes) :], every[: len(blk_sizes)]
     groups = {"rep": (rep_axes, rep_sizes), "blk": (blk_axes, blk_sizes)}
     barrier = pltpu.get_barrier_semaphore()
@@ -343,7 +346,7 @@
     def count(name):
         return math.prod(groups[name][1])
 
-    for name in ("rep", "blk"):
+    for name in ("rep", "blk") if not greeted else ():
         me, n = position(name), count(name)
 
         def greet(o, carry, name=name, me=me, n=n):
@@ -351,7 +354,8 @@
             return carry
 
         lax.fori_loop(1, n, greet, 0)
-    pl.semaphore_wait(barrier, count("rep") + count("blk") - 2)
+    if not greeted:
+        pl.semaphore_wait(barrier, count("rep") + count("blk") - 2)
 
     def run(plans):
         for k, name, source, land, total, out in plans:
@@ -438,6 +442,81 @@
     )(out_c, back_c, act_t)
 
 
+def fused_kernel(blk_sizes, rep_sizes, every, proj_ref, cot_ref, chosen_ref, sent_ref, act_t, out_ref, weight_ref,
+                 full_ref, out_c, back_c, p_got, cot_got, ch_got, send_sem, recv_sem, local_sem, acc, *tail_refs):
+    barrier = pltpu.get_barrier_semaphore()
+    for axes, sizes in ((every[: len(blk_sizes)], blk_sizes), (every[len(blk_sizes) :], rep_sizes)):
+        n = math.prod(sizes)
+        me = 0
+        for a, s in zip(axes, sizes):
+            me = me * s + lax.axis_index(a)
+
+        def greet(o, carry, axes=axes, sizes=sizes, me=me, n=n):
+            rest = (me + o) % n
+            coords = {}
+            for a, s in reversed(list(zip(axes, sizes))):
+                coords[a] = rest % s
+                rest = rest // s
+            device = tuple(coords[a] if a in coords else lax.axis_index(a) for a in every)
+            pl.semaphore_signal(barrier, inc=1, device_id=device, device_id_type=MESH_IDS)
+            return carry
+
+        lax.fori_loop(1, n, greet, 0)
+    pl.semaphore_wait(barrier, math.prod(blk_sizes) + math.prod(rep_sizes) - 2)
+    window_kernel(blk_sizes, rep_sizes, every, proj_ref, cot_ref, chosen_ref, sent_ref, out_c, back_c,
+                  p_got, cot_got, ch_got, send_sem, recv_sem, local_sem, acc, greeted=True)
+    tail_kernel(rep_sizes, blk_sizes, every, out_c, back_c, act_t, out_ref, weight_ref, full_ref, *tail_refs,
+                greeted=True)
+
+
+def fused(projected, cotangent, chosen, chosen_t, act_t, blk_sizes, rep_sizes, every, collective):
+    reps, blks = math.prod(rep_sizes), math.prod(blk_sizes)
+    span = chosen.shape[0]
+    rows, width = projected.shape
+    cols = width // reps
+    vmem = pl.BlockSpec(memory_space=pltpu.VMEM)
+    most = max(reps, blks)
+    moved = (2 * rows * width * 2 + rows * rows * 2) * span + 3 * (reps * rows * cols * 6 + act_t.shape[0] * cols * 4)
+    return pl.pallas_call(
+        functools.partial(fused_kernel, blk_sizes, rep_sizes, every),
+        out_shape=(
+            jax.ShapeDtypeStruct((rows, cols), jnp.bfloat16),
+            jax.ShapeDtypeStruct((act_t.shape[0] // blks, cols), jnp.float32),
+            jax.ShapeDtypeStruct((rows, width), jnp.bfloat16),
+        ),
+        in_specs=[vmem] * 5,
+        out_specs=(vmem, vmem, vmem),
+        scratch_shapes=[
+            pltpu.VMEM((reps, rows, cols), jnp.bfloat16),
+            pltpu.VMEM((reps, rows, cols), jnp.bfloat16),
+            pltpu.VMEM((span, rows, width), projected.dtype),
+            pltpu.VMEM((span, rows, width), cotangent.dtype),
+            pltpu.VMEM((span, rows, rows), chosen.dtype),
+            pltpu.SemaphoreType.DMA((3, 4, span)),
+            pltpu.SemaphoreType.DMA((3, 4, span)),
+            pltpu.SemaphoreType.DMA((3, 4)),
+            pltpu.VMEM((2, rows, width), jnp.float32),
+            pltpu.VMEM((reps, rows, cols), jnp.bfloat16),
+            pltpu.VMEM((reps, rows, cols), jnp.bfloat16),
+            pltpu.VMEM((blks, act_t.shape[0] // blks, cols), jnp.float32),
+            pltpu.VMEM((reps, rows, cols), jnp.bfloat16),
+            pltpu.VMEM((rows, cols), jnp.bfloat16),
+            pltpu.VMEM((blks, act_t.shape[0] // blks, cols), jnp.float32),
+            pltpu.VMEM((rows, cols), jnp.float32),
+            pltpu.VMEM((rows, cols), jnp.float32),
+            pltpu.VMEM((act_t.shape[0] // blks, cols), jnp.float32),
+            pltpu.SemaphoreType.DMA((4, most)),
+            pltpu.SemaphoreType.DMA((4, most)),
+        ],
+        compiler_params=pltpu.CompilerParams(collective_id=collective, has_side_effects=True),
+        cost_estimate=pl.CostEstimate(
+            flops=4 * span * rows * rows * width + 2 * act_t.shape[0] * rows * cols,
+            transcendentals=0,
+            bytes_accessed=moved,
+        ),
+    )(projected, cotangent, chosen, chosen_t, act_t)
+
+
 def shards(hidden_pre, adj_vals, adj_cols, w_out, cotangent):
     row_count, feature_width = hidden_pre.shape
     blk_count = lax.axis_size(BLK)
@@ -459,13 +538,8 @@
     chosen_t = jnp.einsum("tk,kab->tba", picks, own_vals, preferred_element_type=jnp.float32).astype(own_vals.dtype)
     blk_sizes = tuple(lax.axis_size(a) for a in BLK)
     rep_sizes = tuple(lax.axis_size(a) for a in REP)
-    out_sum, back_sum = window(
-        projected, cotangent, chosen, chosen_t, blk_sizes, rep_sizes, EVERY, 3
-    )
-
-    rows = projected.shape[0]
-    out_part, grad_weight, back_full = tail(
-        out_sum, back_sum, jnp.transpose(hidden_act), blk_sizes, rep_sizes, EVERY, 0
+    out_part, grad_weight, back_full = fused(
+        projected, cotangent, chosen, chosen_t, jnp.transpose(hidden_act), blk_sizes, rep_sizes, EVERY, 0
     )
     w_rows = lax.dynamic_slice_in_dim(w_out, rep_pos * cols_here, cols_here, 0)
     grad_in = lax.dot_general(

time: 147 us -> 139 us (0.946); the launches traced: 146 us -> 137 us
  Pallas kernels: 135 us -> 125 us
    pallas_call x2 -> x1, Pallas kernels: 135 us -> 125 us  [fused(): pl.pallas_call(functools.partial(fused_kernel, blk_sizes, rep_sizes, ever...]
where the time goes in v13:
time: 139 us; the launch traced here: 137 us
  Pallas kernels  125 us (90%)
  local copies, waits for them, and re-layouts  4.98 us (4%)
  matrix products  4.14 us (3%)
  other arithmetic  1.54 us (1%)
    pallas_call x1, Pallas kernels, fused(): pl.pallas_call(functools.partial(fused_kernel, blk_sizes, rep_sizes, ever...  125 us
    unnamed x7, local copies, waits for them, and re-layouts  3.9 us

profile of v13, /device:TPU:6, one launch (start us, length us, event | category | flops | bytes accessed | tf_op | source)
XLA Modules:
  0.0 136.8 jit_solution(4673983321443282523)
XLA Ops:
  0.6 0.0 copy-start
  0.7 0.8 fusion.10
  1.5 1.2 fusion.4
  2.6 0.2 copy.10
  2.9 0.0 copy-start.1
  2.9 1.2 copy.8
  4.1 0.7 maximum_bitcast_fusion.act_t
  4.8 0.0 copy-done
  4.8 1.2 convolution_convert_fusion.proj_ref
  6.0 0.9 copy.11.chosen_ref
  6.8 0.0 copy-done.1
  6.8 125.5 %shard_map.76 = (bf16[128,128]{1,0:T(8,128)(2,1)}, f32[16,128]{1,0:T(8,128)}, bf16[128,1024]{1,0:T(8,128)(2,1)}) custom-call(bf16[128,1024]{1,0:T(8,128)(2,1)} %convolution_convert_fusion.proj_ref, bf16[128,1024]{1,0:T(8,128)(2,1)} %cot_ref.1, bf16[8,128,128]{2,1,0:T(8,128)(2,1)} %copy.11.chosen_ref, bf16[8,128,128]{2,1,0:T(8,128)(2,1)} %bitcast.11, ...), custom_call_target="tpu_custom_call" | custom-call | flops 570425344 | bytes 8388608 | tf_op jit(solution)/shard_map/pallas_call | solution.py:480
  132.3 1.8 %fusion = bf16[128,128]{1,0:T(8,128)(2,1)} fusion(bf16[128,1024]{1,0:T(8,128)(2,1)} %get-tuple-element.8, bf16[1024,1024]{1,0:T(8,128)(2,1)S(1)} %copy-done, s32[]{:T(128)S(6)} %select_n.17, bf16[128,1024]{1,0:T(8,128)(2,1)} %param.5), kind=kOutput, calls=%fused_computation.2 | convolution fusion | flops 33636352 | bytes 590848 | tf_op jit(solution)/shard_map/dot_general | solution.py:545
  134.1 1.4 %copy.16 = bf16[128,128]{1,0:T(8,128)(2,1)} copy(bf16[128,128]{1,0:T(8,128)(2,1)} %get-tuple-element.12) | data formatting | bytes 65536
  135.5 1.3 copy.17
Async XLA Ops:
  0.6 4.2 %copy-start = (bf16[1024,1024]{1,0:T(8,128)(2,1)S(1)}, bf16[1024,1024]{1,0:T(8,128)(2,1)}, u32[]{:S(2)}) copy-start(bf16[1024,1024]{1,0:T(8,128)(2,1)} %param.8) | copy-start | bytes 6291460
  2.9 4.0 %copy-start.1 = (bf16[8,128,128]{1,2,0:T(8,128)(2,1)}, bf16[8,128,128]{1,2,0:T(8,128)(2,1)S(1)}, u32[]{:S(2)}) copy-start(bf16[8,128,128]{1,2,0:T(8,128)(2,1)S(1)} %copy.10) | copy-start | bytes 786436

commit v14 on v13

--- a/solution.py
+++ b/solution.py
@@ -534,8 +534,9 @@
     section = jnp.mod(blk_pos - own_cols, blk_count) - rep_pos * span
 
     picks = (section[None, :] == jnp.arange(span, dtype=section.dtype)[:, None]).astype(own_vals.dtype)
-    chosen = jnp.einsum("tk,kab->tab", picks, own_vals, preferred_element_type=jnp.float32).astype(own_vals.dtype)
-    chosen_t = jnp.einsum("tk,kab->tba", picks, own_vals, preferred_element_type=jnp.float32).astype(own_vals.dtype)
+    flipped = jnp.swapaxes(own_vals, 1, 2)
+    chosen = sum(picks[:, k, None, None] * own_vals[k][None] for k in range(slots))
+    chosen_t = sum(picks[:, k, None, None] * flipped[k][None] for k in range(slots))
     blk_sizes = tuple(lax.axis_size(a) for a in BLK)
     rep_sizes = tuple(lax.axis_size(a) for a in REP)
     out_part, grad_weight, back_full = fused(

time: 139 us -> 140 us (level)
    mul x0 -> x5, local copies, waits for them, and re-layouts: none -> 1.81 us  [the longest x3 1.01 us: shards(): picks[:, k, None, None] * flipped[k][None]]
    unnamed x7 -> x5, local copies, waits for them, and re-layouts: 3.9 us -> 3.79 us
where the time goes in v14:
time: 140 us; the launch traced here: 137 us
  Pallas kernels  125 us (89%)
  local copies, waits for them, and re-layouts  5.6 us (4%)
  matrix products  2.99 us (2%)
  other arithmetic  2.55 us (2%)
    pallas_call x1, Pallas kernels, fused(): pl.pallas_call(functools.partial(fused_kernel, blk_sizes, rep_sizes, ever...  125 us
    unnamed x5, local copies, waits for them, and re-layouts  3.79 us

profile of v14, /device:TPU:6, one launch (start us, length us, event | category | flops | bytes accessed | tf_op | source)
XLA Modules:
  0.0 137.3 jit_solution(5455256390446992155)
XLA Ops:
  0.6 0.0 copy-start
  0.7 0.8 fusion.5
  1.5 0.1 compare_convert_fusion
  1.6 0.8 slice_bitcast_fusion.1
  2.3 0.1 copy.9
  2.4 0.1 copy.10
  2.6 0.8 slice_bitcast_fusion.3
  3.4 1.1 copy.8
  4.5 0.7 maximum_bitcast_fusion.act_t
  5.2 0.0 copy-done
  5.2 1.2 convolution_convert_fusion.proj_ref
  6.4 0.9 multiply_add_fusion
  7.3 125.5 %shard_map.76 = (bf16[128,128]{1,0:T(8,128)(2,1)}, f32[16,128]{1,0:T(8,128)}, bf16[128,1024]{1,0:T(8,128)(2,1)}) custom-call(bf16[128,1024]{1,0:T(8,128)(2,1)} %convolution_convert_fusion.proj_ref, bf16[128,1024]{1,0:T(8,128)(2,1)} %cot_ref.1, bf16[8,128,128]{2,1,0:T(8,128)(2,1)} %get-tuple-element.14.chosen_ref, ...), custom_call_target="tpu_custom_call" | custom-call | flops 570425344 | bytes 8388608 | tf_op jit(solution)/shard_map/pallas_call | solution.py:480
  132.8 1.8 %fusion = bf16[128,128]{1,0:T(8,128)(2,1)} fusion(bf16[128,1024]{1,0:T(8,128)(2,1)} %get-tuple-element.8, bf16[1024,1024]{1,0:T(8,128)(2,1)S(1)} %copy-done, s32[]{:T(128)S(6)} %select_n.17, bf16[128,1024]{1,0:T(8,128)(2,1)} %param.5), kind=kOutput, calls=%fused_computation.2 | convolution fusion | flops 33636352 | bytes 590848 | tf_op jit(solution)/shard_map/dot_general | solution.py:546
  134.6 1.4 %copy.13 = bf16[128,128]{1,0:T(8,128)(2,1)} copy(bf16[128,128]{1,0:T(8,128)(2,1)} %get-tuple-element.20) | data formatting | bytes 65536
  136.0 1.3 copy.14
  (1 shorter events, 0.0 us)
Async XLA Ops:
  0.6 4.6 %copy-start = (bf16[1024,1024]{1,0:T(8,128)(2,1)S(1)}, bf16[1024,1024]{1,0:T(8,128)(2,1)}, u32[]{:S(2)}) copy-start(bf16[1024,1024]{1,0:T(8,128)(2,1)} %param.8) | copy-start | bytes 6291460

commit v15 on v13

--- a/solution.py
+++ b/solution.py
@@ -398,7 +398,7 @@
     ])
     out_ref[...] = tot_o[...].astype(out_ref.dtype)
     bg_s[...] = tot_b[...].astype(bg_s.dtype)
-    term = jnp.dot(act_t[...], bg_s[...], preferred_element_type=jnp.float32)
+    term = lax.dot_general(act_t[...], bg_s[...], (((0,), (0,)), ((), ())), preferred_element_type=jnp.float32)
     term_s[...] = term.reshape(term_s.shape)
     run([
         (2, "blk", lambda d: term_s.at[d], land_w, tot_w, None),
@@ -476,12 +476,12 @@
     cols = width // reps
     vmem = pl.BlockSpec(memory_space=pltpu.VMEM)
     most = max(reps, blks)
-    moved = (2 * rows * width * 2 + rows * rows * 2) * span + 3 * (reps * rows * cols * 6 + act_t.shape[0] * cols * 4)
+    moved = (2 * rows * width * 2 + rows * rows * 2) * span + 3 * (reps * rows * cols * 6 + act_t.shape[-1] * cols * 4)
     return pl.pallas_call(
         functools.partial(fused_kernel, blk_sizes, rep_sizes, every),
         out_shape=(
             jax.ShapeDtypeStruct((rows, cols), jnp.bfloat16),
-            jax.ShapeDtypeStruct((act_t.shape[0] // blks, cols), jnp.float32),
+            jax.ShapeDtypeStruct((act_t.shape[-1] // blks, cols), jnp.float32),
             jax.ShapeDtypeStruct((rows, width), jnp.bfloat16),
         ),
         in_specs=[vmem] * 5,
@@ -498,19 +498,19 @@
             pltpu.VMEM((2, rows, width), jnp.float32),
             pltpu.VMEM((reps, rows, cols), jnp.bfloat16),
             pltpu.VMEM((reps, rows, cols), jnp.bfloat16),
-            pltpu.VMEM((blks, act_t.shape[0] // blks, cols), jnp.float32),
+            pltpu.VMEM((blks, act_t.shape[-1] // blks, cols), jnp.float32),
             pltpu.VMEM((reps, rows, cols), jnp.bfloat16),
             pltpu.VMEM((rows, cols), jnp.bfloat16),
-            pltpu.VMEM((blks, act_t.shape[0] // blks, cols), jnp.float32),
+            pltpu.VMEM((blks, act_t.shape[-1] // blks, cols), jnp.float32),
             pltpu.VMEM((rows, cols), jnp.float32),
             pltpu.VMEM((rows, cols), jnp.float32),
-            pltpu.VMEM((act_t.shape[0] // blks, cols), jnp.float32),
+            pltpu.VMEM((act_t.shape[-1] // blks, cols), jnp.float32),
             pltpu.SemaphoreType.DMA((4, most)),
             pltpu.SemaphoreType.DMA((4, most)),
         ],
         compiler_params=pltpu.CompilerParams(collective_id=collective, has_side_effects=True),
         cost_estimate=pl.CostEstimate(
-            flops=4 * span * rows * rows * width + 2 * act_t.shape[0] * rows * cols,
+            flops=4 * span * rows * rows * width + 2 * act_t.shape[-1] * rows * cols,
             transcendentals=0,
             bytes_accessed=moved,
         ),
@@ -539,7 +539,7 @@
     blk_sizes = tuple(lax.axis_size(a) for a in BLK)
     rep_sizes = tuple(lax.axis_size(a) for a in REP)
     out_part, grad_weight, back_full = fused(
-        projected, cotangent, chosen, chosen_t, jnp.transpose(hidden_act), blk_sizes, rep_sizes, EVERY, 0
+        projected, cotangent, chosen, chosen_t, hidden_act, blk_sizes, rep_sizes, EVERY, 0
     )
     w_rows = lax.dynamic_slice_in_dim(w_out, rep_pos * cols_here, cols_here, 0)
     grad_in = lax.dot_general(

time: 139 us -> 139 us (level)
    unnamed x7 -> x8, local copies, waits for them, and re-layouts: 3.9 us -> 2.69 us
where the time goes in v15:
time: 139 us; the launch traced here: 137 us
  Pallas kernels  125 us (90%)
  matrix products  5.07 us (4%)
  local copies, waits for them, and re-layouts  3.75 us (3%)
  other arithmetic  1.53 us (1%)
    pallas_call x1, Pallas kernels, fused(): pl.pallas_call(functools.partial(fused_kernel, blk_sizes, rep_sizes, ever...  125 us

profile of v15, /device:TPU:6, one launch (start us, length us, event | category | flops | bytes accessed | tf_op | source)
XLA Modules:
  0.0 136.5 jit_solution(7526026902845487251)
XLA Ops:
  0.6 0.0 copy-start
  0.6 0.0 copy-start.1
  0.7 0.8 fusion.8
  1.5 1.2 fusion.2
  2.7 0.2 copy.9
  2.9 0.0 copy-start.2
  2.9 0.8 copy.10.chosen_ref
  3.7 0.0 copy-done
  3.7 2.1 %convolution_convert_fusion.proj_ref = bf16[128,1024]{1,0:T(8,128)(2,1)} fusion(bf16[1024,1024]{1,0:T(8,128)(2,1)S(1)} %copy-done, bf16[128,1024]{1,0:T(8,128)(2,1)} %param.5), kind=kOutput, calls=%fused_computation | convolution fusion | flops 268697600 | bytes 2621440 | tf_op jit(solution)/shard_map/dot_general | solution.py:531
  5.8 0.0 copy-done.1
  5.8 0.7 broadcast_maximum_fusion.act_t
  6.5 0.0 copy-done.2
  6.6 125.5 %shard_map.76 = (bf16[128,128]{1,0:T(8,128)(2,1)}, f32[16,128]{1,0:T(8,128)}, bf16[128,1024]{1,0:T(8,128)(2,1)}) custom-call(bf16[128,1024]{1,0:T(8,128)(2,1)} %convolution_convert_fusion.proj_ref, bf16[128,1024]{1,0:T(8,128)(2,1)} %cot_ref.1, bf16[8,128,128]{2,1,0:T(8,128)(2,1)} %copy.10.chosen_ref, bf16[8,128,128]{2,1,0:T(8,128)(2,1)} %bitcast.9, ...), custom_call_target="tpu_custom_call" | custom-call | flops 570425344 | bytes 8388608 | tf_op jit(solution)/shard_map/pallas_call | solution.py:480
  132.0 1.8 %fusion = bf16[128,128]{1,0:T(8,128)(2,1)} fusion(bf16[128,1024]{1,0:T(8,128)(2,1)} %get-tuple-element.8, bf16[1024,1024]{1,0:T(8,128)(2,1)S(1)} %copy-done, s32[]{:T(128)S(6)} %select_n.17, bf16[128,1024]{1,0:T(8,128)(2,1)S(1)} %copy-done.1), kind=kOutput, calls=%fused_computation.2 | convolution fusion | flops 33636352 | bytes 590848 | tf_op jit(solution)/shard_map/dot_general | solution.py:545
  133.8 1.4 %copy.15 = bf16[128,128]{1,0:T(8,128)(2,1)} copy(bf16[128,128]{1,0:T(8,128)(2,1)} %get-tuple-element.12) | data formatting | bytes 65536
  135.2 1.3 copy.16
Async XLA Ops:
  0.6 3.1 %copy-start = (bf16[1024,1024]{1,0:T(8,128)(2,1)S(1)}, bf16[1024,1024]{1,0:T(8,128)(2,1)}, u32[]{:S(2)}) copy-start(bf16[1024,1024]{1,0:T(8,128)(2,1)} %param.8) | copy-start | bytes 6291460
  0.6 5.2 %copy-start.1 = (bf16[128,1024]{1,0:T(8,128)(2,1)S(1)}, bf16[128,1024]{1,0:T(8,128)(2,1)}, u32[]{:S(2)}) copy-start(bf16[128,1024]{1,0:T(8,128)(2,1)} %param.5) | copy-start | bytes 786436
  2.9 3.7 %copy-start.2 = (bf16[8,128,128]{1,2,0:T(8,128)(2,1)}, bf16[8,128,128]{1,2,0:T(8,128)(2,1)S(1)}, u32[]{:S(2)}) copy-start(bf16[8,128,128]{1,2,0:T(8,128)(2,1)S(1)} %copy.9) | copy-start | bytes 786436
